TPU v7x, 256 devices: a whole 4x4x8 slice. The times are simulated.
256 devices in a mesh: ctx: 16 (over z_lo, y, core), heads: 16 (over z_hi, x).
Axes of the slice: x: 4, y: 4, z: 8 (z_hi: 4, z_lo: 2; z = z_hi * 2 + z_lo), core: 2. Of those that a mesh axis runs over, the one named last changes fastest.
Arguments:
- queries: bfloat16 [4096, 8192], P('ctx', 'heads'), may hold values from -48 to 48
- out_grad: bfloat16 [4096, 8192], P('ctx', 'heads'), may hold values from -48 to 48
- attn_out: bfloat16 [4096, 8192], P('ctx', 'heads'), may hold values from -6 to 6
- img_keys: bfloat16 [2048, 1024], P('ctx'), may hold values from -6 to 6
- img_values: bfloat16 [2048, 1024], P('ctx'), may hold values from -6 to 6
- key_weight: bfloat16 [8192, 1024], P('heads'), may hold values from -0.0625 to 0.0625
- value_weight: bfloat16 [8192, 1024], P('heads'), may hold values from -0.0625 to 0.0625
- proj_weight: bfloat16 [7680, 8192], P('heads'), may hold values from -0.0625 to 0.0625
- block_order: int32 [32], replicated, may hold values from 0 to 31, each once
- owner_counts: int32 [16], replicated, may hold values from 1 to 4, 32 in all
Outputs:
- d_query: bfloat16 [4096, 8192], P('ctx', 'heads')
- d_vision: bfloat16 [4096, 7680], P('ctx', 'heads')
Inputs may be any that keep to these rules, and one draw needn't show every extreme that they name: `block_order`: each of the 32 blocks appears once. `owner_counts`: the counts sum to 32; one owner has exactly 4.
All inputs are finite; a program needn't handle non-finite values.
Results may differ from a plain program's by a relative error of at most 0.015.
Values may be sent and summed in bfloat16 or wider, within the bound.
No kernel may reach another device: no remote copies, remote signals or barrier semaphores. Data moves between devices by JAX's collectives and lax.ppermute only.
A program may use at most 64 MiB of HBM per device.

v0:
```python
import jax
import jax.numpy as jnp
from jax import lax
from jax.sharding import PartitionSpec as P

KVH = 8
HD = 128
BR = 64
CAP = 4


CONTRACT_LAST = (((1,), (1,)), ((), ()))
CONTRACT_FIRST = (((0,), (0,)), ((), ()))


def from_everyone(array, axis):
    copies = jnp.broadcast_to(array, (lax.axis_size(axis), *array.shape))
    return lax.all_to_all(copies, axis, split_axis=0, concat_axis=0, tiled=True)


def laid_out(pieces, dim):
    shape = list(pieces.shape[1:])
    shape[dim] *= pieces.shape[0]
    return jnp.moveaxis(pieces, 0, dim).reshape(shape)


def gathered_copies(array, axis, dim):
    pieces = from_everyone(array, axis)
    return laid_out(pieces, dim)


def in_one_piece(arrays, axis, dim, along):
    both = jnp.concatenate(arrays, axis=along)
    filled, at, outs = (gathered_copies(both, axis, dim), 0, [])
    for a in arrays:
        outs.append(lax.slice_in_dim(filled, at, at + a.shape[along], axis=along))
        at += a.shape[along]
    return tuple(outs)


def split_up(array, dim, peers):
    shape = array.shape
    pieces = array.reshape(*shape[:dim], peers, shape[dim] // peers, *shape[dim + 1 :])
    return jnp.moveaxis(pieces, dim, 0)


def sum_at_owner(array, axis, dim):
    peers = lax.axis_size(axis)
    pieces = lax.all_to_all(split_up(array, dim, peers), axis, 0, 0, tiled=True)
    return jnp.sum(pieces, axis=0)


def owner_table(block_order, owner_counts, capacity):
    offsets = jnp.cumsum(owner_counts) - owner_counts
    columns = jnp.arange(capacity, dtype=jnp.int32)
    position = offsets[:, None] + columns[None, :]
    living = columns[None, :] < owner_counts[:, None]
    blocks = jnp.arange(block_order.shape[0], dtype=jnp.int32)
    matches = position[:, :, None] == blocks[None, None, :]
    chosen = jnp.sum(jnp.where(matches, block_order[None, None, :], 0), axis=2)
    return (jnp.where(living, chosen, 0), living)


def image_section(grad_rows, key_weight, value_weight, proj_weight):
    row_count = grad_rows.shape[0]
    group_devices = lax.axis_size("heads") // KVH
    pieces = lax.all_gather(grad_rows.astype(jnp.bfloat16), "heads", axis=1, tiled=True).astype(
        grad_rows.dtype
    )
    pieces = jnp.sum(pieces.reshape(row_count, KVH, group_devices, 2, HD), axis=2).astype(
        jnp.bfloat16
    )
    key_grads = pieces[:, :, 0].reshape(row_count, KVH * HD)
    value_grads = pieces[:, :, 1].reshape(row_count, KVH * HD)
    image_part = lax.dot_general(
        key_grads, key_weight, CONTRACT_LAST, preferred_element_type=jnp.float32
    )
    image_part = image_part + lax.dot_general(
        value_grads, value_weight, CONTRACT_LAST, preferred_element_type=jnp.float32
    )
    image_part = image_part.astype(jnp.bfloat16)
    vision = lax.dot_general(
        lax.all_gather(image_part, "heads", axis=1, tiled=True),
        proj_weight,
        CONTRACT_LAST,
        preferred_element_type=jnp.float32,
    )
    return vision.astype(jnp.bfloat16)


def shards(
    queries,
    out_grad,
    attn_out,
    img_keys,
    img_values,
    key_weight,
    value_weight,
    proj_weight,
    block_order,
    owner_counts,
):
    scaling = HD ** (-0.5)
    text_rows = queries.shape[0]
    local_heads = queries.shape[1] // HD
    group_devices = lax.axis_size("heads") // KVH
    group_index = lax.axis_index("heads") // group_devices
    kv_column = group_index * HD
    own_keys = lax.dynamic_slice_in_dim(img_keys, kv_column, HD, 1)
    own_values = lax.dynamic_slice_in_dim(img_values, kv_column, HD, 1)
    keys_all, values_all = in_one_piece((own_keys, own_values), "ctx", 0, 1)
    query_rows = queries.reshape(text_rows * local_heads, HD)
    grad_rows = out_grad.reshape(text_rows * local_heads, HD)
    output_rows = attn_out.reshape(text_rows * local_heads, HD)
    scores = (
        lax.dot_general(query_rows, keys_all, CONTRACT_LAST, preferred_element_type=jnp.float32)
        * scaling
    )
    weights = jnp.exp(scores - jax.nn.logsumexp(scores, axis=1, keepdims=True))
    weights_low = weights.astype(jnp.bfloat16)
    dweights = lax.dot_general(
        grad_rows, values_all, CONTRACT_LAST, preferred_element_type=jnp.float32
    )
    delta = jnp.sum(
        grad_rows.astype(jnp.float32) * output_rows.astype(jnp.float32), axis=1, keepdims=True
    )
    dscores = (weights * (dweights - delta)).astype(jnp.bfloat16)
    grad_query = jnp.dot(dscores, keys_all, preferred_element_type=jnp.float32) * scaling
    d_query = grad_query.astype(jnp.bfloat16).reshape(text_rows, local_heads * HD)
    ctx_count = lax.axis_size("ctx")
    ctx_index = lax.axis_index("ctx")
    block_total = block_order.shape[0]
    local_count = block_total // ctx_count
    slots, living = owner_table(block_order, owner_counts, CAP)
    my_slots = lax.dynamic_index_in_dim(slots, ctx_index, 0, keepdims=False)
    my_living = lax.dynamic_index_in_dim(living, ctx_index, 0, keepdims=False)
    grad_key = (
        lax.dot_general(dscores, query_rows, CONTRACT_FIRST, preferred_element_type=jnp.float32)
        * scaling
    )
    grad_value = lax.dot_general(
        weights_low, grad_rows, CONTRACT_FIRST, preferred_element_type=jnp.float32
    )
    shared = sum_at_owner(jnp.concatenate([grad_key, grad_value], axis=1), "ctx", 0)
    vision = image_section(shared, key_weight, value_weight, proj_weight)
    width_here = vision.shape[1]
    blocks = jnp.arange(block_total, dtype=jnp.int32)
    owned = jnp.any((slots[:, :, None] == blocks[None, None, :]) & living[:, :, None], axis=1)
    selected = lax.dynamic_slice_in_dim(owned, ctx_index * local_count, local_count, 1)
    local_blocks = vision.reshape(1, local_count, BR, width_here)
    outgoing = jnp.where(selected[:, :, None, None], local_blocks, jnp.zeros((), jnp.bfloat16))
    arrived = lax.all_to_all(outgoing, "ctx", split_axis=0, concat_axis=0, tiled=True)
    arrived = arrived.reshape(block_total, BR, width_here)
    picked = jnp.take(arrived, my_slots, axis=0)
    picked = jnp.where(my_living[:, None, None], picked, jnp.zeros_like(picked))
    d_vision = picked.reshape(CAP * BR, picked.shape[2])
    return (d_query, d_vision)


def solution(mesh):
    placed = (
        P("ctx", "heads"),
        P("ctx", "heads"),
        P("ctx", "heads"),
        P("ctx", None),
        P("ctx", None),
        P("heads", None),
        P("heads", None),
        P("heads", None),
        P(),
        P(),
    )
    return jax.shard_map(
        shards,
        mesh=mesh,
        in_specs=placed,
        out_specs=(P("ctx", "heads"), P("ctx", "heads")),
        check_vma=False,
    )
```

profile of v0, /device:TPU:64, one launch (start us, length us, event | category | flops | bytes accessed | tf_op | source)
XLA Modules:
  0.0 241.0 jit_solution(9903565578479135084)
XLA Ops:
  7.2 0.0 copy-start
  7.2 0.9 constant_dynamic-slice_fusion.1
  8.1 1.1 broadcast_in_dim.90
  9.2 5.9 %all-to-all-start = ((bf16[16,128,256]{2,1,0:T(8,128)(2,1)}), bf16[16,128,256]{2,1,0:T(8,128)(2,1)S(1)}, u32[]{:S(2)}, u32[]{:S(2)}) async-start(bf16[16,128,256]{2,1,0:T(8,128)(2,1)} %broadcast_in_dim.90), calls=%async_computation | async-start | bytes 2097152 | tf_op jit(solution)/shard_map/all_to_all | solution.py:18
  15.1 0.0 all-gather.3.cloned.1.call-start
  15.2 1.1 reshape.180
  16.3 1.1 reshape.181
  17.4 1.1 reshape.189
  18.5 0.2 multiply_reduce_fusion.1
  18.7 13.0 %all-to-all-done = bf16[16,128,256]{2,1,0:T(8,128)(2,1)S(1)} async-done(((bf16[16,128,256]{2,1,0:T(8,128)(2,1)}), bf16[16,128,256]{2,1,0:T(8,128)(2,1)S(1)}, u32[]{:S(2)}, u32[]{:S(2)}) %all-to-all-start) | async-done | bytes 1048608 | tf_op jit(solution)/shard_map/all_to_all | solution.py:18
  31.7 1.3 multiply_reduce_fusion
  33.0 1.4 exponential_reduce_fusion
  34.4 1.7 fusion.1
  36.1 2.1 multiply_convert_fusion
  38.3 1.9 copy-done.1
  40.2 1.5 convolution_multiply_fusion
  41.8 0.2 copy_bitcast_fusion
  42.0 30.4 %all_to_all.15 = f32[16,128,256]{1,2,0:T(8,128)S(1)} all-to-all(f32[16,128,256]{1,2,0:T(8,128)S(1)} %copy_bitcast_fusion), channel_id=1, replica_groups=mesh['ctx'=16,'heads'=16] {'ctx'}, dimensions={0} | all-to-all | bytes 4194304 | tf_op jit(solution)/shard_map/all_to_all | solution.py:49
  72.3 0.7 reduce_sum.48
  73.1 0.0 all-gather.3.cloned.1.call-update
  73.1 0.0 all-gather.5.cloned.1.call-start
  73.2 50.6 %all-gather.3.cloned.1.call-done = bf16[128,4096]{0,1:T(8,128)(2,1)} async-done(((bf16[128,256]{0,1:T(8,128)(2,1)}), bf16[128,4096]{0,1:T(8,128)(2,1)}) %all-gather.3.cloned.1.call-update) | async-done | bytes 1048592 | tf_op jit(solution)/shard_map/all_gather | solution.py:67
  123.7 1.5 reduce.2
  125.3 0.5 fusion.17
  125.8 2.4 fusion.6
  128.1 0.0 all-gather.5.cloned.1.call-update
  128.2 0.1 copy.32
  128.3 0.1 reduce.4
  128.4 0.2 select_reduce_fusion
  128.7 0.1 fusion.13
  128.8 0.1 constant_dynamic-slice_fusion
  128.8 60.8 %all-gather.5.cloned.1.call-done = bf16[128,8192]{1,0:T(8,128)(2,1)} async-done(((bf16[128,512]{1,0:T(8,128)(2,1)}), bf16[128,8192]{1,0:T(8,128)(2,1)}) %all-gather.5.cloned.1.call-update) | async-done | bytes 2097168 | tf_op jit(solution)/shard_map/all_gather | solution.py:83
  189.6 6.1 %convolution_convert_fusion = bf16[128,480]{0,1:T(8,128)(2,1)S(1)} fusion(bf16[128,8192]{1,0:T(8,128)(2,1)} %all-gather.5.cloned.1.call-done, bf16[480,8192]{1,0:T(8,128)(2,1)} %param.17), kind=kOutput, calls=%fused_computation.17 | convolution fusion | flops 1006694400 | bytes 10084352 | tf_op jit(solution)/shard_map/dot_general | solution.py:82
  195.7 0.1 copy.35
  195.8 1.6 broadcast_select_fusion
  197.3 4.8 %all-to-all-start.2 = ((bf16[16,2,64,480]{3,2,1,0:T(8,128)(2,1)}), bf16[16,2,64,480]{3,2,1,0:T(8,128)(2,1)}, u32[]{:S(2)}, u32[]{:S(2)}) async-start(bf16[16,2,64,480]{3,2,1,0:T(8,128)(2,1)} %broadcast_select_fusion), calls=%async_computation.2 | async-start | bytes 4194304 | tf_op jit(solution)/shard_map/all_to_all | solution.py:152
  202.2 0.2 dynamic-slice_reduce_fusion
  202.4 0.2 dynamic-slice_reduce_fusion.1
  202.6 0.1 broadcast_in_dim.99
  202.6 0.1 broadcast_in_dim.100
  202.7 0.1 broadcast_in_dim.93
  202.8 0.1 broadcast_in_dim.94
  202.9 3.5 %fusion.5 = bf16[1024,128]{1,0:T(8,128)(2,1)S(1)} fusion(bf16[2048,1024]{1,0:T(8,128)(2,1)} %copy-done.1, bf16[2048,256]{1,0:T(8,128)(2,1)S(1)} %bitcast.34), kind=kOutput, calls=%fused_computation.14 | convolution fusion | flops 537133056 | bytes 4980736 | tf_op jit(solution)/shard_map/dot_general | solution.py:128
  206.4 0.9 reshape.182
  207.3 23.7 %all-to-all-done.2 = bf16[16,2,64,480]{3,2,1,0:T(8,128)(2,1)} async-done(((bf16[16,2,64,480]{3,2,1,0:T(8,128)(2,1)}), bf16[16,2,64,480]{3,2,1,0:T(8,128)(2,1)}, u32[]{:S(2)}, u32[]{:S(2)}) %all-to-all-start.2) | async-done | bytes 1966112 | tf_op jit(solution)/shard_map/all_to_all | solution.py:152
  231.0 2.2 gather_fusion
  233.1 0.1 fusion.11
  233.3 0.8 copy.36
  (22 shorter events, 0.2 us)
Async XLA Ops:
  7.2 118.1 %copy-start = (bf16[512,1024]{1,0:T(8,128)(2,1)S(1)}, bf16[512,1024]{1,0:T(8,128)(2,1)}, u32[]{:S(2)}) copy-start(bf16[512,1024]{1,0:T(8,128)(2,1)} %param.15) | copy-start | bytes 3145732
  9.2 22.5 %all-to-all-start = ((bf16[16,128,256]{2,1,0:T(8,128)(2,1)}), bf16[16,128,256]{2,1,0:T(8,128)(2,1)S(1)}, u32[]{:S(2)}, u32[]{:S(2)}) async-start(bf16[16,128,256]{2,1,0:T(8,128)(2,1)} %broadcast_in_dim.90), calls=%async_computation | async-start | bytes 2097152 | tf_op jit(solution)/shard_map/all_to_all | solution.py:18
  15.1 108.6 %all-gather.3.cloned.1.call-start = ((), (), s32[]{:S(2)}) async-start(), calls=%async_computation.3 | async-start | bytes 1114112 | tf_op jit(solution)/shard_map/all_gather | solution.py:67
  31.7 4.4 %copy-start.2 = (bf16[16,128,256]{2,1,0:T(8,128)(2,1)}, bf16[16,128,256]{2,1,0:T(8,128)(2,1)S(1)}, u32[]{:S(2)}) copy-start(bf16[16,128,256]{2,1,0:T(8,128)(2,1)S(1)} %all-to-all-done) | copy-start | bytes 3145732
  38.3 1.9 copy-start.1
  41.8 86.4 %copy-start.4 = (s32[16]{0:T(128)S(1)}, s32[16]{0:T(128)}, u32[]{:S(2)}) copy-start(s32[16]{0:T(128)} %param.19) | copy-start | bytes 196
  41.8 86.7 %copy-start.5 = (s32[32]{0:T(128)S(1)}, s32[32]{0:T(128)}, u32[]{:S(2)}) copy-start(s32[32]{0:T(128)} %param.18) | copy-start | bytes 388
  73.1 116.5 %all-gather.5.cloned.1.call-start = ((), (), s32[]{:S(2)}) async-start(), calls=%async_computation.4 | async-start | bytes 2228224 | tf_op jit(solution)/shard_map/all_gather | solution.py:83
  128.8 74.1 %copy-start.3 = (bf16[16,128,256]{2,1,0:T(8,128)(2,1)S(1)}, bf16[16,128,256]{2,1,0:T(8,128)(2,1)}, u32[]{:S(2)}) copy-start(bf16[16,128,256]{2,1,0:T(8,128)(2,1)} %copy-done.2) | copy-start | bytes 3145732
  197.3 33.6 %all-to-all-start.2 = ((bf16[16,2,64,480]{3,2,1,0:T(8,128)(2,1)}), bf16[16,2,64,480]{3,2,1,0:T(8,128)(2,1)}, u32[]{:S(2)}, u32[]{:S(2)}) async-start(bf16[16,2,64,480]{3,2,1,0:T(8,128)(2,1)} %broadcast_select_fusion), calls=%async_computation.2 | async-start | bytes 4194304 | tf_op jit(solution)/shard_map/all_to_all | solution.py:152
Sparse Core Ops, SparseCore 0:
  73.2 50.4 all-gather.2
  128.3 61.2 all-gather.4
where the time goes:
time: 244 us; the launch traced here: 241 us
  waiting for transfers between devices  148 us (61%)
  blocking collectives  30.4 us (12%)
  matrix products  19 us (8%)
  between operations  14.3 us (6%)
  local copies, waits for them, and re-layouts  12.1 us (5%)
  starting transfers between devices  10.8 us (4%)
  other arithmetic  6.27 us (3%)
    all_gather x1, waiting for transfers between devices, image_section(): lax.all_gather(image_part, 'heads', axis=1, tiled=True)  60.8 us
    all_gather x1, waiting for transfers between devices, image_section(): lax.all_gather(grad_rows.astype(jnp.bfloat16), 'heads', axis=1, tiled=True)  50.6 us
    all_to_all x1, blocking collectives, sum_at_owner(): pieces = lax.all_to_all(split_up(array, dim, peers), axis, 0, 0, tiled=True)  30.4 us
    all_to_all x1, waiting for transfers between devices, shards(): lax.all_to_all(outgoing, 'ctx', split_axis=0, concat_axis=0, tiled=True)  23.7 us
    all_to_all x1, waiting for transfers between devices, from_everyone(): return lax.all_to_all(copies, axis, split_axis=0, concat_axis=0, tiled=True)  13 us
    dot_general x1, matrix products, image_section(): lax.dot_general(lax.all_gather(image_part, 'heads', axis=1, tiled=True),...  6.06 us
    all_to_all x1, starting transfers between devices, from_everyone(): return lax.all_to_all(copies, axis, split_axis=0, concat_axis=0, tiled=True)  5.93 us
  transfers between devices with their start and end apart: 4, of which 4 were waited for; matrix products, arithmetic and copies ran while one was open for 4% of the time, Pallas kernels for 0%

commit v1 on v0

v1 whole, which is shorter than its diff:
```python
import functools

import jax
import jax.numpy as jnp
from jax import lax
from jax.experimental import pallas as pl
from jax.experimental.pallas import tpu as pltpu
from jax.sharding import Mesh
from jax.sharding import PartitionSpec as P

HD = 128
BR = 64
CAP = 4
SCALE = HD**-0.5
LOG2E = 1.4426950408889634

CHIPS = ("zl", "y")
HEADS = ("zh", "xh", "xl")
CTX = ("zl", "y", "co")

LAST = (((1,), (1,)), ((), ()))


def attention_kernel(order, counts, core, kv, q, do, ao, dq, mine, other, gk, gv, kt):
    step = pl.program_id(0)
    keys = kv[:, 0:HD]
    values = kv[:, HD : 2 * HD]

    @pl.when(step == 0)
    def _():
        gk[...] = jnp.zeros_like(gk)
        gv[...] = jnp.zeros_like(gv)
        kt[...] = keys.T

    s = lax.dot_general(keys, q[...], LAST, preferred_element_type=jnp.float32)
    s = s * (SCALE * LOG2E)
    e = jnp.exp2(s - jnp.max(s, axis=0, keepdims=True))
    p = e * (1.0 / jnp.sum(e, axis=0, keepdims=True))
    p_low = p.astype(jnp.bfloat16)
    dp = lax.dot_general(values, do[...], LAST, preferred_element_type=jnp.float32)
    both = do[...].astype(jnp.float32) * ao[...].astype(jnp.float32)
    delta = jnp.sum(both.T, axis=0, keepdims=True)
    ds = (p * (dp - delta)).astype(jnp.bfloat16)
    dq_t = jnp.dot(kt[...], ds, preferred_element_type=jnp.float32) * SCALE
    dq[...] = dq_t.T.astype(jnp.bfloat16)
    gk[...] += jnp.dot(ds, q[...], preferred_element_type=jnp.float32)
    gv[...] += jnp.dot(p_low, do[...], preferred_element_type=jnp.float32)

    @pl.when(step == pl.num_programs(0) - 1)
    def _():
        me = core[0]
        start = jnp.int32(0)
        for chip in range(8):
            begin = [None, None]
            count = [None, None]
            for c in range(2):
                begin[c] = start
                count[c] = counts[2 * chip + c]
                start = start + count[c]
            for out, flip in ((mine, False), (other, True)):
                second = (me == 0) if flip else (me == 1)
                first = jnp.where(second, begin[1], begin[0])
                alive = jnp.where(second, count[1], count[0])
                for slot in range(CAP):
                    block = order[jnp.minimum(first + slot, 31)]
                    owner = block // 2
                    row = (owner % 2) * 1024 + (owner // 2) * 128 + (block % 2) * BR
                    rows = pl.ds(pl.multiple_of(row, BR), BR)
                    keep = jnp.where(slot < alive, 1.0, 0.0).astype(jnp.float32)
                    to = pl.ds(slot * BR, BR)
                    out[chip, 0, to, :] = (gk[rows, :] * (keep * SCALE)).astype(jnp.bfloat16)
                    out[chip, 1, to, :] = (gv[rows, :] * keep).astype(jnp.bfloat16)


def attention(order, counts, core, kv, queries, out_grad, attn_out):
    rows, width = queries.shape
    heads = width // HD
    image = kv.shape[0]
    column = pl.BlockSpec((rows, HD), lambda i: (0, i))
    smem = pl.BlockSpec(memory_space=pltpu.SMEM)
    routed = pl.BlockSpec((8, 2, CAP * BR, HD), lambda i: (0, 0, 0, 0))
    grads = jax.ShapeDtypeStruct((8, 2, CAP * BR, HD), jnp.bfloat16)
    return pl.pallas_call(
        attention_kernel,
        grid=(heads,),
        in_specs=[smem, smem, smem, pl.BlockSpec(kv.shape, lambda i: (0, 0)), column, column, column],
        out_specs=[column, routed, routed],
        out_shape=[jax.ShapeDtypeStruct(queries.shape, jnp.bfloat16), grads, grads],
        scratch_shapes=[
            pltpu.VMEM((image, HD), jnp.float32),
            pltpu.VMEM((image, HD), jnp.float32),
            pltpu.VMEM((HD, image), jnp.bfloat16),
        ],
        compiler_params=pltpu.CompilerParams(vmem_limit_bytes=40 << 20),
        cost_estimate=pl.CostEstimate(
            flops=10 * rows * width * image, transcendentals=rows * heads * image, bytes_accessed=5 << 20
        ),
        name="attention",
    )(order, counts, core, kv, queries, out_grad, attn_out)


def product_kernel(w, wp, out, acc):
    step = pl.program_id(0)

    @pl.when(step == 0)
    def _():
        acc[...] = jnp.zeros_like(acc)

    acc[...] += jnp.dot(wp[...], w[0, 0], preferred_element_type=jnp.float32)

    @pl.when(step == pl.num_programs(0) - 1)
    def _():
        out[...] = acc[...].astype(jnp.bfloat16)


def weight_product(gathered, proj_weight):
    width, model = proj_weight.shape
    xs, zhs, part, cols = gathered.shape
    return pl.pallas_call(
        product_kernel,
        grid=(xs * zhs,),
        in_specs=[
            pl.BlockSpec((1, 1, part, cols), lambda i: (i % 4, i // 4, 0, 0)),
            pl.BlockSpec((width, part), lambda i: (0, i)),
        ],
        out_specs=pl.BlockSpec((width, cols), lambda i: (0, 0)),
        out_shape=jax.ShapeDtypeStruct((width, cols), jnp.bfloat16),
        scratch_shapes=[pltpu.VMEM((width, cols), jnp.float32)],
        compiler_params=pltpu.CompilerParams(vmem_limit_bytes=16 << 20),
        cost_estimate=pl.CostEstimate(
            flops=2 * width * model * cols, transcendentals=0, bytes_accessed=10 << 20
        ),
        name="weight_product",
    )(gathered, proj_weight)


def final_kernel(grads, product, out):
    total = None
    for group in range(16):
        term = lax.dot_general(
            grads[group], product[group % 2, group // 2], LAST, preferred_element_type=jnp.float32
        )
        total = term if total is None else total + term
    out[...] = total.astype(jnp.bfloat16)


def final_product(grads, product):
    rows = grads.shape[1]
    width = product.shape[2]
    return pl.pallas_call(
        final_kernel,
        out_shape=jax.ShapeDtypeStruct((rows, width), jnp.bfloat16),
        in_specs=[pl.BlockSpec(memory_space=pltpu.VMEM)] * 2,
        out_specs=pl.BlockSpec(memory_space=pltpu.VMEM),
        compiler_params=pltpu.CompilerParams(vmem_limit_bytes=16 << 20),
        cost_estimate=pl.CostEstimate(
            flops=2 * rows * width * 2048, transcendentals=0, bytes_accessed=4 << 20
        ),
        name="final_product",
    )(grads, product)


def everywhere(array, axes, count):
    copies = jnp.broadcast_to(array, (count, *array.shape))
    return lax.all_to_all(copies, axes, split_axis=0, concat_axis=0, tiled=True)


def shards(
    queries,
    out_grad,
    attn_out,
    img_keys,
    img_values,
    key_weight,
    value_weight,
    proj_weight,
    block_order,
    owner_counts,
):
    core = lax.axis_index("co")
    chip = lax.axis_index(CHIPS)
    group = lax.axis_index(("zh", "xh"))

    own = jnp.concatenate(
        [
            lax.dynamic_slice_in_dim(img_keys, group * HD, HD, 1),
            lax.dynamic_slice_in_dim(img_values, group * HD, HD, 1),
        ],
        axis=1,
    )
    kv = everywhere(own, CHIPS, 8).reshape(1024, 2 * HD)

    w = jnp.where(
        core == 0,
        lax.dynamic_slice_in_dim(key_weight, chip * HD, HD, 1),
        lax.dynamic_slice_in_dim(value_weight, chip * HD, HD, 1),
    )
    w = everywhere(w, "zh", 4)
    w = everywhere(w, ("xh", "xl"), 4)

    kv = lax.all_gather(kv, "co", axis=0, tiled=True)
    d_query, mine, other = attention(
        block_order, owner_counts, core.reshape(1), kv, queries, out_grad, attn_out
    )
    theirs = lax.ppermute(other, "co", [(0, 1), (1, 0)])
    pair = (mine.astype(jnp.float32) + theirs.astype(jnp.float32)).astype(jnp.bfloat16)
    pieces = lax.all_to_all(
        pair.reshape(16, CAP * BR, HD), ("zl", "y", "xl"), split_axis=0, concat_axis=0, tiled=True
    )
    summed = jnp.sum(pieces.astype(jnp.float32), axis=0).astype(jnp.bfloat16)
    grads = everywhere(summed, HEADS, 16)

    product = weight_product(w, proj_weight)
    product = everywhere(product, CHIPS, 8)
    product = lax.all_gather(product, "co", axis=0, tiled=False)
    d_vision = final_product(grads, product)
    return (d_query, d_vision)


def solution(mesh):
    fine = Mesh(mesh.devices.reshape(2, 4, 2, 4, 2, 2), (*CTX, *HEADS))
    placed = (
        P(CTX, HEADS),
        P(CTX, HEADS),
        P(CTX, HEADS),
        P(CTX, None),
        P(CTX, None),
        P(HEADS, None),
        P(HEADS, None),
        P(HEADS, None),
        P(),
        P(),
    )
    return jax.shard_map(
        shards,
        mesh=fine,
        in_specs=placed,
        out_specs=(P(CTX, HEADS), P(CTX, HEADS)),
        check_vma=False,
    )
```

time: 244 us -> 176 us (0.72)
  waiting for transfers between devices: 148 us -> 83.3 us
  Pallas kernels: 0 us -> 19.9 us
  matrix products: 19 us -> 0 us
  blocking collectives: 30.4 us -> 13.4 us
  starting transfers between devices: 10.8 us -> 27.7 us
  other arithmetic: 6.27 us -> 2.4 us
    all_gather x2, waiting for transfers between devices: 111 us -> 0.02 us  [the longest x1 0.01 us: shards(): product = lax.all_gather(product, 'co', axis=0, tiled=False)]
    all_to_all x2 -> x5, waiting for transfers between devices: 36.7 us -> 79.2 us  [the longest x4 63.8 us: everywhere(): return lax.all_to_all(copies, axes, split_axis=0, concat_axis=0, tiled=True)]
    pallas_call x0 -> x3, Pallas kernels: none -> 19.9 us  [the longest x1 13.2 us: attention(): pl.pallas_call(attention_kernel, grid=(heads,), in_specs=[smem, smem, sme...]
    dot_general x8 -> x0, matrix products: 19 us -> none  [the longest x1 6.06 us: image_section(): lax.dot_general(lax.all_gather(image_part, 'heads', axis=1, tiled=True),...]
    all_to_all x1, blocking collectives: 30.4 us -> 13.4 us  [everywhere(): return lax.all_to_all(copies, axes, split_axis=0, concat_axis=0, tiled=True)]
    all_to_all x2 -> x5, starting transfers between devices: 10.8 us -> 27.7 us  [the longest x4 21.9 us: everywhere(): return lax.all_to_all(copies, axes, split_axis=0, concat_axis=0, tiled=True)]
    unnamed x13 -> x19, local copies, waits for them, and re-layouts: 2.78 us -> 6.86 us
    reduce_sum x5 -> x1, other arithmetic: 4.07 us -> 0.14 us  [shards(): summed = jnp.sum(pieces.astype(jnp.float32), axis=0).astype(jnp.bfloat16)]
  transfers between devices with their start and end apart: 4 -> 8, of which waited for: 4 -> 5; matrix products, arithmetic and copies ran while one was open for 4% -> 3% of each run, Pallas kernels for 0% -> 11%
where the time goes in v1:
time: 176 us; the launch traced here: 173 us
  waiting for transfers between devices  83.3 us (47%)
  starting transfers between devices  27.7 us (16%)
  Pallas kernels  19.9 us (11%)
  between operations  14.2 us (8%)
  blocking collectives  13.4 us (8%)
  local copies, waits for them, and re-layouts  12.5 us (7%)
  other arithmetic  2.4 us (1%)
    all_to_all x4, waiting for transfers between devices, everywhere(): return lax.all_to_all(copies, axes, split_axis=0, concat_axis=0, tiled=True)  63.8 us
    all_to_all x4, starting transfers between devices, everywhere(): return lax.all_to_all(copies, axes, split_axis=0, concat_axis=0, tiled=True)  21.9 us
    all_to_all x1, waiting for transfers between devices, shards(): lax.all_to_all(pair.reshape(16, CAP * BR, HD), ('zl', 'y', 'xl'), split_a...  15.4 us
    all_to_all x1, blocking collectives, everywhere(): return lax.all_to_all(copies, axes, split_axis=0, concat_axis=0, tiled=True)  13.4 us
    pallas_call x1, Pallas kernels, attention(): pl.pallas_call(attention_kernel, grid=(heads,), in_specs=[smem, smem, sme...  13.2 us
    unnamed x19, local copies, waits for them, and re-layouts  6.86 us
    all_to_all x1, starting transfers between devices, shards(): lax.all_to_all(pair.reshape(16, CAP * BR, HD), ('zl', 'y', 'xl'), split_a...  5.79 us
    pallas_call x1, Pallas kernels, weight_product(): pl.pallas_call(product_kernel, grid=(xs * zhs,), in_specs=[pl.BlockSpec((...  5.45 us
  transfers between devices with their start and end apart: 8, of which 5 were waited for; matrix products, arithmetic and copies ran while one was open for 3% of the time, Pallas kernels for 11%

profile of v1, /device:TPU:64, one launch (start us, length us, event | category | flops | bytes accessed | tf_op | source)
XLA Modules:
  0.0 173.4 jit_solution(6850955221082404753)
XLA Ops:
  7.2 1.0 dynamic-slice_select_fusion
  8.2 0.9 broadcast_in_dim.17
  9.1 8.1 %all-to-all-start.3 = ((bf16[4,512,128]{2,1,0:T(8,128)(2,1)}), bf16[4,512,128]{2,1,0:T(8,128)(2,1)S(1)}, u32[]{:S(2)}, u32[]{:S(2)}) async-start(bf16[4,512,128]{2,1,0:T(8,128)(2,1)} %broadcast_in_dim.17), calls=%async_computation.3 | async-start | bytes 1048576 | tf_op jit(solution)/shard_map/all_to_all | solution.py:165
  17.2 0.8 constant_dynamic-slice_fusion
  18.0 14.4 %all-to-all-done.3 = bf16[4,512,128]{2,1,0:T(8,128)(2,1)S(1)} async-done(((bf16[4,512,128]{2,1,0:T(8,128)(2,1)}), bf16[4,512,128]{2,1,0:T(8,128)(2,1)S(1)}, u32[]{:S(2)}, u32[]{:S(2)}) %all-to-all-start.3) | async-done | bytes 524320 | tf_op jit(solution)/shard_map/all_to_all | solution.py:165
  32.4 13.4 %all_to_all.30 = bf16[8,128,256]{2,1,0:T(8,128)(2,1)} all-to-all(bf16[8,128,256]{2,1,0:T(8,128)(2,1)S(1)} %broadcast_in_dim.15), channel_id=1, replica_groups=mesh['zl'=2,'y'=4,'co'=2,'zh'=4,'xh'=2,'xl'=2] {'zl','y'}, dimensions={0} | all-to-all | bytes 1048576 | tf_op jit(solution)/shard_map/all_to_all | solution.py:165
  45.8 1.7 %broadcast_in_dim.18 = bf16[4,4,512,128]{3,2,1,0:T(8,128)(2,1)} broadcast(bf16[4,512,128]{2,1,0:T(8,128)(2,1)S(1)} %all-to-all-done.3), dimensions={1,2,3} | broadcast | bytes 2621440 | tf_op jit(solution)/shard_map/broadcast_in_dim | solution.py:164
  47.5 4.3 %all-to-all-start.4 = ((bf16[4,4,512,128]{3,2,1,0:T(8,128)(2,1)}), bf16[4,4,512,128]{3,2,1,0:T(8,128)(2,1)S(1)}, u32[]{:S(2)}, u32[]{:S(2)}) async-start(bf16[4,4,512,128]{3,2,1,0:T(8,128)(2,1)} %broadcast_in_dim.18), calls=%async_computation.4 | async-start | bytes 4194304 | tf_op jit(solution)/shard_map/all_to_all | solution.py:165
  51.8 0.0 all-gather.4.cloned.1.call-start
  51.8 0.7 all-gather.4.cloned.1.call-update
  52.5 22.9 %all-to-all-done.4.w = bf16[4,4,512,128]{3,2,1,0:T(8,128)(2,1)S(1)} async-done(((bf16[4,4,512,128]{3,2,1,0:T(8,128)(2,1)}), bf16[4,4,512,128]{3,2,1,0:T(8,128)(2,1)S(1)}, u32[]{:S(2)}, u32[]{:S(2)}) %all-to-all-start.4) | async-done | bytes 2097184 | tf_op jit(solution)/shard_map/all_to_all | solution.py:165
  75.5 0.0 copy-start
  75.5 3.2 %copy-done = bf16[480,8192]{1,0:T(8,128)(2,1)S(1)} copy-done((bf16[480,8192]{1,0:T(8,128)(2,1)S(1)}, bf16[480,8192]{1,0:T(8,128)(2,1)}, u32[]{:S(2)}) %copy-start) | copy-done | bytes 7864344
  78.7 5.4 %weight_product.1 = bf16[480,128]{1,0:T(8,128)(2,1)S(1)} custom-call(bf16[4,4,512,128]{3,2,1,0:T(8,128)(2,1)S(1)} %all-to-all-done.4.w, bf16[480,8192]{1,0:T(8,128)(2,1)S(1)} %copy-done), custom_call_target="tpu_custom_call" | custom-call | flops 1006632960 | bytes 10485760 | tf_op jit(solution)/shard_map/weight_product/pallas_call | solution.py:119
  84.1 0.0 copy-start.3
  84.2 0.0 copy-start.4
  84.2 0.0 copy-start.5
  84.2 0.0 copy-start.6
  84.2 0.0 copy-start.7
  84.2 1.1 broadcast_in_dim.19
  85.3 3.8 %all-to-all-start.5 = ((bf16[8,480,128]{2,1,0:T(8,128)(2,1)}), bf16[8,480,128]{2,1,0:T(8,128)(2,1)S(1)}, u32[]{:S(2)}, u32[]{:S(2)}) async-start(bf16[8,480,128]{2,1,0:T(8,128)(2,1)} %broadcast_in_dim.19), calls=%async_computation.5 | async-start | bytes 1966080 | tf_op jit(solution)/shard_map/all_to_all | solution.py:165
  89.1 0.0 all-gather.4.cloned.1.call-done.kv
  89.1 0.0 copy-done.3
  89.1 0.0 copy-done.4
  89.1 0.0 copy-done.5
  89.1 0.0 copy-done.6
  89.1 0.0 copy-done.7
  89.1 0.0 copy-start.2
  89.1 1.2 copy-done.2
  90.4 13.2 %attention.1 = (bf16[256,512]{1,0:T(8,128)(2,1)}, bf16[8,2,256,128]{3,2,1,0:T(8,128)(2,1)S(1)}, bf16[8,2,256,128]{3,2,1,0:T(8,128)(2,1)S(1)}) custom-call(s32[32]{0:T(128)S(1)} %copy-done.6, s32[16]{0:T(128)S(1)} %copy-done.7, s32[1]{0:T(128)} %bitcast.core, bf16[2048,256]{1,0:T(8,128)(2,1)S(1)} %copy-done.2, bf16[256,512]{1,0:T(8,128)(2,1)S(1)} %copy-done.3, ...), custom_call_target="tpu_custom_call" | custom-call | flops 2684354560 | bytes 5242880 | tf_op jit(solution)/shard_map/attention/pallas_call | solution.py:83
  103.5 0.0 collective-permute-start
  103.5 2.7 %collective-permute-done = bf16[8,2,256,128]{3,2,1,0:T(8,128)(2,1)S(1)} collective-permute-done((bf16[8,2,256,128]{3,2,1,0:T(8,128)(2,1)S(1)}, bf16[8,2,256,128]{3,2,1,0:T(8,128)(2,1)S(1)}, u32[]{:S(2)}, u32[]{:S(2)}) %collective-permute-start) | collective-permute-done | bytes 1048608 | tf_op jit(solution)/shard_map/ppermute | solution.py:205
  106.2 1.2 add_convert_fusion
  107.4 0.0 all-to-all-done.5
  107.4 0.0 copy-start.8
  107.4 5.8 %all-to-all-start.1 = ((bf16[16,256,128]{2,1,0:T(8,128)(2,1)}), bf16[16,256,128]{2,1,0:T(8,128)(2,1)S(1)}, u32[]{:S(2)}, u32[]{:S(2)}) async-start(bf16[16,256,128]{2,1,0:T(8,128)(2,1)} %bitcast.2), calls=%async_computation.1 | async-start | bytes 2097152 | tf_op jit(solution)/shard_map/all_to_all | solution.py:207
  113.2 0.0 all-gather.6.cloned.1.call-start
  113.3 0.0 copy-done.8
  113.3 0.7 all-gather.6.cloned.1.call-update
  114.0 15.4 %all-to-all-done.1 = bf16[16,256,128]{2,1,0:T(8,128)(2,1)S(1)} async-done(((bf16[16,256,128]{2,1,0:T(8,128)(2,1)}), bf16[16,256,128]{2,1,0:T(8,128)(2,1)S(1)}, u32[]{:S(2)}, u32[]{:S(2)}) %all-to-all-start.1) | async-done | bytes 1048608 | tf_op jit(solution)/shard_map/all_to_all | solution.py:207
  129.4 0.1 reduce_sum.12
  129.5 1.2 broadcast_in_dim.16
  130.7 5.7 %all-to-all-start.2 = ((bf16[16,256,128]{2,1,0:T(8,128)(2,1)}), bf16[16,256,128]{2,1,0:T(8,128)(2,1)S(1)}, u32[]{:S(2)}, u32[]{:S(2)}) async-start(bf16[16,256,128]{2,1,0:T(8,128)(2,1)} %broadcast_in_dim.16), calls=%async_computation.2 | async-start | bytes 2097152 | tf_op jit(solution)/shard_map/all_to_all | solution.py:165
  136.4 0.0 all-gather.6.cloned.1.call-done
  136.4 26.5 %all-to-all-done.2.grads = bf16[16,256,128]{2,1,0:T(8,128)(2,1)S(1)} async-done(((bf16[16,256,128]{2,1,0:T(8,128)(2,1)}), bf16[16,256,128]{2,1,0:T(8,128)(2,1)S(1)}, u32[]{:S(2)}, u32[]{:S(2)}) %all-to-all-start.2) | async-done | bytes 1048608 | tf_op jit(solution)/shard_map/all_to_all | solution.py:165
  162.9 1.5 copy-done.1
  164.5 1.2 final_product.1
  165.7 0.8 copy.13
  (3 shorter events, 0.0 us)
Async XLA Ops:
  9.1 23.3 %all-to-all-start.3 = ((bf16[4,512,128]{2,1,0:T(8,128)(2,1)}), bf16[4,512,128]{2,1,0:T(8,128)(2,1)S(1)}, u32[]{:S(2)}, u32[]{:S(2)}) async-start(bf16[4,512,128]{2,1,0:T(8,128)(2,1)} %broadcast_in_dim.17), calls=%async_computation.3 | async-start | bytes 1048576 | tf_op jit(solution)/shard_map/all_to_all | solution.py:165
  47.5 27.9 %all-to-all-start.4 = ((bf16[4,4,512,128]{3,2,1,0:T(8,128)(2,1)}), bf16[4,4,512,128]{3,2,1,0:T(8,128)(2,1)S(1)}, u32[]{:S(2)}, u32[]{:S(2)}) async-start(bf16[4,4,512,128]{3,2,1,0:T(8,128)(2,1)} %broadcast_in_dim.18), calls=%async_computation.4 | async-start | bytes 4194304 | tf_op jit(solution)/shard_map/all_to_all | solution.py:165
  51.8 37.3 %all-gather.4.cloned.1.call-start = ((), (), s32[]{:S(2)}) async-start(), calls=%async_computation.6 | async-start | bytes 1572864 | tf_op jit(solution)/shard_map/all_gather | solution.py:201
  75.5 3.2 %copy-start = (bf16[480,8192]{1,0:T(8,128)(2,1)S(1)}, bf16[480,8192]{1,0:T(8,128)(2,1)}, u32[]{:S(2)}) copy-start(bf16[480,8192]{1,0:T(8,128)(2,1)} %wp.1) | copy-start | bytes 23592964
  84.1 4.9 %copy-start.3 = (bf16[256,512]{1,0:T(8,128)(2,1)S(1)}, bf16[256,512]{1,0:T(8,128)(2,1)}, u32[]{:S(2)}) copy-start(bf16[256,512]{1,0:T(8,128)(2,1)} %q.1) | copy-start | bytes 786436
  84.2 4.9 %copy-start.4 = (bf16[256,512]{1,0:T(8,128)(2,1)S(1)}, bf16[256,512]{1,0:T(8,128)(2,1)}, u32[]{:S(2)}) copy-start(bf16[256,512]{1,0:T(8,128)(2,1)} %do.1) | copy-start | bytes 786436
  84.2 4.9 %copy-start.5 = (bf16[256,512]{1,0:T(8,128)(2,1)S(1)}, bf16[256,512]{1,0:T(8,128)(2,1)}, u32[]{:S(2)}) copy-start(bf16[256,512]{1,0:T(8,128)(2,1)} %ao.1) | copy-start | bytes 786436
  84.2 4.9 %copy-start.6 = (s32[32]{0:T(128)S(1)}, s32[32]{0:T(128)}, u32[]{:S(2)}) copy-start(s32[32]{0:T(128)} %order.1) | copy-start | bytes 388
  84.2 4.9 %copy-start.7 = (s32[16]{0:T(128)S(1)}, s32[16]{0:T(128)}, u32[]{:S(2)}) copy-start(s32[16]{0:T(128)} %counts.1) | copy-start | bytes 196
  85.3 22.1 %all-to-all-start.5 = ((bf16[8,480,128]{2,1,0:T(8,128)(2,1)}), bf16[8,480,128]{2,1,0:T(8,128)(2,1)S(1)}, u32[]{:S(2)}, u32[]{:S(2)}) async-start(bf16[8,480,128]{2,1,0:T(8,128)(2,1)} %broadcast_in_dim.19), calls=%async_computation.5 | async-start | bytes 1966080 | tf_op jit(solution)/shard_map/all_to_all | solution.py:165
  89.1 1.2 copy-start.2
  103.5 2.7 %collective-permute-start = (bf16[8,2,256,128]{3,2,1,0:T(8,128)(2,1)S(1)}, bf16[8,2,256,128]{3,2,1,0:T(8,128)(2,1)S(1)}, u32[]{:S(2)}, u32[]{:S(2)}) collective-permute-start(bf16[8,2,256,128]{3,2,1,0:T(8,128)(2,1)S(1)} %get-tuple-element.7), channel_id=1, source_target_pairs={{0,16},{16,0},{1,17},{17,1},{2,18},{18,2},{3,19},{19,3},{4,20},{20... | collective-permute-start | bytes 3145736 | tf_op jit(solution)/shard_map/ppermute | solution.py:205
  107.4 5.8 %copy-start.8 = (bf16[8,480,128]{2,1,0:T(8,128)(2,1)}, bf16[8,480,128]{2,1,0:T(8,128)(2,1)S(1)}, u32[]{:S(2)}) copy-start(bf16[8,480,128]{2,1,0:T(8,128)(2,1)S(1)} %all-to-all-done.5) | copy-start | bytes 2949124
  107.4 21.9 %all-to-all-start.1 = ((bf16[16,256,128]{2,1,0:T(8,128)(2,1)}), bf16[16,256,128]{2,1,0:T(8,128)(2,1)S(1)}, u32[]{:S(2)}, u32[]{:S(2)}) async-start(bf16[16,256,128]{2,1,0:T(8,128)(2,1)} %bitcast.2), calls=%async_computation.1 | async-start | bytes 2097152 | tf_op jit(solution)/shard_map/all_to_all | solution.py:207
  113.2 23.2 %all-gather.6.cloned.1.call-start = ((), (), s32[]{:S(2)}) async-start(), calls=%async_computation.7 | async-start | bytes 2949120 | tf_op jit(solution)/shard_map/all_gather | solution.py:215
  130.7 32.2 %all-to-all-start.2 = ((bf16[16,256,128]{2,1,0:T(8,128)(2,1)}), bf16[16,256,128]{2,1,0:T(8,128)(2,1)S(1)}, u32[]{:S(2)}, u32[]{:S(2)}) async-start(bf16[16,256,128]{2,1,0:T(8,128)(2,1)} %broadcast_in_dim.16), calls=%async_computation.2 | async-start | bytes 2097152 | tf_op jit(solution)/shard_map/all_to_all | solution.py:165
  162.9 1.5 copy-start.1
Sparse Core Ops, SparseCore 0:
  54.4 11.5 all-gather.3
  115.9 14.2 all-gather.5

commit v2 on v1

v2 whole, which is shorter than its diff:
```python
import functools

import jax
import jax.numpy as jnp
from jax import lax
from jax.experimental import pallas as pl
from jax.experimental.pallas import tpu as pltpu
from jax.sharding import Mesh
from jax.sharding import PartitionSpec as P

HD = 128
BR = 64
CAP = 4
SCALE = HD**-0.5
CHUNK = 512
LOG2E = 1.4426950408889634

CHIPS = ("zl", "y")
HEADS = ("zh", "xh", "xl")
CTX = ("zl", "y", "co")

LAST = (((1,), (1,)), ((), ()))


def route(order, counts, core, gk, gv, mine, other):
    me = core[0]
    start = jnp.int32(0)
    for chip in range(8):
        begin, count = [], []
        for c in range(2):
            begin.append(start)
            count.append(counts[2 * chip + c])
            start = start + count[c]
        for out, second in ((mine, me == 1), (other, me == 0)):
            first = jnp.where(second, begin[1], begin[0])
            alive = jnp.where(second, count[1], count[0])
            for slot in range(CAP):
                block = order[jnp.minimum(first + slot, 31)]
                ctx = block // 2
                away = jnp.where(ctx % 2 == me, 0, 1024)
                row = away + (ctx // 2) * 128 + (block % 2) * BR
                rows = pl.ds(pl.multiple_of(row, BR), BR)
                keep = jnp.where(slot < alive, 1.0, 0.0).astype(jnp.float32)
                to = pl.ds(slot * BR, BR)
                out[chip, 0, to, :] = (gk[rows, :] * (keep * SCALE)).astype(jnp.bfloat16)
                out[chip, 1, to, :] = (gv[rows, :] * keep).astype(jnp.bfloat16)


def attention_kernel(order, counts, core, kv0, kv1, q_ref, do_ref, ao_ref, dq, mine, other, gk, gv, kt):
    half = kv0.shape[0]
    pieces = [(r, at) for r in (kv0, kv1) for at in range(0, half, CHUNK)]
    spans = [slice(i * CHUNK, (i + 1) * CHUNK) for i in range(len(pieces))]
    keys = lambda i: pieces[i][0][pieces[i][1] : pieces[i][1] + CHUNK, 0:HD]
    values = lambda i: pieces[i][0][pieces[i][1] : pieces[i][1] + CHUNK, HD : 2 * HD]
    every = range(len(pieces))
    for i in every:
        kt[:, spans[i]] = keys(i).T
    for head in range(q_ref.shape[1] // HD):
        cols = slice(head * HD, (head + 1) * HD)
        q, do = q_ref[:, cols], do_ref[:, cols]
        s = [lax.dot_general(keys(i), q, LAST, preferred_element_type=jnp.float32) for i in every]
        top = functools.reduce(jnp.maximum, [x.max(axis=0, keepdims=True) for x in s])
        top = top * (SCALE * LOG2E)
        e = [jnp.exp2(x * (SCALE * LOG2E) - top) for x in s]
        inverse = 1.0 / functools.reduce(jnp.add, [x.sum(axis=0, keepdims=True) for x in e])
        both = do.astype(jnp.float32) * ao_ref[:, cols].astype(jnp.float32)
        delta = jnp.sum(both.T, axis=0, keepdims=True)
        dq_t = None
        for i in every:
            dp = lax.dot_general(values(i), do, LAST, preferred_element_type=jnp.float32)
            p = e[i] * inverse
            ds = (p * (dp - delta)).astype(jnp.bfloat16)
            part = jnp.dot(kt[:, spans[i]], ds, preferred_element_type=jnp.float32)
            dq_t = part if dq_t is None else dq_t + part
            key_part = jnp.dot(ds, q, preferred_element_type=jnp.float32)
            value_part = jnp.dot(p.astype(jnp.bfloat16), do, preferred_element_type=jnp.float32)
            if head == 0:
                gk[spans[i]] = key_part
                gv[spans[i]] = value_part
            else:
                gk[spans[i]] += key_part
                gv[spans[i]] += value_part
        dq[:, cols] = (dq_t * SCALE).T.astype(jnp.bfloat16)
    route(order, counts, core, gk, gv, mine, other)


def attention(order, counts, core, kv_here, kv_there, queries, out_grad, attn_out):
    rows, width = queries.shape
    image = 2 * kv_here.shape[0]
    smem = pl.BlockSpec(memory_space=pltpu.SMEM)
    vmem = pl.BlockSpec(memory_space=pltpu.VMEM)
    grads = jax.ShapeDtypeStruct((8, 2, CAP * BR, HD), jnp.bfloat16)
    return pl.pallas_call(
        attention_kernel,
        in_specs=[smem] * 3 + [vmem] * 5,
        out_specs=[vmem] * 3,
        out_shape=[jax.ShapeDtypeStruct(queries.shape, jnp.bfloat16), grads, grads],
        scratch_shapes=[
            pltpu.VMEM((image, HD), jnp.float32),
            pltpu.VMEM((image, HD), jnp.float32),
            pltpu.VMEM((HD, image), jnp.bfloat16),
        ],
        compiler_params=pltpu.CompilerParams(vmem_limit_bytes=24 << 20),
        cost_estimate=pl.CostEstimate(
            flops=10 * rows * width * image, transcendentals=rows * width // HD * image, bytes_accessed=5 << 20
        ),
        name="attention",
    )(order, counts, core, kv_here, kv_there, queries, out_grad, attn_out)


def product_kernel(at, w, wp, out, held, kept, sems, w_sems):
    part = w.shape[1] // 4
    copies, pieces = [], []
    w_copies = [pltpu.make_async_copy(w.at[x], kept.at[x], w_sems.at[x]) for x in range(4)]
    for x in range(4):
        for kz in range(4):
            heads = lax.rem(at[0] + 4 - kz, 4) * 4 + x
            cols = pl.ds(pl.multiple_of(heads * part, part), part)
            i = len(copies)
            copies.append(pltpu.make_async_copy(wp.at[:, cols], held.at[i], sems.at[i]))
            pieces.append((x, kz * part))
    for x in range(4):
        w_copies[x].start()
        for copy in copies[4 * x : 4 * x + 4]:
            copy.start()
    total = None
    for i, (x, row) in enumerate(pieces):
        if row == 0:
            w_copies[x].wait()
        copies[i].wait()
        term = jnp.dot(held[i], kept[x, row : row + part, :], preferred_element_type=jnp.float32)
        total = term if total is None else total + term
    out[...] = total.astype(jnp.bfloat16)


def weight_product(at, w, proj_weight):
    width, model = proj_weight.shape
    vmem = pl.BlockSpec(memory_space=pltpu.VMEM)
    return pl.pallas_call(
        product_kernel,
        in_specs=[pl.BlockSpec(memory_space=pltpu.SMEM)] + [pl.BlockSpec(memory_space=pl.ANY)] * 2,
        out_specs=vmem,
        out_shape=jax.ShapeDtypeStruct((width, HD), jnp.bfloat16),
        scratch_shapes=[
            pltpu.VMEM((16, width, model // 16), jnp.bfloat16),
            pltpu.VMEM(w.shape, jnp.bfloat16),
            pltpu.SemaphoreType.DMA((16,)),
            pltpu.SemaphoreType.DMA((4,)),
        ],
        compiler_params=pltpu.CompilerParams(vmem_limit_bytes=60 << 20),
        cost_estimate=pl.CostEstimate(
            flops=2 * width * model * HD, transcendentals=0, bytes_accessed=10 << 20
        ),
        name="weight_product",
    )(at, w, proj_weight)


def final_kernel(at, grads, *refs):
    here, there, out = refs[:4], refs[4:8], refs[8]
    total = None
    for back in range(4):
        for lane in range(2):
            chip = (at[0] ^ lane) * 4 + lax.rem(at[1] + 4 - back, 4)
            for product, c in ((here[back], at[2]), (there[back], 1 - at[2])):
                term = lax.dot_general(
                    product[lane], grads[2 * chip + c], LAST, preferred_element_type=jnp.float32
                )
                total = term if total is None else total + term
    out[...] = total.astype(jnp.bfloat16)


def final_product(at, grads, here, there):
    rows = grads.shape[1]
    width = here[0].shape[1]
    smem = pl.BlockSpec(memory_space=pltpu.SMEM)
    vmem = pl.BlockSpec(memory_space=pltpu.VMEM)
    return pl.pallas_call(
        final_kernel,
        out_shape=jax.ShapeDtypeStruct((width, rows), jnp.bfloat16),
        in_specs=[smem] + [vmem] * 9,
        out_specs=vmem,
        compiler_params=pltpu.CompilerParams(vmem_limit_bytes=16 << 20),
        cost_estimate=pl.CostEstimate(
            flops=2 * rows * width * 2048, transcendentals=0, bytes_accessed=4 << 20
        ),
        name="final_product",
    )(at, grads, *here, *there)


def everywhere(array, axes, count):
    copies = jnp.broadcast_to(array, (count, *array.shape))
    return lax.all_to_all(copies, axes, split_axis=0, concat_axis=0, tiled=True)


def swap(axis, array):
    return lax.ppermute(array, axis, [(0, 1), (1, 0)])


def ring(array, axes):
    return [array] + [lax.ppermute(array, axes, [(i, (i + k) % 4) for i in range(4)]) for k in (1, 2, 3)]


def shards(
    queries,
    out_grad,
    attn_out,
    img_keys,
    img_values,
    key_weight,
    value_weight,
    proj_weight,
    block_order,
    owner_counts,
):
    core = lax.axis_index("co")
    chip = lax.axis_index(CHIPS)
    group = lax.axis_index(("zh", "xh"))

    w = jnp.where(
        core == 0,
        lax.dynamic_slice_in_dim(key_weight, chip * HD, HD, 1),
        lax.dynamic_slice_in_dim(value_weight, chip * HD, HD, 1),
    )
    w = jnp.concatenate(ring(w, "zh"), axis=0)

    own = jnp.concatenate(
        [
            lax.dynamic_slice_in_dim(img_keys, group * HD, HD, 1),
            lax.dynamic_slice_in_dim(img_values, group * HD, HD, 1),
        ],
        axis=1,
    )
    kv = everywhere(own, CHIPS, 8).reshape(1024, 2 * HD)
    kv, w = lax.optimization_barrier((kv, w))
    w = lax.all_gather(w, ("xh", "xl"), axis=0, tiled=False)
    d_query, mine, other = attention(
        block_order, owner_counts, core.reshape(1), kv, swap("co", kv), queries, out_grad, attn_out
    )
    pair = mine.astype(jnp.float32) + swap("co", other).astype(jnp.float32)
    pieces = lax.all_to_all(
        pair.astype(jnp.bfloat16).reshape(16, CAP * BR, HD),
        ("zl", "y", "xl"),
        split_axis=0,
        concat_axis=0,
        tiled=True,
    )
    summed = jnp.sum(pieces.astype(jnp.float32), axis=0).astype(jnp.bfloat16)
    grads = everywhere(summed, HEADS, 16)

    at = jnp.stack([lax.axis_index(a) for a in CTX])
    product = weight_product(lax.axis_index("zh").reshape(1), w, proj_weight)
    product = jnp.stack([product, swap("zl", product)])
    product = ring(product, "y")
    d_vision = final_product(at, grads, product, [swap("co", p) for p in product])
    return (d_query, d_vision.T)


def solution(mesh):
    fine = Mesh(mesh.devices.reshape(2, 4, 2, 4, 2, 2), (*CTX, *HEADS))
    placed = (
        P(CTX, HEADS),
        P(CTX, HEADS),
        P(CTX, HEADS),
        P(CTX, None),
        P(CTX, None),
        P(HEADS, None),
        P(HEADS, None),
        P(HEADS, None),
        P(),
        P(),
    )
    return jax.shard_map(
        shards,
        mesh=fine,
        in_specs=placed,
        out_specs=(P(CTX, HEADS), P(CTX, HEADS)),
        check_vma=False,
    )
```

time: 176 us -> 142 us (0.81); the launches traced: 173 us -> 142 us
  waiting for transfers between devices: 83.3 us -> 41.7 us
  blocking collectives: 13.4 us -> 29.8 us
  local copies, waits for them, and re-layouts: 12.5 us -> 2.91 us
  other arithmetic: 2.4 us -> 4.5 us
    all_to_all x4 -> x2, waiting for transfers between devices: 63.8 us -> 0.01 us  [everywhere(): return lax.all_to_all(copies, axes, split_axis=0, concat_axis=0, tiled=True)]
    ppermute x1 -> x13, waiting for transfers between devices: 2.66 us -> 27.8 us  [the longest x6 16.5 us: ring(): lax.ppermute(array, axes, [(i, (i + k) % 4) for i in range(4)])]
    all_to_all x1, blocking collectives: 13.4 us -> 29.8 us  [shards(): lax.all_to_all(pair.astype(jnp.bfloat16).reshape(16, CAP * BR, HD), ('zl'...]
    all_to_all x1 -> x0, waiting for transfers between devices: 15.4 us -> none  [shards(): lax.all_to_all(pair.reshape(16, CAP * BR, HD), ('zl', 'y', 'xl'), split_a...]
    ppermute x1 -> x13, starting transfers between devices: 0.01 us -> 15.2 us  [the longest x6 14.5 us: ring(): lax.ppermute(array, axes, [(i, (i + k) % 4) for i in range(4)])]
    all_gather x2 -> x1, waiting for transfers between devices: 0.02 us -> 13.8 us  [shards(): w = lax.all_gather(w, ('xh', 'xl'), axis=0, tiled=False)]
    all_to_all x4 -> x2, starting transfers between devices: 21.9 us -> 12.4 us  [everywhere(): return lax.all_to_all(copies, axes, split_axis=0, concat_axis=0, tiled=True)]
    unnamed x19 -> x10, local copies, waits for them, and re-layouts: 6.86 us -> 0.02 us
  transfers between devices with their start and end apart: 8 -> 16, of which waited for: 5 -> 9; matrix products, arithmetic and copies ran while one was open for 3% -> 4% of each run, Pallas kernels for 11% -> 6%
where the time goes in v2:
time: 142 us
  waiting for transfers between devices  41.7 us (29%)
  blocking collectives  29.8 us (21%)
  starting transfers between devices  27.7 us (20%)
  Pallas kernels  21 us (15%)
  between operations  14.2 us (10%)
  other arithmetic  4.5 us (3%)
  local copies, waits for them, and re-layouts  2.91 us (2%)
    all_to_all x1, blocking collectives, shards(): lax.all_to_all(pair.astype(jnp.bfloat16).reshape(16, CAP * BR, HD), ('zl'...  29.8 us
    ppermute x6, waiting for transfers between devices, ring(): lax.ppermute(array, axes, [(i, (i + k) % 4) for i in range(4)])  16.5 us
    ppermute x6, starting transfers between devices, ring(): lax.ppermute(array, axes, [(i, (i + k) % 4) for i in range(4)])  14.5 us
    all_gather x1, waiting for transfers between devices, shards(): w = lax.all_gather(w, ('xh', 'xl'), axis=0, tiled=False)  13.8 us
    all_to_all x2, starting transfers between devices, everywhere(): return lax.all_to_all(copies, axes, split_axis=0, concat_axis=0, tiled=True)  12.4 us
    ppermute x7, waiting for transfers between devices, swap(): return lax.ppermute(array, axis, [(0, 1), (1, 0)])  11.3 us
    pallas_call x1, Pallas kernels, attention(): pl.pallas_call(attention_kernel, in_specs=[smem] * 3 + [vmem] * 5, out_sp...  10 us
    pallas_call x1, Pallas kernels, weight_product(): pl.pallas_call(product_kernel, in_specs=[pl.BlockSpec(memory_space=pltpu....  8.51 us
  transfers between devices with their start and end apart: 16, of which 9 were waited for; matrix products, arithmetic and copies ran while one was open for 4% of the time, Pallas kernels for 6%

profile of v2, /device:TPU:64, one launch (start us, length us, event | category | flops | bytes accessed | tf_op | source)
XLA Modules:
  0.0 141.8 jit_solution(12066268092732731485)
XLA Ops:
  7.2 0.0 copy-start.3
  7.2 0.9 constant_dynamic-slice_fusion
  8.1 0.8 broadcast_in_dim.6
  8.9 5.8 %all-to-all-start = ((bf16[8,128,256]{2,1,0:T(8,128)(2,1)}), bf16[8,128,256]{2,1,0:T(8,128)(2,1)S(1)}, u32[]{:S(2)}, u32[]{:S(2)}) async-start(bf16[8,128,256]{2,1,0:T(8,128)(2,1)} %broadcast_in_dim.6), calls=%async_computation | async-start | bytes 1048576 | tf_op jit(solution)/shard_map/all_to_all | solution.py:192
  14.8 0.0 all-gather.3.cloned.1.call-start
  14.8 1.0 dynamic-slice_select_fusion
  15.8 0.1 collective-permute-start.2
  15.9 5.9 %collective-permute-start.1 = (bf16[512,128]{1,0:T(8,128)(2,1)S(1)}, bf16[512,128]{1,0:T(8,128)(2,1)S(1)}, u32[]{:S(2)}, u32[]{:S(2)}) collective-permute-start(bf16[512,128]{1,0:T(8,128)(2,1)S(1)} %dynamic-slice_select_fusion), channel_id=1, source_target_pairs={{0,8},{4,12},{8,0},{12,4},{1,9},{5,13},{9,1},{13,5},{2,10},{6,14},... | collective-permute-start | bytes 393224 | tf_op jit(solution)/shard_map/ppermute | solution.py:200
  21.9 2.7 %collective-permute-start = (bf16[512,128]{1,0:T(8,128)(2,1)S(1)}, bf16[512,128]{1,0:T(8,128)(2,1)S(1)}, u32[]{:S(2)}, u32[]{:S(2)}) collective-permute-start(bf16[512,128]{1,0:T(8,128)(2,1)S(1)} %dynamic-slice_select_fusion), channel_id=1, source_target_pairs={{0,4},{4,8},{8,12},{12,0},{1,5},{5,9},{9,13},{13,1},{2,6},{6,10},{... | collective-permute-start | bytes 393224 | tf_op jit(solution)/shard_map/ppermute | solution.py:200
  24.5 0.0 collective-permute-done.2
  24.5 7.6 %collective-permute-done.1 = bf16[512,128]{1,0:T(8,128)(2,1)S(1)} collective-permute-done((bf16[512,128]{1,0:T(8,128)(2,1)S(1)}, bf16[512,128]{1,0:T(8,128)(2,1)S(1)}, u32[]{:S(2)}, u32[]{:S(2)}) %collective-permute-start.1) | collective-permute-done | bytes 131104 | tf_op jit(solution)/shard_map/ppermute | solution.py:200
  32.2 0.0 collective-permute-done
  32.2 0.8 pad_maximum_fusion
  33.0 0.0 all-to-all-done
  33.0 0.0 collective-permute-start.3
  33.0 1.9 %collective-permute-done.3.kv1 = bf16[1024,256]{1,0:T(8,128)(2,1)S(1)} collective-permute-done((bf16[1024,256]{1,0:T(8,128)(2,1)S(1)}, bf16[1024,256]{1,0:T(8,128)(2,1)S(1)}, u32[]{:S(2)}, u32[]{:S(2)}) %collective-permute-start.3) | collective-permute-done | bytes 524320 | tf_op jit(solution)/shard_map/ppermute | solution.py:196
  34.9 0.0 copy-done.4
  35.0 10.0 %attention.1 = (bf16[256,512]{1,0:T(8,128)(2,1)}, bf16[8,2,256,128]{3,2,1,0:T(8,128)(2,1)S(1)}, bf16[8,2,256,128]{3,2,1,0:T(8,128)(2,1)S(1)}) custom-call(s32[32]{0:T(128)S(1)} %copy-done.3, s32[16]{0:T(128)S(1)} %copy-done.4, s32[1]{0:T(128)} %bitcast.core, bf16[1024,256]{1,0:T(8,128)(2,1)S(1)} %bitcast.11, ...), custom_call_target="tpu_custom_call" | custom-call | flops 2684354560 | bytes 5242880 | tf_op jit(solution)/shard_map/attention/pallas_call | solution.py:93
  45.0 0.1 collective-permute-start.4
  45.1 0.0 all-gather.3.cloned.1.call-update
  45.1 2.6 %collective-permute-done.4 = bf16[8,2,256,128]{3,2,1,0:T(8,128)(2,1)} collective-permute-done((bf16[8,2,256,128]{3,2,1,0:T(8,128)(2,1)S(1)}, bf16[8,2,256,128]{3,2,1,0:T(8,128)(2,1)}, u32[]{:S(2)}, u32[]{:S(2)}) %collective-permute-start.4) | collective-permute-done | bytes 1048608 | tf_op jit(solution)/shard_map/ppermute | solution.py:196
  47.8 1.5 %add_convert_fusion = bf16[8,2,256,128]{3,2,1,0:T(8,128)(2,1)S(1)} fusion(bf16[8,2,256,128]{3,2,1,0:T(8,128)(2,1)} %collective-permute-done.4, bf16[8,2,256,128]{3,2,1,0:T(8,128)(2,1)S(1)} %get-tuple-element.9), kind=kLoop, calls=%fused_computation | loop fusion | flops 2097152 | bytes 3145728 | tf_op jit(solution)/shard_map/convert_element_type | solution.py:241
  49.3 29.8 %all_to_all.15 = bf16[16,256,128]{2,1,0:T(8,128)(2,1)S(1)} all-to-all(bf16[16,256,128]{2,1,0:T(8,128)(2,1)S(1)} %bitcast.12), channel_id=1, replica_groups=mesh['zl'=2,'y'=4,'co'=2,'zh'=4,'xh'=2,'xl'=2] {'zl','y','xl'}, dimensions={0} | all-to-all | bytes 2097152 | tf_op jit(solution)/shard_map/all_to_all | solution.py:240
  79.1 0.1 reduce_sum.12
  79.3 1.2 broadcast_in_dim.7
  80.5 6.6 %all-to-all-start.2 = ((bf16[16,256,128]{2,1,0:T(8,128)(2,1)}), bf16[16,256,128]{2,1,0:T(8,128)(2,1)S(1)}, u32[]{:S(2)}, u32[]{:S(2)}) async-start(bf16[16,256,128]{2,1,0:T(8,128)(2,1)} %broadcast_in_dim.7), calls=%async_computation.2 | async-start | bytes 2097152 | tf_op jit(solution)/shard_map/all_to_all | solution.py:192
  87.1 13.8 %all-gather.3.cloned.1.call-done = bf16[8192,128]{1,0:T(8,128)(2,1)} async-done(((bf16[2048,128]{1,0:T(8,128)(2,1)}), bf16[8192,128]{1,0:T(8,128)(2,1)}) %all-gather.3.cloned.1.call-update) | async-done | bytes 2097168 | tf_op jit(solution)/shard_map/all_gather | solution.py:235
  100.9 8.5 %weight_product.1 = bf16[480,128]{1,0:T(8,128)(2,1)} custom-call(s32[1]{0:T(128)} %bitcast.5.at, bf16[4,2048,128]{2,1,0:T(8,128)(2,1)} %bitcast.13, bf16[480,8192]{1,0:T(8,128)(2,1)} %wp.1), custom_call_target="tpu_custom_call" | custom-call | flops 1006632960 | bytes 10485760 | tf_op jit(solution)/shard_map/weight_product/pallas_call | solution.py:139
  109.4 0.1 collective-permute-start.5
  109.5 5.5 %collective-permute-done.5 = bf16[480,128]{1,0:T(8,128)(2,1)S(1)} collective-permute-done((bf16[480,128]{1,0:T(8,128)(2,1)}, bf16[480,128]{1,0:T(8,128)(2,1)S(1)}, u32[]{:S(2)}, u32[]{:S(2)}) %collective-permute-start.5) | collective-permute-done | bytes 122912 | tf_op jit(solution)/shard_map/ppermute | solution.py:196
  115.0 0.9 pad_maximum_fusion.1.refs_0_
  115.9 1.7 %collective-permute-start.6 = (bf16[2,480,128]{2,1,0:T(8,128)(2,1)S(1)}, bf16[2,480,128]{2,1,0:T(8,128)(2,1)S(1)}, u32[]{:S(2)}, u32[]{:S(2)}) collective-permute-start(bf16[2,480,128]{2,1,0:T(8,128)(2,1)S(1)} %pad_maximum_fusion.1.refs_0_), channel_id=1, source_target_pairs={{0,32},{32,64},{64,96},{96,0},{1,33},{33,65},{65,97},{97,1},{2,34}... | collective-permute-start | bytes 737288 | tf_op jit(solution)/shard_map/ppermute | solution.py:200
  117.6 2.8 %collective-permute-start.7 = (bf16[2,480,128]{2,1,0:T(8,128)(2,1)S(1)}, bf16[2,480,128]{2,1,0:T(8,128)(2,1)S(1)}, u32[]{:S(2)}, u32[]{:S(2)}) collective-permute-start(bf16[2,480,128]{2,1,0:T(8,128)(2,1)S(1)} %pad_maximum_fusion.1.refs_0_), channel_id=1, source_target_pairs={{0,64},{32,96},{64,0},{96,32},{1,65},{33,97},{65,1},{97,33},{2,66}... | collective-permute-start | bytes 737288 | tf_op jit(solution)/shard_map/ppermute | solution.py:200
  120.4 1.4 collective-permute-start.8
  121.8 0.0 collective-permute-start.9
  121.8 3.3 %collective-permute-done.6.refs_1_ = bf16[2,480,128]{2,1,0:T(8,128)(2,1)S(1)} collective-permute-done((bf16[2,480,128]{2,1,0:T(8,128)(2,1)S(1)}, bf16[2,480,128]{2,1,0:T(8,128)(2,1)S(1)}, u32[]{:S(2)}, u32[]{:S(2)}) %collective-permute-start.6) | collective-permute-done | bytes 245792 | tf_op jit(solution)/shard_map/ppermute | solution.py:200
  125.1 0.0 collective-permute-start.10
  125.1 5.6 %collective-permute-done.7.refs_2_ = bf16[2,480,128]{2,1,0:T(8,128)(2,1)S(1)} collective-permute-done((bf16[2,480,128]{2,1,0:T(8,128)(2,1)S(1)}, bf16[2,480,128]{2,1,0:T(8,128)(2,1)S(1)}, u32[]{:S(2)}, u32[]{:S(2)}) %collective-permute-start.7) | collective-permute-done | bytes 245792 | tf_op jit(solution)/shard_map/ppermute | solution.py:200
  130.7 0.0 collective-permute-start.11
  130.7 0.0 collective-permute-done.8.refs_3_
  130.7 0.5 collective-permute-start.12
  131.2 0.1 pad_add_fusion.at
  131.2 0.0 collective-permute-done.9.refs_4_
  131.3 0.0 collective-permute-done.10.refs_5_
  131.3 0.9 collective-permute-done.11.refs_6_
  132.2 0.4 collective-permute-done.12.refs_7_
  132.5 0.0 all-to-all-done.2.grads
  132.5 2.4 %final_product.1 = bf16[480,256]{1,0:T(8,128)(2,1)} custom-call(s32[3]{0:T(128)S(1)} %pad_add_fusion.at, bf16[16,256,128]{2,1,0:T(8,128)(2,1)S(1)} %all-to-all-done.2.grads, bf16[2,480,128]{2,1,0:T(8,128)(2,1)S(1)} %pad_maximum_fusion.1.refs_0_, bf16[2,480,128]{2,1,0:T(8,128)(2,1)S(1)} %collective-permute-done.6.refs_1_, ...), custom_call_target="tpu_custom_call" | custom-call | flops 503316480 | bytes 4194304 | tf_op jit(solution)/shard_map/final_product/pallas_call | solution.py:177
  (9 shorter events, 0.0 us)
Async XLA Ops:
  7.2 27.8 %copy-start.3 = (s32[32]{0:T(128)S(1)}, s32[32]{0:T(128)}, u32[]{:S(2)}) copy-start(s32[32]{0:T(128)} %order.1) | copy-start | bytes 388
  7.2 27.8 %copy-start.4 = (s32[16]{0:T(128)S(1)}, s32[16]{0:T(128)}, u32[]{:S(2)}) copy-start(s32[16]{0:T(128)} %counts.1) | copy-start | bytes 196
  7.2 27.8 %copy-start = (bf16[256,512]{1,0:T(8,128)(2,1)S(1)}, bf16[256,512]{1,0:T(8,128)(2,1)}, u32[]{:S(2)}) copy-start(bf16[256,512]{1,0:T(8,128)(2,1)} %q_ref.1) | copy-start | bytes 786436
  7.2 27.8 %copy-start.1 = (bf16[256,512]{1,0:T(8,128)(2,1)S(1)}, bf16[256,512]{1,0:T(8,128)(2,1)}, u32[]{:S(2)}) copy-start(bf16[256,512]{1,0:T(8,128)(2,1)} %do_ref.1) | copy-start | bytes 786436
  7.2 27.8 %copy-start.2 = (bf16[256,512]{1,0:T(8,128)(2,1)S(1)}, bf16[256,512]{1,0:T(8,128)(2,1)}, u32[]{:S(2)}) copy-start(bf16[256,512]{1,0:T(8,128)(2,1)} %ao_ref.1) | copy-start | bytes 786436
  8.9 24.1 %all-to-all-start = ((bf16[8,128,256]{2,1,0:T(8,128)(2,1)}), bf16[8,128,256]{2,1,0:T(8,128)(2,1)S(1)}, u32[]{:S(2)}, u32[]{:S(2)}) async-start(bf16[8,128,256]{2,1,0:T(8,128)(2,1)} %broadcast_in_dim.6), calls=%async_computation | async-start | bytes 1048576 | tf_op jit(solution)/shard_map/all_to_all | solution.py:192
  14.8 86.2 %all-gather.3.cloned.1.call-start = ((), (), s32[]{:S(2)}) async-start(), calls=%async_computation.3 | async-start | bytes 2621440 | tf_op jit(solution)/shard_map/all_gather | solution.py:235
  15.8 8.7 %collective-permute-start.2 = (bf16[512,128]{1,0:T(8,128)(2,1)S(1)}, bf16[512,128]{1,0:T(8,128)(2,1)S(1)}, u32[]{:S(2)}, u32[]{:S(2)}) collective-permute-start(bf16[512,128]{1,0:T(8,128)(2,1)S(1)} %dynamic-slice_select_fusion), channel_id=1, source_target_pairs={{0,12},{4,0},{8,4},{12,8},{1,13},{5,1},{9,5},{13,9},{2,14},{6,2},{... | collective-permute-start | bytes 393224 | tf_op jit(solution)/shard_map/ppermute | solution.py:200
  15.9 16.3 %collective-permute-start.1 = (bf16[512,128]{1,0:T(8,128)(2,1)S(1)}, bf16[512,128]{1,0:T(8,128)(2,1)S(1)}, u32[]{:S(2)}, u32[]{:S(2)}) collective-permute-start(bf16[512,128]{1,0:T(8,128)(2,1)S(1)} %dynamic-slice_select_fusion), channel_id=1, source_target_pairs={{0,8},{4,12},{8,0},{12,4},{1,9},{5,13},{9,1},{13,5},{2,10},{6,14},... | collective-permute-start | bytes 393224 | tf_op jit(solution)/shard_map/ppermute | solution.py:200
  21.9 10.3 %collective-permute-start = (bf16[512,128]{1,0:T(8,128)(2,1)S(1)}, bf16[512,128]{1,0:T(8,128)(2,1)S(1)}, u32[]{:S(2)}, u32[]{:S(2)}) collective-permute-start(bf16[512,128]{1,0:T(8,128)(2,1)S(1)} %dynamic-slice_select_fusion), channel_id=1, source_target_pairs={{0,4},{4,8},{8,12},{12,0},{1,5},{5,9},{9,13},{13,1},{2,6},{6,10},{... | collective-permute-start | bytes 393224 | tf_op jit(solution)/shard_map/ppermute | solution.py:200
  33.0 1.9 %collective-permute-start.3 = (bf16[1024,256]{1,0:T(8,128)(2,1)S(1)}, bf16[1024,256]{1,0:T(8,128)(2,1)S(1)}, u32[]{:S(2)}, u32[]{:S(2)}) collective-permute-start(bf16[1024,256]{1,0:T(8,128)(2,1)S(1)} %bitcast.10), channel_id=1, source_target_pairs={{0,16},{16,0},{1,17},{17,1},{2,18},{18,2},{3,19},{19,3},{4,20},{20... | collective-permute-start | bytes 1572872 | tf_op jit(solution)/shard_map/ppermute | solution.py:196
  45.0 2.8 %collective-permute-start.4 = (bf16[8,2,256,128]{3,2,1,0:T(8,128)(2,1)S(1)}, bf16[8,2,256,128]{3,2,1,0:T(8,128)(2,1)}, u32[]{:S(2)}, u32[]{:S(2)}) collective-permute-start(bf16[8,2,256,128]{3,2,1,0:T(8,128)(2,1)S(1)} %get-tuple-element.10), channel_id=1, source_target_pairs={{0,16},{16,0},{1,17},{17,1},{2,18},{18,2},{3,19},{19,3},{4,20},{20... | collective-permute-start | bytes 3145736 | tf_op jit(solution)/shard_map/ppermute | solution.py:196
  80.5 52.0 %all-to-all-start.2 = ((bf16[16,256,128]{2,1,0:T(8,128)(2,1)}), bf16[16,256,128]{2,1,0:T(8,128)(2,1)S(1)}, u32[]{:S(2)}, u32[]{:S(2)}) async-start(bf16[16,256,128]{2,1,0:T(8,128)(2,1)} %broadcast_in_dim.7), calls=%async_computation.2 | async-start | bytes 2097152 | tf_op jit(solution)/shard_map/all_to_all | solution.py:192
  109.4 5.6 %collective-permute-start.5 = (bf16[480,128]{1,0:T(8,128)(2,1)}, bf16[480,128]{1,0:T(8,128)(2,1)S(1)}, u32[]{:S(2)}, u32[]{:S(2)}) collective-permute-start(bf16[480,128]{1,0:T(8,128)(2,1)} %weight_product.1), channel_id=1, source_target_pairs={{0,128},{128,0},{1,129},{129,1},{2,130},{130,2},{3,131},{131,3},{4... | collective-permute-start | bytes 368648 | tf_op jit(solution)/shard_map/ppermute | solution.py:196
  115.9 9.1 %collective-permute-start.6 = (bf16[2,480,128]{2,1,0:T(8,128)(2,1)S(1)}, bf16[2,480,128]{2,1,0:T(8,128)(2,1)S(1)}, u32[]{:S(2)}, u32[]{:S(2)}) collective-permute-start(bf16[2,480,128]{2,1,0:T(8,128)(2,1)S(1)} %pad_maximum_fusion.1.refs_0_), channel_id=1, source_target_pairs={{0,32},{32,64},{64,96},{96,0},{1,33},{33,65},{65,97},{97,1},{2,34}... | collective-permute-start | bytes 737288 | tf_op jit(solution)/shard_map/ppermute | solution.py:200
  117.6 13.1 %collective-permute-start.7 = (bf16[2,480,128]{2,1,0:T(8,128)(2,1)S(1)}, bf16[2,480,128]{2,1,0:T(8,128)(2,1)S(1)}, u32[]{:S(2)}, u32[]{:S(2)}) collective-permute-start(bf16[2,480,128]{2,1,0:T(8,128)(2,1)S(1)} %pad_maximum_fusion.1.refs_0_), channel_id=1, source_target_pairs={{0,64},{32,96},{64,0},{96,32},{1,65},{33,97},{65,1},{97,33},{2,66}... | collective-permute-start | bytes 737288 | tf_op jit(solution)/shard_map/ppermute | solution.py:200
  120.4 10.3 %collective-permute-start.8 = (bf16[2,480,128]{2,1,0:T(8,128)(2,1)S(1)}, bf16[2,480,128]{2,1,0:T(8,128)(2,1)S(1)}, u32[]{:S(2)}, u32[]{:S(2)}) collective-permute-start(bf16[2,480,128]{2,1,0:T(8,128)(2,1)S(1)} %pad_maximum_fusion.1.refs_0_), channel_id=1, source_target_pairs={{0,96},{32,0},{64,32},{96,64},{1,97},{33,1},{65,33},{97,65},{2,98}... | collective-permute-start | bytes 737288 | tf_op jit(solution)/shard_map/ppermute | solution.py:200
  121.8 9.5 %collective-permute-start.9 = (bf16[2,480,128]{2,1,0:T(8,128)(2,1)S(1)}, bf16[2,480,128]{2,1,0:T(8,128)(2,1)S(1)}, u32[]{:S(2)}, u32[]{:S(2)}) collective-permute-start(bf16[2,480,128]{2,1,0:T(8,128)(2,1)S(1)} %pad_maximum_fusion.1.refs_0_), channel_id=1, source_target_pairs={{0,16},{16,0},{1,17},{17,1},{2,18},{18,2},{3,19},{19,3},{4,20},{20... | collective-permute-start | bytes 737288 | tf_op jit(solution)/shard_map/ppermute | solution.py:196
  125.1 6.2 %collective-permute-start.10 = (bf16[2,480,128]{2,1,0:T(8,128)(2,1)S(1)}, bf16[2,480,128]{2,1,0:T(8,128)(2,1)S(1)}, u32[]{:S(2)}, u32[]{:S(2)}) collective-permute-start(bf16[2,480,128]{2,1,0:T(8,128)(2,1)S(1)} %collective-permute-done.6.refs_1_), channel_id=1, source_target_pairs={{0,16},{16,0},{1,17},{17,1},{2,18},{18,2},{3,19},{19,3},{4,20},{20... | collective-permute-start | bytes 737288 | tf_op jit(solution)/shard_map/ppermute | solution.py:196
  130.7 1.5 %collective-permute-start.11 = (bf16[2,480,128]{2,1,0:T(8,128)(2,1)S(1)}, bf16[2,480,128]{2,1,0:T(8,128)(2,1)S(1)}, u32[]{:S(2)}, u32[]{:S(2)}) collective-permute-start(bf16[2,480,128]{2,1,0:T(8,128)(2,1)S(1)} %collective-permute-done.7.refs_2_), channel_id=1, source_target_pairs={{0,16},{16,0},{1,17},{17,1},{2,18},{18,2},{3,19},{19,3},{4,20},{20... | collective-permute-start | bytes 737288 | tf_op jit(solution)/shard_map/ppermute | solution.py:196
  130.7 1.9 %collective-permute-start.12 = (bf16[2,480,128]{2,1,0:T(8,128)(2,1)S(1)}, bf16[2,480,128]{2,1,0:T(8,128)(2,1)S(1)}, u32[]{:S(2)}, u32[]{:S(2)}) collective-permute-start(bf16[2,480,128]{2,1,0:T(8,128)(2,1)S(1)} %collective-permute-done.8.refs_3_), channel_id=1, source_target_pairs={{0,16},{16,0},{1,17},{17,1},{2,18},{18,2},{3,19},{19,3},{4,20},{20... | collective-permute-start | bytes 737288 | tf_op jit(solution)/shard_map/ppermute | solution.py:196
Sparse Core Ops, SparseCore 0:
  45.3 55.6 all-gather.2

commit v3 on v2

--- a/solution.py
+++ b/solution.py
@@ -108,51 +108,32 @@
     )(order, counts, core, kv_here, kv_there, queries, out_grad, attn_out)
 
 
-def product_kernel(at, w, wp, out, held, kept, sems, w_sems):
-    part = w.shape[1] // 4
-    copies, pieces = [], []
-    w_copies = [pltpu.make_async_copy(w.at[x], kept.at[x], w_sems.at[x]) for x in range(4)]
-    for x in range(4):
+def product_kernel(at, w0, w1, w2, w3, wp, out):
+    part = w0.shape[0] // 4
+    total = None
+    for kx, w in enumerate((w0, w1, w2, w3)):
         for kz in range(4):
-            heads = lax.rem(at[0] + 4 - kz, 4) * 4 + x
+            heads = lax.rem(at[0] + 4 - kz, 4) * 4 + lax.rem(at[1] + 4 - kx, 4)
             cols = pl.ds(pl.multiple_of(heads * part, part), part)
-            i = len(copies)
-            copies.append(pltpu.make_async_copy(wp.at[:, cols], held.at[i], sems.at[i]))
-            pieces.append((x, kz * part))
-    for x in range(4):
-        w_copies[x].start()
-        for copy in copies[4 * x : 4 * x + 4]:
-            copy.start()
-    total = None
-    for i, (x, row) in enumerate(pieces):
-        if row == 0:
-            w_copies[x].wait()
-        copies[i].wait()
-        term = jnp.dot(held[i], kept[x, row : row + part, :], preferred_element_type=jnp.float32)
-        total = term if total is None else total + term
+            term = jnp.dot(wp[:, cols], w[kz * part : (kz + 1) * part, :], preferred_element_type=jnp.float32)
+            total = term if total is None else total + term
     out[...] = total.astype(jnp.bfloat16)
 
 
-def weight_product(at, w, proj_weight):
+def weight_product(at, pieces, proj_weight):
     width, model = proj_weight.shape
     vmem = pl.BlockSpec(memory_space=pltpu.VMEM)
     return pl.pallas_call(
         product_kernel,
-        in_specs=[pl.BlockSpec(memory_space=pltpu.SMEM)] + [pl.BlockSpec(memory_space=pl.ANY)] * 2,
+        in_specs=[pl.BlockSpec(memory_space=pltpu.SMEM)] + [vmem] * 5,
         out_specs=vmem,
         out_shape=jax.ShapeDtypeStruct((width, HD), jnp.bfloat16),
-        scratch_shapes=[
-            pltpu.VMEM((16, width, model // 16), jnp.bfloat16),
-            pltpu.VMEM(w.shape, jnp.bfloat16),
-            pltpu.SemaphoreType.DMA((16,)),
-            pltpu.SemaphoreType.DMA((4,)),
-        ],
-        compiler_params=pltpu.CompilerParams(vmem_limit_bytes=60 << 20),
+        compiler_params=pltpu.CompilerParams(vmem_limit_bytes=14 << 20),
         cost_estimate=pl.CostEstimate(
             flops=2 * width * model * HD, transcendentals=0, bytes_accessed=10 << 20
         ),
         name="weight_product",
-    )(at, w, proj_weight)
+    )(at, *pieces, proj_weight)
 
 
 def final_kernel(at, grads, *refs):
@@ -232,24 +213,28 @@
     )
     kv = everywhere(own, CHIPS, 8).reshape(1024, 2 * HD)
     kv, w = lax.optimization_barrier((kv, w))
-    w = lax.all_gather(w, ("xh", "xl"), axis=0, tiled=False)
+    w = ring(w, ("xh", "xl"))
     d_query, mine, other = attention(
         block_order, owner_counts, core.reshape(1), kv, swap("co", kv), queries, out_grad, attn_out
     )
+    other, *w = lax.optimization_barrier((other, *w))
     pair = mine.astype(jnp.float32) + swap("co", other).astype(jnp.float32)
+    pair = pair.astype(jnp.bfloat16).reshape(16, CAP * BR, HD)
     pieces = lax.all_to_all(
-        pair.astype(jnp.bfloat16).reshape(16, CAP * BR, HD),
+        pair,
         ("zl", "y", "xl"),
         split_axis=0,
         concat_axis=0,
         tiled=True,
     )
     summed = jnp.sum(pieces.astype(jnp.float32), axis=0).astype(jnp.bfloat16)
+
+    at = jnp.stack([lax.axis_index(a) for a in CTX])
+    heads_at = jnp.stack([lax.axis_index("zh"), lax.axis_index(("xh", "xl"))])
+    product = weight_product(heads_at, w, proj_weight)
+    product = jnp.stack([product, swap("zl", product)])
+    summed, product = lax.optimization_barrier((summed, product))
     grads = everywhere(summed, HEADS, 16)
-
-    at = jnp.stack([lax.axis_index(a) for a in CTX])
-    product = weight_product(lax.axis_index("zh").reshape(1), w, proj_weight)
-    product = jnp.stack([product, swap("zl", product)])
     product = ring(product, "y")
     d_vision = final_product(at, grads, product, [swap("co", p) for p in product])
     return (d_query, d_vision.T)

time: 142 us -> 124 us (0.87); the launches traced: 142 us -> 122 us
  blocking collectives: 29.8 us -> 0 us
  waiting for transfers between devices: 41.7 us -> 58.3 us
  between operations: 14.2 us -> 0.79 us
  starting transfers between devices: 27.7 us -> 39 us
  Pallas kernels: 21 us -> 15.2 us
  local copies, waits for them, and re-layouts: 2.91 us -> 6.16 us
  other arithmetic: 4.5 us -> 2.66 us
    all_to_all x1 -> x0, blocking collectives: 29.8 us -> none  [shards(): lax.all_to_all(pair.astype(jnp.bfloat16).reshape(16, CAP * BR, HD), ('zl'...]
    ppermute x6 -> x9, waiting for transfers between devices: 16.5 us -> 33.8 us  [ring(): lax.ppermute(array, axes, [(i, (i + k) % 4) for i in range(4)])]
    all_gather x1 -> x0, waiting for transfers between devices: 13.8 us -> none  [shards(): w = lax.all_gather(w, ('xh', 'xl'), axis=0, tiled=False)]
    all_to_all x2, waiting for transfers between devices: 0.01 us -> 11.4 us  [everywhere(): return lax.all_to_all(copies, axes, split_axis=0, concat_axis=0, tiled=True)]
    pallas_call x1, Pallas kernels: 8.51 us -> 2.75 us  [weight_product(): pl.pallas_call(product_kernel, in_specs=[pl.BlockSpec(memory_space=pltpu....]
    all_to_all x0 -> x1, starting transfers between devices: none -> 5.4 us  [shards(): lax.all_to_all(pair, ('zl', 'y', 'xl'), split_axis=0, concat_axis=0, tile...]
    ppermute x6 -> x9, starting transfers between devices: 14.5 us -> 18.1 us  [ring(): lax.ppermute(array, axes, [(i, (i + k) % 4) for i in range(4)])]
    unnamed x10 -> x12, local copies, waits for them, and re-layouts: 0.02 us -> 3.25 us
  transfers between devices with their start and end apart: 16 -> 19, of which waited for: 9 -> 11; matrix products, arithmetic and copies ran while one was open for 4% -> 1% of each run, Pallas kernels for 6% -> 10%
where the time goes in v3:
time: 124 us; the launch traced here: 122 us
  waiting for transfers between devices  58.3 us (47%)
  starting transfers between devices  39 us (31%)
  Pallas kernels  15.2 us (12%)
  local copies, waits for them, and re-layouts  6.16 us (5%)
  other arithmetic  2.66 us (2%)
    ppermute x9, waiting for transfers between devices, ring(): lax.ppermute(array, axes, [(i, (i + k) % 4) for i in range(4)])  33.8 us
    ppermute x9, starting transfers between devices, ring(): lax.ppermute(array, axes, [(i, (i + k) % 4) for i in range(4)])  18.1 us
    all_to_all x2, starting transfers between devices, everywhere(): return lax.all_to_all(copies, axes, split_axis=0, concat_axis=0, tiled=True)  12.9 us
    ppermute x7, waiting for transfers between devices, swap(): return lax.ppermute(array, axis, [(0, 1), (1, 0)])  12.6 us
    all_to_all x2, waiting for transfers between devices, everywhere(): return lax.all_to_all(copies, axes, split_axis=0, concat_axis=0, tiled=True)  11.4 us
    pallas_call x1, Pallas kernels, attention(): pl.pallas_call(attention_kernel, in_specs=[smem] * 3 + [vmem] * 5, out_sp...  10 us
    all_to_all x1, starting transfers between devices, shards(): lax.all_to_all(pair, ('zl', 'y', 'xl'), split_axis=0, concat_axis=0, tile...  5.4 us
    unnamed x12, local copies, waits for them, and re-layouts  3.25 us
  transfers between devices with their start and end apart: 19, of which 11 were waited for; matrix products, arithmetic and copies ran while one was open for 1% of the time, Pallas kernels for 10%

profile of v3, /device:TPU:64, one launch (start us, length us, event | category | flops | bytes accessed | tf_op | source)
XLA Modules:
  0.0 122.1 jit_solution(9453392601890340022)
XLA Ops:
  0.7 0.8 constant_dynamic-slice_fusion
  1.6 0.8 broadcast_in_dim.6
  2.4 5.8 %all-to-all-start = ((bf16[8,128,256]{2,1,0:T(8,128)(2,1)}), bf16[8,128,256]{2,1,0:T(8,128)(2,1)S(1)}, u32[]{:S(2)}, u32[]{:S(2)}) async-start(bf16[8,128,256]{2,1,0:T(8,128)(2,1)} %broadcast_in_dim.6), calls=%async_computation | async-start | bytes 1048576 | tf_op jit(solution)/shard_map/all_to_all | solution.py:173
  8.2 1.0 dynamic-slice_select_fusion
  9.2 3.7 %collective-permute-start = (bf16[512,128]{1,0:T(8,128)(2,1)S(1)}, bf16[512,128]{1,0:T(8,128)(2,1)S(1)}, u32[]{:S(2)}, u32[]{:S(2)}) collective-permute-start(bf16[512,128]{1,0:T(8,128)(2,1)S(1)} %dynamic-slice_select_fusion), channel_id=1, source_target_pairs={{0,4},{4,8},{8,12},{12,0},{1,5},{5,9},{9,13},{13,1},{2,6},{6,10},{... | collective-permute-start | bytes 393224 | tf_op jit(solution)/shard_map/ppermute | solution.py:181
  12.9 1.0 collective-permute-start.1
  13.9 2.8 %collective-permute-start.2 = (bf16[512,128]{1,0:T(8,128)(2,1)S(1)}, bf16[512,128]{1,0:T(8,128)(2,1)S(1)}, u32[]{:S(2)}, u32[]{:S(2)}) collective-permute-start(bf16[512,128]{1,0:T(8,128)(2,1)S(1)} %dynamic-slice_select_fusion), channel_id=1, source_target_pairs={{0,12},{4,0},{8,4},{12,8},{1,13},{5,1},{9,5},{13,9},{2,14},{6,2},{... | collective-permute-start | bytes 393224 | tf_op jit(solution)/shard_map/ppermute | solution.py:181
  16.7 6.8 %collective-permute-done = bf16[512,128]{1,0:T(8,128)(2,1)S(1)} collective-permute-done((bf16[512,128]{1,0:T(8,128)(2,1)S(1)}, bf16[512,128]{1,0:T(8,128)(2,1)S(1)}, u32[]{:S(2)}, u32[]{:S(2)}) %collective-permute-start) | collective-permute-done | bytes 131104 | tf_op jit(solution)/shard_map/ppermute | solution.py:181
  23.6 6.6 %collective-permute-done.1 = bf16[512,128]{1,0:T(8,128)(2,1)S(1)} collective-permute-done((bf16[512,128]{1,0:T(8,128)(2,1)S(1)}, bf16[512,128]{1,0:T(8,128)(2,1)S(1)}, u32[]{:S(2)}, u32[]{:S(2)}) %collective-permute-start.1) | collective-permute-done | bytes 131104 | tf_op jit(solution)/shard_map/ppermute | solution.py:181
  30.2 0.0 collective-permute-done.2
  30.2 0.0 all-to-all-done
  30.2 0.1 collective-permute-start.3
  30.3 1.6 %collective-permute-start.4 = (bf16[2048,128]{1,0:T(8,128)(2,1)S(1)}, bf16[2048,128]{1,0:T(8,128)(2,1)S(1)}, u32[]{:S(2)}, u32[]{:S(2)}) collective-permute-start(bf16[2048,128]{1,0:T(8,128)(2,1)S(1)} %pad_maximum_fusion.w0), channel_id=1, source_target_pairs={{0,1},{1,2},{2,3},{3,0},{4,5},{5,6},{6,7},{7,4},{8,9},{9,10},{10,1... | collective-permute-start | bytes 1572872 | tf_op jit(solution)/shard_map/ppermute | solution.py:181
  31.9 2.7 %collective-permute-start.5 = (bf16[2048,128]{1,0:T(8,128)(2,1)S(1)}, bf16[2048,128]{1,0:T(8,128)(2,1)S(1)}, u32[]{:S(2)}, u32[]{:S(2)}) collective-permute-start(bf16[2048,128]{1,0:T(8,128)(2,1)S(1)} %pad_maximum_fusion.w0), channel_id=1, source_target_pairs={{0,2},{1,3},{2,0},{3,1},{4,6},{5,7},{6,4},{7,5},{8,10},{9,11},{10,... | collective-permute-start | bytes 1572872 | tf_op jit(solution)/shard_map/ppermute | solution.py:181
  34.6 1.4 %collective-permute-start.6 = (bf16[2048,128]{1,0:T(8,128)(2,1)S(1)}, bf16[2048,128]{1,0:T(8,128)(2,1)S(1)}, u32[]{:S(2)}, u32[]{:S(2)}) collective-permute-start(bf16[2048,128]{1,0:T(8,128)(2,1)S(1)} %pad_maximum_fusion.w0), channel_id=1, source_target_pairs={{0,3},{1,0},{2,1},{3,2},{4,7},{5,4},{6,5},{7,6},{8,11},{9,8},{10,9... | collective-permute-start | bytes 1572872 | tf_op jit(solution)/shard_map/ppermute | solution.py:181
  36.1 0.0 collective-permute-done.3.kv1
  36.1 10.0 %attention.1 = (bf16[256,512]{1,0:T(8,128)(2,1)}, bf16[8,2,256,128]{3,2,1,0:T(8,128)(2,1)S(1)}, bf16[8,2,256,128]{3,2,1,0:T(8,128)(2,1)S(1)}) custom-call(s32[32]{0:T(128)S(1)} %copy-done.4, s32[16]{0:T(128)S(1)} %copy-done.5, s32[1]{0:T(128)} %bitcast.core, bf16[1024,256]{1,0:T(8,128)(2,1)S(1)} %bitcast.11, ...), custom_call_target="tpu_custom_call" | custom-call | flops 2684354560 | bytes 5242880 | tf_op jit(solution)/shard_map/attention/pallas_call | solution.py:93
  46.1 0.0 collective-permute-done.4.w1
  46.1 12.0 %collective-permute-done.5.w2 = bf16[2048,128]{1,0:T(8,128)(2,1)S(1)} collective-permute-done((bf16[2048,128]{1,0:T(8,128)(2,1)S(1)}, bf16[2048,128]{1,0:T(8,128)(2,1)S(1)}, u32[]{:S(2)}, u32[]{:S(2)}) %collective-permute-start.5) | collective-permute-done | bytes 524320 | tf_op jit(solution)/shard_map/ppermute | solution.py:181
  58.1 0.0 collective-permute-done.6.w3
  58.1 0.0 collective-permute-start.7
  58.1 2.7 %collective-permute-done.7 = bf16[8,2,256,128]{3,2,1,0:T(8,128)(2,1)S(1)} collective-permute-done((bf16[8,2,256,128]{3,2,1,0:T(8,128)(2,1)S(1)}, bf16[8,2,256,128]{3,2,1,0:T(8,128)(2,1)S(1)}, u32[]{:S(2)}, u32[]{:S(2)}) %collective-permute-start.7) | collective-permute-done | bytes 1048608 | tf_op jit(solution)/shard_map/ppermute | solution.py:177
  60.8 1.3 %add_convert_fusion = bf16[8,2,256,128]{3,2,1,0:T(8,128)(2,1)} fusion(bf16[8,2,256,128]{3,2,1,0:T(8,128)(2,1)S(1)} %collective-permute-done.7, bf16[8,2,256,128]{3,2,1,0:T(8,128)(2,1)S(1)} %get-tuple-element.16), kind=kLoop, calls=%fused_computation | loop fusion | flops 2097152 | bytes 3145728 | tf_op jit(solution)/shard_map/convert_element_type | solution.py:222
  62.1 5.4 %all-to-all-start.1 = ((bf16[16,256,128]{2,1,0:T(8,128)(2,1)}), bf16[16,256,128]{2,1,0:T(8,128)(2,1)S(1)}, u32[]{:S(2)}, u32[]{:S(2)}) async-start(bf16[16,256,128]{2,1,0:T(8,128)(2,1)} %bitcast.4), calls=%async_computation.1 | async-start | bytes 2097152 | tf_op jit(solution)/shard_map/all_to_all | solution.py:223
  67.5 0.1 pad_add_fusion.1.at
  67.5 3.2 %copy-done = bf16[480,8192]{1,0:T(8,128)(2,1)S(1)} copy-done((bf16[480,8192]{1,0:T(8,128)(2,1)S(1)}, bf16[480,8192]{1,0:T(8,128)(2,1)}, u32[]{:S(2)}) %copy-start) | copy-done | bytes 7864344
  70.8 2.7 %weight_product.1 = bf16[480,128]{1,0:T(8,128)(2,1)S(1)} custom-call(s32[2]{0:T(128)S(1)} %pad_add_fusion.1.at, bf16[2048,128]{1,0:T(8,128)(2,1)S(1)} %pad_maximum_fusion.w0, bf16[2048,128]{1,0:T(8,128)(2,1)S(1)} %collective-permute-done.4.w1, bf16[2048,128]{1,0:T(8,128)(2,1)S(1)} %collective-permute-done.5.w2, ...), custom_call_target="tpu_custom_call" | custom-call | flops 1006632960 | bytes 10485760 | tf_op jit(solution)/shard_map/weight_product/pallas_call | solution.py:126
  73.5 2.0 %collective-permute-start.8 = (bf16[480,128]{1,0:T(8,128)(2,1)S(1)}, bf16[480,128]{1,0:T(8,128)(2,1)S(1)}, u32[]{:S(2)}, u32[]{:S(2)}) collective-permute-start(bf16[480,128]{1,0:T(8,128)(2,1)S(1)} %weight_product.1), channel_id=1, source_target_pairs={{0,128},{128,0},{1,129},{129,1},{2,130},{130,2},{3,131},{131,3},{4... | collective-permute-start | bytes 368648 | tf_op jit(solution)/shard_map/ppermute | solution.py:177
  75.5 8.7 %collective-permute-done.8 = bf16[480,128]{1,0:T(8,128)(2,1)S(1)} collective-permute-done((bf16[480,128]{1,0:T(8,128)(2,1)S(1)}, bf16[480,128]{1,0:T(8,128)(2,1)S(1)}, u32[]{:S(2)}, u32[]{:S(2)}) %collective-permute-start.8) | collective-permute-done | bytes 122912 | tf_op jit(solution)/shard_map/ppermute | solution.py:177
  84.2 0.5 all-to-all-done.1
  84.7 0.1 reduce_sum.12
  84.8 1.2 broadcast_in_dim.7
  86.0 7.1 %all-to-all-start.2 = ((bf16[16,256,128]{2,1,0:T(8,128)(2,1)}), bf16[16,256,128]{2,1,0:T(8,128)(2,1)S(1)}, u32[]{:S(2)}, u32[]{:S(2)}) async-start(bf16[16,256,128]{2,1,0:T(8,128)(2,1)} %broadcast_in_dim.7), calls=%async_computation.2 | async-start | bytes 2097152 | tf_op jit(solution)/shard_map/all_to_all | solution.py:173
  93.2 0.7 collective-permute-start.9
  93.9 2.9 %collective-permute-start.10 = (bf16[2,480,128]{2,1,0:T(8,128)(2,1)S(1)}, bf16[2,480,128]{2,1,0:T(8,128)(2,1)S(1)}, u32[]{:S(2)}, u32[]{:S(2)}) collective-permute-start(bf16[2,480,128]{2,1,0:T(8,128)(2,1)S(1)} %pad_maximum_fusion.1.refs_0_), channel_id=1, source_target_pairs={{0,64},{32,96},{64,0},{96,32},{1,65},{33,97},{65,1},{97,33},{2,66}... | collective-permute-start | bytes 737288 | tf_op jit(solution)/shard_map/ppermute | solution.py:181
  96.8 1.2 collective-permute-start.11
  98.0 0.0 collective-permute-start.12
  98.0 4.6 %collective-permute-done.9.refs_1_ = bf16[2,480,128]{2,1,0:T(8,128)(2,1)S(1)} collective-permute-done((bf16[2,480,128]{2,1,0:T(8,128)(2,1)S(1)}, bf16[2,480,128]{2,1,0:T(8,128)(2,1)S(1)}, u32[]{:S(2)}, u32[]{:S(2)}) %collective-permute-start.9) | collective-permute-done | bytes 245792 | tf_op jit(solution)/shard_map/ppermute | solution.py:181
  102.6 0.0 collective-permute-start.13
  102.6 3.8 %collective-permute-done.10.refs_2_ = bf16[2,480,128]{2,1,0:T(8,128)(2,1)S(1)} collective-permute-done((bf16[2,480,128]{2,1,0:T(8,128)(2,1)S(1)}, bf16[2,480,128]{2,1,0:T(8,128)(2,1)S(1)}, u32[]{:S(2)}, u32[]{:S(2)}) %collective-permute-start.10) | collective-permute-done | bytes 245792 | tf_op jit(solution)/shard_map/ppermute | solution.py:181
  106.4 0.5 collective-permute-start.15
  106.9 0.1 pad_add_fusion.at
  107.0 0.0 collective-permute-done.12.refs_4_
  107.0 0.0 collective-permute-done.13.refs_5_
  107.0 0.9 collective-permute-done.14.refs_6_
  107.9 0.4 collective-permute-done.15.refs_7_
  108.2 11.4 %all-to-all-done.2.grads = bf16[16,256,128]{2,1,0:T(8,128)(2,1)S(1)} async-done(((bf16[16,256,128]{2,1,0:T(8,128)(2,1)}), bf16[16,256,128]{2,1,0:T(8,128)(2,1)S(1)}, u32[]{:S(2)}, u32[]{:S(2)}) %all-to-all-start.2) | async-done | bytes 1048608 | tf_op jit(solution)/shard_map/all_to_all | solution.py:173
  119.7 2.4 %final_product.1 = bf16[480,256]{1,0:T(8,128)(2,1)} custom-call(s32[3]{0:T(128)S(1)} %pad_add_fusion.at, bf16[16,256,128]{2,1,0:T(8,128)(2,1)S(1)} %all-to-all-done.2.grads, bf16[2,480,128]{2,1,0:T(8,128)(2,1)S(1)} %pad_maximum_fusion.1.refs_0_, bf16[2,480,128]{2,1,0:T(8,128)(2,1)S(1)} %collective-permute-done.9.refs_1_, ...), custom_call_target="tpu_custom_call" | custom-call | flops 503316480 | bytes 4194304 | tf_op jit(solution)/shard_map/final_product/pallas_call | solution.py:158
  (16 shorter events, 0.1 us)
Async XLA Ops:
  0.6 35.4 %copy-start.1 = (bf16[256,512]{1,0:T(8,128)(2,1)S(1)}, bf16[256,512]{1,0:T(8,128)(2,1)}, u32[]{:S(2)}) copy-start(bf16[256,512]{1,0:T(8,128)(2,1)} %q_ref.1) | copy-start | bytes 786436
  0.6 35.4 %copy-start.2 = (bf16[256,512]{1,0:T(8,128)(2,1)S(1)}, bf16[256,512]{1,0:T(8,128)(2,1)}, u32[]{:S(2)}) copy-start(bf16[256,512]{1,0:T(8,128)(2,1)} %do_ref.1) | copy-start | bytes 786436
  0.7 35.4 %copy-start.3 = (bf16[256,512]{1,0:T(8,128)(2,1)S(1)}, bf16[256,512]{1,0:T(8,128)(2,1)}, u32[]{:S(2)}) copy-start(bf16[256,512]{1,0:T(8,128)(2,1)} %ao_ref.1) | copy-start | bytes 786436
  0.7 35.4 %copy-start.4 = (s32[32]{0:T(128)S(1)}, s32[32]{0:T(128)}, u32[]{:S(2)}) copy-start(s32[32]{0:T(128)} %order.1) | copy-start | bytes 388
  0.7 35.4 %copy-start.5 = (s32[16]{0:T(128)S(1)}, s32[16]{0:T(128)}, u32[]{:S(2)}) copy-start(s32[16]{0:T(128)} %counts.1) | copy-start | bytes 196
  2.4 27.8 %all-to-all-start = ((bf16[8,128,256]{2,1,0:T(8,128)(2,1)}), bf16[8,128,256]{2,1,0:T(8,128)(2,1)S(1)}, u32[]{:S(2)}, u32[]{:S(2)}) async-start(bf16[8,128,256]{2,1,0:T(8,128)(2,1)} %broadcast_in_dim.6), calls=%async_computation | async-start | bytes 1048576 | tf_op jit(solution)/shard_map/all_to_all | solution.py:173
  9.2 14.3 %collective-permute-start = (bf16[512,128]{1,0:T(8,128)(2,1)S(1)}, bf16[512,128]{1,0:T(8,128)(2,1)S(1)}, u32[]{:S(2)}, u32[]{:S(2)}) collective-permute-start(bf16[512,128]{1,0:T(8,128)(2,1)S(1)} %dynamic-slice_select_fusion), channel_id=1, source_target_pairs={{0,4},{4,8},{8,12},{12,0},{1,5},{5,9},{9,13},{13,1},{2,6},{6,10},{... | collective-permute-start | bytes 393224 | tf_op jit(solution)/shard_map/ppermute | solution.py:181
  12.9 17.3 %collective-permute-start.1 = (bf16[512,128]{1,0:T(8,128)(2,1)S(1)}, bf16[512,128]{1,0:T(8,128)(2,1)S(1)}, u32[]{:S(2)}, u32[]{:S(2)}) collective-permute-start(bf16[512,128]{1,0:T(8,128)(2,1)S(1)} %dynamic-slice_select_fusion), channel_id=1, source_target_pairs={{0,8},{4,12},{8,0},{12,4},{1,9},{5,13},{9,1},{13,5},{2,10},{6,14},... | collective-permute-start | bytes 393224 | tf_op jit(solution)/shard_map/ppermute | solution.py:181
  13.9 16.3 %collective-permute-start.2 = (bf16[512,128]{1,0:T(8,128)(2,1)S(1)}, bf16[512,128]{1,0:T(8,128)(2,1)S(1)}, u32[]{:S(2)}, u32[]{:S(2)}) collective-permute-start(bf16[512,128]{1,0:T(8,128)(2,1)S(1)} %dynamic-slice_select_fusion), channel_id=1, source_target_pairs={{0,12},{4,0},{8,4},{12,8},{1,13},{5,1},{9,5},{13,9},{2,14},{6,2},{... | collective-permute-start | bytes 393224 | tf_op jit(solution)/shard_map/ppermute | solution.py:181
  30.2 5.8 %collective-permute-start.3 = (bf16[1024,256]{1,0:T(8,128)(2,1)S(1)}, bf16[1024,256]{1,0:T(8,128)(2,1)S(1)}, u32[]{:S(2)}, u32[]{:S(2)}) collective-permute-start(bf16[1024,256]{1,0:T(8,128)(2,1)S(1)} %bitcast.10), channel_id=1, source_target_pairs={{0,16},{16,0},{1,17},{17,1},{2,18},{18,2},{3,19},{19,3},{4,20},{20... | collective-permute-start | bytes 1572872 | tf_op jit(solution)/shard_map/ppermute | solution.py:177
  30.3 15.8 %collective-permute-start.4 = (bf16[2048,128]{1,0:T(8,128)(2,1)S(1)}, bf16[2048,128]{1,0:T(8,128)(2,1)S(1)}, u32[]{:S(2)}, u32[]{:S(2)}) collective-permute-start(bf16[2048,128]{1,0:T(8,128)(2,1)S(1)} %pad_maximum_fusion.w0), channel_id=1, source_target_pairs={{0,1},{1,2},{2,3},{3,0},{4,5},{5,6},{6,7},{7,4},{8,9},{9,10},{10,1... | collective-permute-start | bytes 1572872 | tf_op jit(solution)/shard_map/ppermute | solution.py:181
  31.9 26.2 %collective-permute-start.5 = (bf16[2048,128]{1,0:T(8,128)(2,1)S(1)}, bf16[2048,128]{1,0:T(8,128)(2,1)S(1)}, u32[]{:S(2)}, u32[]{:S(2)}) collective-permute-start(bf16[2048,128]{1,0:T(8,128)(2,1)S(1)} %pad_maximum_fusion.w0), channel_id=1, source_target_pairs={{0,2},{1,3},{2,0},{3,1},{4,6},{5,7},{6,4},{7,5},{8,10},{9,11},{10,... | collective-permute-start | bytes 1572872 | tf_op jit(solution)/shard_map/ppermute | solution.py:181
  34.6 23.5 %collective-permute-start.6 = (bf16[2048,128]{1,0:T(8,128)(2,1)S(1)}, bf16[2048,128]{1,0:T(8,128)(2,1)S(1)}, u32[]{:S(2)}, u32[]{:S(2)}) collective-permute-start(bf16[2048,128]{1,0:T(8,128)(2,1)S(1)} %pad_maximum_fusion.w0), channel_id=1, source_target_pairs={{0,3},{1,0},{2,1},{3,2},{4,7},{5,4},{6,5},{7,6},{8,11},{9,8},{10,9... | collective-permute-start | bytes 1572872 | tf_op jit(solution)/shard_map/ppermute | solution.py:181
  58.1 2.7 %collective-permute-start.7 = (bf16[8,2,256,128]{3,2,1,0:T(8,128)(2,1)S(1)}, bf16[8,2,256,128]{3,2,1,0:T(8,128)(2,1)S(1)}, u32[]{:S(2)}, u32[]{:S(2)}) collective-permute-start(bf16[8,2,256,128]{3,2,1,0:T(8,128)(2,1)S(1)} %get-tuple-element.19), channel_id=1, source_target_pairs={{0,16},{16,0},{1,17},{17,1},{2,18},{18,2},{3,19},{19,3},{4,20},{20... | collective-permute-start | bytes 3145736 | tf_op jit(solution)/shard_map/ppermute | solution.py:177
  62.1 22.6 %all-to-all-start.1 = ((bf16[16,256,128]{2,1,0:T(8,128)(2,1)}), bf16[16,256,128]{2,1,0:T(8,128)(2,1)S(1)}, u32[]{:S(2)}, u32[]{:S(2)}) async-start(bf16[16,256,128]{2,1,0:T(8,128)(2,1)} %bitcast.4), calls=%async_computation.1 | async-start | bytes 2097152 | tf_op jit(solution)/shard_map/all_to_all | solution.py:223
  67.5 3.2 %copy-start = (bf16[480,8192]{1,0:T(8,128)(2,1)S(1)}, bf16[480,8192]{1,0:T(8,128)(2,1)}, u32[]{:S(2)}) copy-start(bf16[480,8192]{1,0:T(8,128)(2,1)} %wp.1) | copy-start | bytes 23592964
  73.5 10.7 %collective-permute-start.8 = (bf16[480,128]{1,0:T(8,128)(2,1)S(1)}, bf16[480,128]{1,0:T(8,128)(2,1)S(1)}, u32[]{:S(2)}, u32[]{:S(2)}) collective-permute-start(bf16[480,128]{1,0:T(8,128)(2,1)S(1)} %weight_product.1), channel_id=1, source_target_pairs={{0,128},{128,0},{1,129},{129,1},{2,130},{130,2},{3,131},{131,3},{4... | collective-permute-start | bytes 368648 | tf_op jit(solution)/shard_map/ppermute | solution.py:177
  86.0 33.6 %all-to-all-start.2 = ((bf16[16,256,128]{2,1,0:T(8,128)(2,1)}), bf16[16,256,128]{2,1,0:T(8,128)(2,1)S(1)}, u32[]{:S(2)}, u32[]{:S(2)}) async-start(bf16[16,256,128]{2,1,0:T(8,128)(2,1)} %broadcast_in_dim.7), calls=%async_computation.2 | async-start | bytes 2097152 | tf_op jit(solution)/shard_map/all_to_all | solution.py:173
  93.2 9.4 %collective-permute-start.9 = (bf16[2,480,128]{2,1,0:T(8,128)(2,1)S(1)}, bf16[2,480,128]{2,1,0:T(8,128)(2,1)S(1)}, u32[]{:S(2)}, u32[]{:S(2)}) collective-permute-start(bf16[2,480,128]{2,1,0:T(8,128)(2,1)S(1)} %pad_maximum_fusion.1.refs_0_), channel_id=1, source_target_pairs={{0,32},{32,64},{64,96},{96,0},{1,33},{33,65},{65,97},{97,1},{2,34}... | collective-permute-start | bytes 737288 | tf_op jit(solution)/shard_map/ppermute | solution.py:181
  93.9 12.5 %collective-permute-start.10 = (bf16[2,480,128]{2,1,0:T(8,128)(2,1)S(1)}, bf16[2,480,128]{2,1,0:T(8,128)(2,1)S(1)}, u32[]{:S(2)}, u32[]{:S(2)}) collective-permute-start(bf16[2,480,128]{2,1,0:T(8,128)(2,1)S(1)} %pad_maximum_fusion.1.refs_0_), channel_id=1, source_target_pairs={{0,64},{32,96},{64,0},{96,32},{1,65},{33,97},{65,1},{97,33},{2,66}... | collective-permute-start | bytes 737288 | tf_op jit(solution)/shard_map/ppermute | solution.py:181
  96.8 9.6 %collective-permute-start.11 = (bf16[2,480,128]{2,1,0:T(8,128)(2,1)S(1)}, bf16[2,480,128]{2,1,0:T(8,128)(2,1)S(1)}, u32[]{:S(2)}, u32[]{:S(2)}) collective-permute-start(bf16[2,480,128]{2,1,0:T(8,128)(2,1)S(1)} %pad_maximum_fusion.1.refs_0_), channel_id=1, source_target_pairs={{0,96},{32,0},{64,32},{96,64},{1,97},{33,1},{65,33},{97,65},{2,98}... | collective-permute-start | bytes 737288 | tf_op jit(solution)/shard_map/ppermute | solution.py:181
  98.0 9.0 %collective-permute-start.12 = (bf16[2,480,128]{2,1,0:T(8,128)(2,1)S(1)}, bf16[2,480,128]{2,1,0:T(8,128)(2,1)S(1)}, u32[]{:S(2)}, u32[]{:S(2)}) collective-permute-start(bf16[2,480,128]{2,1,0:T(8,128)(2,1)S(1)} %pad_maximum_fusion.1.refs_0_), channel_id=1, source_target_pairs={{0,16},{16,0},{1,17},{17,1},{2,18},{18,2},{3,19},{19,3},{4,20},{20... | collective-permute-start | bytes 737288 | tf_op jit(solution)/shard_map/ppermute | solution.py:177
  102.6 4.4 %collective-permute-start.13 = (bf16[2,480,128]{2,1,0:T(8,128)(2,1)S(1)}, bf16[2,480,128]{2,1,0:T(8,128)(2,1)S(1)}, u32[]{:S(2)}, u32[]{:S(2)}) collective-permute-start(bf16[2,480,128]{2,1,0:T(8,128)(2,1)S(1)} %collective-permute-done.9.refs_1_), channel_id=1, source_target_pairs={{0,16},{16,0},{1,17},{17,1},{2,18},{18,2},{3,19},{19,3},{4,20},{20... | collective-permute-start | bytes 737288 | tf_op jit(solution)/shard_map/ppermute | solution.py:177
  106.4 1.5 %collective-permute-start.14 = (bf16[2,480,128]{2,1,0:T(8,128)(2,1)S(1)}, bf16[2,480,128]{2,1,0:T(8,128)(2,1)S(1)}, u32[]{:S(2)}, u32[]{:S(2)}) collective-permute-start(bf16[2,480,128]{2,1,0:T(8,128)(2,1)S(1)} %collective-permute-done.10.refs_2_), channel_id=1, source_target_pairs={{0,16},{16,0},{1,17},{17,1},{2,18},{18,2},{3,19},{19,3},{4,20},{20... | collective-permute-start | bytes 737288 | tf_op jit(solution)/shard_map/ppermute | solution.py:177
  106.4 1.9 %collective-permute-start.15 = (bf16[2,480,128]{2,1,0:T(8,128)(2,1)S(1)}, bf16[2,480,128]{2,1,0:T(8,128)(2,1)S(1)}, u32[]{:S(2)}, u32[]{:S(2)}) collective-permute-start(bf16[2,480,128]{2,1,0:T(8,128)(2,1)S(1)} %collective-permute-done.11.refs_3_), channel_id=1, source_target_pairs={{0,16},{16,0},{1,17},{17,1},{2,18},{18,2},{3,19},{19,3},{4,20},{20... | collective-permute-start | bytes 737288 | tf_op jit(solution)/shard_map/ppermute | solution.py:177

commit v4 on v3

--- a/solution.py
+++ b/solution.py
@@ -130,7 +130,7 @@
         out_shape=jax.ShapeDtypeStruct((width, HD), jnp.bfloat16),
         compiler_params=pltpu.CompilerParams(vmem_limit_bytes=14 << 20),
         cost_estimate=pl.CostEstimate(
-            flops=2 * width * model * HD, transcendentals=0, bytes_accessed=10 << 20
+            flops=40 * width * model * HD, transcendentals=0, bytes_accessed=10 << 20
         ),
         name="weight_product",
     )(at, *pieces, proj_weight)
@@ -217,7 +217,6 @@
     d_query, mine, other = attention(
         block_order, owner_counts, core.reshape(1), kv, swap("co", kv), queries, out_grad, attn_out
     )
-    other, *w = lax.optimization_barrier((other, *w))
     pair = mine.astype(jnp.float32) + swap("co", other).astype(jnp.float32)
     pair = pair.astype(jnp.bfloat16).reshape(16, CAP * BR, HD)
     pieces = lax.all_to_all(
@@ -233,7 +232,6 @@
     heads_at = jnp.stack([lax.axis_index("zh"), lax.axis_index(("xh", "xl"))])
     product = weight_product(heads_at, w, proj_weight)
     product = jnp.stack([product, swap("zl", product)])
-    summed, product = lax.optimization_barrier((summed, product))
     grads = everywhere(summed, HEADS, 16)
     product = ring(product, "y")
     d_vision = final_product(at, grads, product, [swap("co", p) for p in product])

time: 124 us -> 130 us (1.048)
  starting transfers between devices: 39 us -> 51.8 us
  waiting for transfers between devices: 58.3 us -> 51.3 us
    all_to_all x2, waiting for transfers between devices: 11.4 us -> 0.01 us  [everywhere(): return lax.all_to_all(copies, axes, split_axis=0, concat_axis=0, tiled=True)]
    all_to_all x1, waiting for transfers between devices: 0.46 us -> 10.6 us  [shards(): lax.all_to_all(pair, ('zl', 'y', 'xl'), split_axis=0, concat_axis=0, tile...]
    ppermute x7, starting transfers between devices: 2.62 us -> 8.67 us  [swap(): return lax.ppermute(array, axis, [(0, 1), (1, 0)])]
    all_to_all x1, starting transfers between devices: 5.4 us -> 10.9 us  [shards(): lax.all_to_all(pair, ('zl', 'y', 'xl'), split_axis=0, concat_axis=0, tile...]
    ppermute x7, waiting for transfers between devices: 12.6 us -> 8.56 us  [swap(): return lax.ppermute(array, axis, [(0, 1), (1, 0)])]
    ppermute x9, starting transfers between devices: 18.1 us -> 20.1 us  [ring(): lax.ppermute(array, axes, [(i, (i + k) % 4) for i in range(4)])]
    ppermute x9, waiting for transfers between devices: 33.8 us -> 32.1 us  [ring(): lax.ppermute(array, axes, [(i, (i + k) % 4) for i in range(4)])]
  transfers between devices with their start and end apart: 19 -> 19, of which waited for: 11 -> 11; matrix products, arithmetic and copies ran while one was open for 1% -> 2% of each run, Pallas kernels for 10% -> 2%
where the time goes in v4:
time: 130 us; the launch traced here: 128 us
  starting transfers between devices  51.8 us (40%)
  waiting for transfers between devices  51.3 us (39%)
  Pallas kernels  15.2 us (12%)
  local copies, waits for them, and re-layouts  6.17 us (5%)
  other arithmetic  2.66 us (2%)
    ppermute x9, waiting for transfers between devices, ring(): lax.ppermute(array, axes, [(i, (i + k) % 4) for i in range(4)])  32.1 us
    ppermute x9, starting transfers between devices, ring(): lax.ppermute(array, axes, [(i, (i + k) % 4) for i in range(4)])  20.1 us
    all_to_all x2, starting transfers between devices, everywhere(): return lax.all_to_all(copies, axes, split_axis=0, concat_axis=0, tiled=True)  12.2 us
    all_to_all x1, starting transfers between devices, shards(): lax.all_to_all(pair, ('zl', 'y', 'xl'), split_axis=0, concat_axis=0, tile...  10.9 us
    all_to_all x1, waiting for transfers between devices, shards(): lax.all_to_all(pair, ('zl', 'y', 'xl'), split_axis=0, concat_axis=0, tile...  10.6 us
    pallas_call x1, Pallas kernels, attention(): pl.pallas_call(attention_kernel, in_specs=[smem] * 3 + [vmem] * 5, out_sp...  10 us
    ppermute x7, starting transfers between devices, swap(): return lax.ppermute(array, axis, [(0, 1), (1, 0)])  8.67 us
    ppermute x7, waiting for transfers between devices, swap(): return lax.ppermute(array, axis, [(0, 1), (1, 0)])  8.56 us
  transfers between devices with their start and end apart: 19, of which 11 were waited for; matrix products, arithmetic and copies ran while one was open for 2% of the time, Pallas kernels for 2%

profile of v4, /device:TPU:64, one launch (start us, length us, event | category | flops | bytes accessed | tf_op | source)
XLA Modules:
  0.0 127.9 jit_solution(7520870085418347093)
XLA Ops:
  0.7 0.9 constant_dynamic-slice_fusion
  1.6 0.8 broadcast_in_dim.6
  2.4 5.8 %all-to-all-start = ((bf16[8,128,256]{2,1,0:T(8,128)(2,1)}), bf16[8,128,256]{2,1,0:T(8,128)(2,1)S(1)}, u32[]{:S(2)}, u32[]{:S(2)}) async-start(bf16[8,128,256]{2,1,0:T(8,128)(2,1)} %broadcast_in_dim.6), calls=%async_computation | async-start | bytes 1048576 | tf_op jit(solution)/shard_map/all_to_all | solution.py:173
  8.2 1.0 dynamic-slice_select_fusion
  9.2 0.1 collective-permute-start.2
  9.3 5.9 %collective-permute-start.1 = (bf16[512,128]{1,0:T(8,128)(2,1)S(1)}, bf16[512,128]{1,0:T(8,128)(2,1)S(1)}, u32[]{:S(2)}, u32[]{:S(2)}) collective-permute-start(bf16[512,128]{1,0:T(8,128)(2,1)S(1)} %dynamic-slice_select_fusion), channel_id=1, source_target_pairs={{0,8},{4,12},{8,0},{12,4},{1,9},{5,13},{9,1},{13,5},{2,10},{6,14},... | collective-permute-start | bytes 393224 | tf_op jit(solution)/shard_map/ppermute | solution.py:181
  15.3 2.7 %collective-permute-start = (bf16[512,128]{1,0:T(8,128)(2,1)S(1)}, bf16[512,128]{1,0:T(8,128)(2,1)S(1)}, u32[]{:S(2)}, u32[]{:S(2)}) collective-permute-start(bf16[512,128]{1,0:T(8,128)(2,1)S(1)} %dynamic-slice_select_fusion), channel_id=1, source_target_pairs={{0,4},{4,8},{8,12},{12,0},{1,5},{5,9},{9,13},{13,1},{2,6},{6,10},{... | collective-permute-start | bytes 393224 | tf_op jit(solution)/shard_map/ppermute | solution.py:181
  17.9 0.0 collective-permute-done.2
  17.9 7.8 %collective-permute-done.1 = bf16[512,128]{1,0:T(8,128)(2,1)S(1)} collective-permute-done((bf16[512,128]{1,0:T(8,128)(2,1)S(1)}, bf16[512,128]{1,0:T(8,128)(2,1)S(1)}, u32[]{:S(2)}, u32[]{:S(2)}) %collective-permute-start.1) | collective-permute-done | bytes 131104 | tf_op jit(solution)/shard_map/ppermute | solution.py:181
  25.7 0.0 collective-permute-done
  25.8 0.0 all-to-all-done
  25.8 0.1 collective-permute-start.3
  25.9 1.9 %collective-permute-done.3.kv1 = bf16[1024,256]{1,0:T(8,128)(2,1)S(1)} collective-permute-done((bf16[1024,256]{1,0:T(8,128)(2,1)S(1)}, bf16[1024,256]{1,0:T(8,128)(2,1)S(1)}, u32[]{:S(2)}, u32[]{:S(2)}) %collective-permute-start.3) | collective-permute-done | bytes 524320 | tf_op jit(solution)/shard_map/ppermute | solution.py:177
  27.8 10.0 %attention.1 = (bf16[256,512]{1,0:T(8,128)(2,1)}, bf16[8,2,256,128]{3,2,1,0:T(8,128)(2,1)S(1)}, bf16[8,2,256,128]{3,2,1,0:T(8,128)(2,1)S(1)}) custom-call(s32[32]{0:T(128)S(1)} %copy-done.4, s32[16]{0:T(128)S(1)} %copy-done.5, s32[1]{0:T(128)} %bitcast.core, bf16[1024,256]{1,0:T(8,128)(2,1)S(1)} %bitcast.11, ...), custom_call_target="tpu_custom_call" | custom-call | flops 2684354560 | bytes 5242880 | tf_op jit(solution)/shard_map/attention/pallas_call | solution.py:93
  37.8 0.1 collective-permute-start.4
  38.0 2.5 %collective-permute-done.4 = bf16[8,2,256,128]{3,2,1,0:T(8,128)(2,1)S(1)} collective-permute-done((bf16[8,2,256,128]{3,2,1,0:T(8,128)(2,1)S(1)}, bf16[8,2,256,128]{3,2,1,0:T(8,128)(2,1)S(1)}, u32[]{:S(2)}, u32[]{:S(2)}) %collective-permute-start.4) | collective-permute-done | bytes 1048608 | tf_op jit(solution)/shard_map/ppermute | solution.py:177
  40.5 1.3 %add_convert_fusion = bf16[8,2,256,128]{3,2,1,0:T(8,128)(2,1)} fusion(bf16[8,2,256,128]{3,2,1,0:T(8,128)(2,1)S(1)} %collective-permute-done.4, bf16[8,2,256,128]{3,2,1,0:T(8,128)(2,1)S(1)} %get-tuple-element.9), kind=kLoop, calls=%fused_computation | loop fusion | flops 2097152 | bytes 3145728 | tf_op jit(solution)/shard_map/convert_element_type | solution.py:221
  41.8 10.9 %all-to-all-start.1 = ((bf16[16,256,128]{2,1,0:T(8,128)(2,1)}), bf16[16,256,128]{2,1,0:T(8,128)(2,1)S(1)}, u32[]{:S(2)}, u32[]{:S(2)}) async-start(bf16[16,256,128]{2,1,0:T(8,128)(2,1)} %bitcast.4), calls=%async_computation.1 | async-start | bytes 2097152 | tf_op jit(solution)/shard_map/all_to_all | solution.py:222
  52.7 1.9 %collective-permute-start.5 = (bf16[2048,128]{1,0:T(8,128)(2,1)S(1)}, bf16[2048,128]{1,0:T(8,128)(2,1)S(1)}, u32[]{:S(2)}, u32[]{:S(2)}) collective-permute-start(bf16[2048,128]{1,0:T(8,128)(2,1)S(1)} %pad_maximum_fusion.w0), channel_id=1, source_target_pairs={{0,1},{1,2},{2,3},{3,0},{4,5},{5,6},{6,7},{7,4},{8,9},{9,10},{10,1... | collective-permute-start | bytes 1572872 | tf_op jit(solution)/shard_map/ppermute | solution.py:181
  54.6 2.7 %collective-permute-start.6 = (bf16[2048,128]{1,0:T(8,128)(2,1)S(1)}, bf16[2048,128]{1,0:T(8,128)(2,1)S(1)}, u32[]{:S(2)}, u32[]{:S(2)}) collective-permute-start(bf16[2048,128]{1,0:T(8,128)(2,1)S(1)} %pad_maximum_fusion.w0), channel_id=1, source_target_pairs={{0,2},{1,3},{2,0},{3,1},{4,6},{5,7},{6,4},{7,5},{8,10},{9,11},{10,... | collective-permute-start | bytes 1572872 | tf_op jit(solution)/shard_map/ppermute | solution.py:181
  57.4 0.8 collective-permute-start.7
  58.1 0.1 pad_add_fusion.1.at
  58.2 10.6 %all-to-all-done.1 = bf16[16,256,128]{2,1,0:T(8,128)(2,1)S(1)} async-done(((bf16[16,256,128]{2,1,0:T(8,128)(2,1)}), bf16[16,256,128]{2,1,0:T(8,128)(2,1)S(1)}, u32[]{:S(2)}, u32[]{:S(2)}) %all-to-all-start.1) | async-done | bytes 1048608 | tf_op jit(solution)/shard_map/all_to_all | solution.py:222
  68.8 0.1 reduce_sum.12
  69.0 1.2 broadcast_in_dim.7
  70.2 6.4 %all-to-all-start.2 = ((bf16[16,256,128]{2,1,0:T(8,128)(2,1)}), bf16[16,256,128]{2,1,0:T(8,128)(2,1)S(1)}, u32[]{:S(2)}, u32[]{:S(2)}) async-start(bf16[16,256,128]{2,1,0:T(8,128)(2,1)} %broadcast_in_dim.7), calls=%async_computation.2 | async-start | bytes 2097152 | tf_op jit(solution)/shard_map/all_to_all | solution.py:173
  76.6 0.6 collective-permute-done.5.w1
  77.2 17.2 %collective-permute-done.6.w2 = bf16[2048,128]{1,0:T(8,128)(2,1)S(1)} collective-permute-done((bf16[2048,128]{1,0:T(8,128)(2,1)S(1)}, bf16[2048,128]{1,0:T(8,128)(2,1)S(1)}, u32[]{:S(2)}, u32[]{:S(2)}) %collective-permute-start.6) | collective-permute-done | bytes 524320 | tf_op jit(solution)/shard_map/ppermute | solution.py:181
  94.4 0.0 collective-permute-done.7.w3
  94.4 3.2 %copy-done = bf16[480,8192]{1,0:T(8,128)(2,1)S(1)} copy-done((bf16[480,8192]{1,0:T(8,128)(2,1)S(1)}, bf16[480,8192]{1,0:T(8,128)(2,1)}, u32[]{:S(2)}) %copy-start) | copy-done | bytes 7864344
  97.6 2.7 %weight_product.1 = bf16[480,128]{1,0:T(8,128)(2,1)S(1)} custom-call(s32[2]{0:T(128)S(1)} %pad_add_fusion.1.at, bf16[2048,128]{1,0:T(8,128)(2,1)S(1)} %pad_maximum_fusion.w0, bf16[2048,128]{1,0:T(8,128)(2,1)S(1)} %collective-permute-done.5.w1, bf16[2048,128]{1,0:T(8,128)(2,1)S(1)} %collective-permute-done.6.w2, ...), custom_call_target="tpu_custom_call" | custom-call | flops 20132659200 | bytes 10485760 | tf_op jit(solution)/shard_map/weight_product/pallas_call | solution.py:126
  100.4 7.9 %collective-permute-start.8 = (bf16[480,128]{1,0:T(8,128)(2,1)S(1)}, bf16[480,128]{1,0:T(8,128)(2,1)S(1)}, u32[]{:S(2)}, u32[]{:S(2)}) collective-permute-start(bf16[480,128]{1,0:T(8,128)(2,1)S(1)} %weight_product.1), channel_id=1, source_target_pairs={{0,128},{128,0},{1,129},{129,1},{2,130},{130,2},{3,131},{131,3},{4... | collective-permute-start | bytes 368648 | tf_op jit(solution)/shard_map/ppermute | solution.py:177
  108.3 2.9 %collective-permute-done.8 = bf16[480,128]{1,0:T(8,128)(2,1)S(1)} collective-permute-done((bf16[480,128]{1,0:T(8,128)(2,1)S(1)}, bf16[480,128]{1,0:T(8,128)(2,1)S(1)}, u32[]{:S(2)}, u32[]{:S(2)}) %collective-permute-start.8) | collective-permute-done | bytes 122912 | tf_op jit(solution)/shard_map/ppermute | solution.py:177
  111.2 1.3 %collective-permute-start.9 = (bf16[2,480,128]{2,1,0:T(8,128)(2,1)S(1)}, bf16[2,480,128]{2,1,0:T(8,128)(2,1)S(1)}, u32[]{:S(2)}, u32[]{:S(2)}) collective-permute-start(bf16[2,480,128]{2,1,0:T(8,128)(2,1)S(1)} %pad_maximum_fusion.1.refs_0_), channel_id=1, source_target_pairs={{0,32},{32,64},{64,96},{96,0},{1,33},{33,65},{65,97},{97,1},{2,34}... | collective-permute-start | bytes 737288 | tf_op jit(solution)/shard_map/ppermute | solution.py:181
  112.6 2.9 %collective-permute-start.10 = (bf16[2,480,128]{2,1,0:T(8,128)(2,1)S(1)}, bf16[2,480,128]{2,1,0:T(8,128)(2,1)S(1)}, u32[]{:S(2)}, u32[]{:S(2)}) collective-permute-start(bf16[2,480,128]{2,1,0:T(8,128)(2,1)S(1)} %pad_maximum_fusion.1.refs_0_), channel_id=1, source_target_pairs={{0,64},{32,96},{64,0},{96,32},{1,65},{33,97},{65,1},{97,33},{2,66}... | collective-permute-start | bytes 737288 | tf_op jit(solution)/shard_map/ppermute | solution.py:181
  115.5 1.6 %collective-permute-start.11 = (bf16[2,480,128]{2,1,0:T(8,128)(2,1)S(1)}, bf16[2,480,128]{2,1,0:T(8,128)(2,1)S(1)}, u32[]{:S(2)}, u32[]{:S(2)}) collective-permute-start(bf16[2,480,128]{2,1,0:T(8,128)(2,1)S(1)} %pad_maximum_fusion.1.refs_0_), channel_id=1, source_target_pairs={{0,96},{32,0},{64,32},{96,64},{1,97},{33,1},{65,33},{97,65},{2,98}... | collective-permute-start | bytes 737288 | tf_op jit(solution)/shard_map/ppermute | solution.py:181
  117.2 0.0 collective-permute-start.12
  117.2 3.8 %collective-permute-done.9.refs_1_ = bf16[2,480,128]{2,1,0:T(8,128)(2,1)S(1)} collective-permute-done((bf16[2,480,128]{2,1,0:T(8,128)(2,1)S(1)}, bf16[2,480,128]{2,1,0:T(8,128)(2,1)S(1)}, u32[]{:S(2)}, u32[]{:S(2)}) %collective-permute-start.9) | collective-permute-done | bytes 245792 | tf_op jit(solution)/shard_map/ppermute | solution.py:181
  121.0 0.0 collective-permute-start.13
  121.0 2.6 %collective-permute-done.10.refs_2_ = bf16[2,480,128]{2,1,0:T(8,128)(2,1)S(1)} collective-permute-done((bf16[2,480,128]{2,1,0:T(8,128)(2,1)S(1)}, bf16[2,480,128]{2,1,0:T(8,128)(2,1)S(1)}, u32[]{:S(2)}, u32[]{:S(2)}) %collective-permute-start.10) | collective-permute-done | bytes 245792 | tf_op jit(solution)/shard_map/ppermute | solution.py:181
  123.6 0.0 collective-permute-start.14
  123.6 0.0 collective-permute-done.11.refs_3_
  123.6 0.5 collective-permute-start.15
  124.1 0.1 pad_add_fusion.at
  124.2 0.9 collective-permute-done.14.refs_6_
  125.1 0.4 collective-permute-done.15.refs_7_
  125.5 0.0 all-to-all-done.2.grads
  125.5 2.4 %final_product.1 = bf16[480,256]{1,0:T(8,128)(2,1)} custom-call(s32[3]{0:T(128)S(1)} %pad_add_fusion.at, bf16[16,256,128]{2,1,0:T(8,128)(2,1)S(1)} %all-to-all-done.2.grads, bf16[2,480,128]{2,1,0:T(8,128)(2,1)S(1)} %pad_maximum_fusion.1.refs_0_, bf16[2,480,128]{2,1,0:T(8,128)(2,1)S(1)} %collective-permute-done.9.refs_1_, ...), custom_call_target="tpu_custom_call" | custom-call | flops 503316480 | bytes 4194304 | tf_op jit(solution)/shard_map/final_product/pallas_call | solution.py:158
  (16 shorter events, 0.1 us)
Async XLA Ops:
  0.6 27.2 %copy-start.4 = (s32[32]{0:T(128)S(1)}, s32[32]{0:T(128)}, u32[]{:S(2)}) copy-start(s32[32]{0:T(128)} %order.1) | copy-start | bytes 388
  0.6 27.2 %copy-start.5 = (s32[16]{0:T(128)S(1)}, s32[16]{0:T(128)}, u32[]{:S(2)}) copy-start(s32[16]{0:T(128)} %counts.1) | copy-start | bytes 196
  0.7 27.2 %copy-start.1 = (bf16[256,512]{1,0:T(8,128)(2,1)S(1)}, bf16[256,512]{1,0:T(8,128)(2,1)}, u32[]{:S(2)}) copy-start(bf16[256,512]{1,0:T(8,128)(2,1)} %q_ref.1) | copy-start | bytes 786436
  0.7 27.1 %copy-start.2 = (bf16[256,512]{1,0:T(8,128)(2,1)S(1)}, bf16[256,512]{1,0:T(8,128)(2,1)}, u32[]{:S(2)}) copy-start(bf16[256,512]{1,0:T(8,128)(2,1)} %do_ref.1) | copy-start | bytes 786436
  0.7 27.1 %copy-start.3 = (bf16[256,512]{1,0:T(8,128)(2,1)S(1)}, bf16[256,512]{1,0:T(8,128)(2,1)}, u32[]{:S(2)}) copy-start(bf16[256,512]{1,0:T(8,128)(2,1)} %ao_ref.1) | copy-start | bytes 786436
  2.4 23.4 %all-to-all-start = ((bf16[8,128,256]{2,1,0:T(8,128)(2,1)}), bf16[8,128,256]{2,1,0:T(8,128)(2,1)S(1)}, u32[]{:S(2)}, u32[]{:S(2)}) async-start(bf16[8,128,256]{2,1,0:T(8,128)(2,1)} %broadcast_in_dim.6), calls=%async_computation | async-start | bytes 1048576 | tf_op jit(solution)/shard_map/all_to_all | solution.py:173
  9.2 8.7 %collective-permute-start.2 = (bf16[512,128]{1,0:T(8,128)(2,1)S(1)}, bf16[512,128]{1,0:T(8,128)(2,1)S(1)}, u32[]{:S(2)}, u32[]{:S(2)}) collective-permute-start(bf16[512,128]{1,0:T(8,128)(2,1)S(1)} %dynamic-slice_select_fusion), channel_id=1, source_target_pairs={{0,12},{4,0},{8,4},{12,8},{1,13},{5,1},{9,5},{13,9},{2,14},{6,2},{... | collective-permute-start | bytes 393224 | tf_op jit(solution)/shard_map/ppermute | solution.py:181
  9.3 16.4 %collective-permute-start.1 = (bf16[512,128]{1,0:T(8,128)(2,1)S(1)}, bf16[512,128]{1,0:T(8,128)(2,1)S(1)}, u32[]{:S(2)}, u32[]{:S(2)}) collective-permute-start(bf16[512,128]{1,0:T(8,128)(2,1)S(1)} %dynamic-slice_select_fusion), channel_id=1, source_target_pairs={{0,8},{4,12},{8,0},{12,4},{1,9},{5,13},{9,1},{13,5},{2,10},{6,14},... | collective-permute-start | bytes 393224 | tf_op jit(solution)/shard_map/ppermute | solution.py:181
  15.3 10.5 %collective-permute-start = (bf16[512,128]{1,0:T(8,128)(2,1)S(1)}, bf16[512,128]{1,0:T(8,128)(2,1)S(1)}, u32[]{:S(2)}, u32[]{:S(2)}) collective-permute-start(bf16[512,128]{1,0:T(8,128)(2,1)S(1)} %dynamic-slice_select_fusion), channel_id=1, source_target_pairs={{0,4},{4,8},{8,12},{12,0},{1,5},{5,9},{9,13},{13,1},{2,6},{6,10},{... | collective-permute-start | bytes 393224 | tf_op jit(solution)/shard_map/ppermute | solution.py:181
  25.8 2.0 %collective-permute-start.3 = (bf16[1024,256]{1,0:T(8,128)(2,1)S(1)}, bf16[1024,256]{1,0:T(8,128)(2,1)S(1)}, u32[]{:S(2)}, u32[]{:S(2)}) collective-permute-start(bf16[1024,256]{1,0:T(8,128)(2,1)S(1)} %bitcast.10), channel_id=1, source_target_pairs={{0,16},{16,0},{1,17},{17,1},{2,18},{18,2},{3,19},{19,3},{4,20},{20... | collective-permute-start | bytes 1572872 | tf_op jit(solution)/shard_map/ppermute | solution.py:177
  37.8 2.7 %collective-permute-start.4 = (bf16[8,2,256,128]{3,2,1,0:T(8,128)(2,1)S(1)}, bf16[8,2,256,128]{3,2,1,0:T(8,128)(2,1)S(1)}, u32[]{:S(2)}, u32[]{:S(2)}) collective-permute-start(bf16[8,2,256,128]{3,2,1,0:T(8,128)(2,1)S(1)} %get-tuple-element.10), channel_id=1, source_target_pairs={{0,16},{16,0},{1,17},{17,1},{2,18},{18,2},{3,19},{19,3},{4,20},{20... | collective-permute-start | bytes 3145736 | tf_op jit(solution)/shard_map/ppermute | solution.py:177
  41.8 27.0 %all-to-all-start.1 = ((bf16[16,256,128]{2,1,0:T(8,128)(2,1)}), bf16[16,256,128]{2,1,0:T(8,128)(2,1)S(1)}, u32[]{:S(2)}, u32[]{:S(2)}) async-start(bf16[16,256,128]{2,1,0:T(8,128)(2,1)} %bitcast.4), calls=%async_computation.1 | async-start | bytes 2097152 | tf_op jit(solution)/shard_map/all_to_all | solution.py:222
  52.7 24.5 %collective-permute-start.5 = (bf16[2048,128]{1,0:T(8,128)(2,1)S(1)}, bf16[2048,128]{1,0:T(8,128)(2,1)S(1)}, u32[]{:S(2)}, u32[]{:S(2)}) collective-permute-start(bf16[2048,128]{1,0:T(8,128)(2,1)S(1)} %pad_maximum_fusion.w0), channel_id=1, source_target_pairs={{0,1},{1,2},{2,3},{3,0},{4,5},{5,6},{6,7},{7,4},{8,9},{9,10},{10,1... | collective-permute-start | bytes 1572872 | tf_op jit(solution)/shard_map/ppermute | solution.py:181
  54.6 39.8 %collective-permute-start.6 = (bf16[2048,128]{1,0:T(8,128)(2,1)S(1)}, bf16[2048,128]{1,0:T(8,128)(2,1)S(1)}, u32[]{:S(2)}, u32[]{:S(2)}) collective-permute-start(bf16[2048,128]{1,0:T(8,128)(2,1)S(1)} %pad_maximum_fusion.w0), channel_id=1, source_target_pairs={{0,2},{1,3},{2,0},{3,1},{4,6},{5,7},{6,4},{7,5},{8,10},{9,11},{10,... | collective-permute-start | bytes 1572872 | tf_op jit(solution)/shard_map/ppermute | solution.py:181
  57.4 37.1 %collective-permute-start.7 = (bf16[2048,128]{1,0:T(8,128)(2,1)S(1)}, bf16[2048,128]{1,0:T(8,128)(2,1)S(1)}, u32[]{:S(2)}, u32[]{:S(2)}) collective-permute-start(bf16[2048,128]{1,0:T(8,128)(2,1)S(1)} %pad_maximum_fusion.w0), channel_id=1, source_target_pairs={{0,3},{1,0},{2,1},{3,2},{4,7},{5,4},{6,5},{7,6},{8,11},{9,8},{10,9... | collective-permute-start | bytes 1572872 | tf_op jit(solution)/shard_map/ppermute | solution.py:181
  70.2 55.3 %all-to-all-start.2 = ((bf16[16,256,128]{2,1,0:T(8,128)(2,1)}), bf16[16,256,128]{2,1,0:T(8,128)(2,1)S(1)}, u32[]{:S(2)}, u32[]{:S(2)}) async-start(bf16[16,256,128]{2,1,0:T(8,128)(2,1)} %broadcast_in_dim.7), calls=%async_computation.2 | async-start | bytes 2097152 | tf_op jit(solution)/shard_map/all_to_all | solution.py:173
  94.4 3.2 %copy-start = (bf16[480,8192]{1,0:T(8,128)(2,1)S(1)}, bf16[480,8192]{1,0:T(8,128)(2,1)}, u32[]{:S(2)}) copy-start(bf16[480,8192]{1,0:T(8,128)(2,1)} %wp.1) | copy-start | bytes 23592964
  100.4 10.8 %collective-permute-start.8 = (bf16[480,128]{1,0:T(8,128)(2,1)S(1)}, bf16[480,128]{1,0:T(8,128)(2,1)S(1)}, u32[]{:S(2)}, u32[]{:S(2)}) collective-permute-start(bf16[480,128]{1,0:T(8,128)(2,1)S(1)} %weight_product.1), channel_id=1, source_target_pairs={{0,128},{128,0},{1,129},{129,1},{2,130},{130,2},{3,131},{131,3},{4... | collective-permute-start | bytes 368648 | tf_op jit(solution)/shard_map/ppermute | solution.py:177
  111.2 9.7 %collective-permute-start.9 = (bf16[2,480,128]{2,1,0:T(8,128)(2,1)S(1)}, bf16[2,480,128]{2,1,0:T(8,128)(2,1)S(1)}, u32[]{:S(2)}, u32[]{:S(2)}) collective-permute-start(bf16[2,480,128]{2,1,0:T(8,128)(2,1)S(1)} %pad_maximum_fusion.1.refs_0_), channel_id=1, source_target_pairs={{0,32},{32,64},{64,96},{96,0},{1,33},{33,65},{65,97},{97,1},{2,34}... | collective-permute-start | bytes 737288 | tf_op jit(solution)/shard_map/ppermute | solution.py:181
  112.6 11.0 %collective-permute-start.10 = (bf16[2,480,128]{2,1,0:T(8,128)(2,1)S(1)}, bf16[2,480,128]{2,1,0:T(8,128)(2,1)S(1)}, u32[]{:S(2)}, u32[]{:S(2)}) collective-permute-start(bf16[2,480,128]{2,1,0:T(8,128)(2,1)S(1)} %pad_maximum_fusion.1.refs_0_), channel_id=1, source_target_pairs={{0,64},{32,96},{64,0},{96,32},{1,65},{33,97},{65,1},{97,33},{2,66}... | collective-permute-start | bytes 737288 | tf_op jit(solution)/shard_map/ppermute | solution.py:181
  115.5 8.1 %collective-permute-start.11 = (bf16[2,480,128]{2,1,0:T(8,128)(2,1)S(1)}, bf16[2,480,128]{2,1,0:T(8,128)(2,1)S(1)}, u32[]{:S(2)}, u32[]{:S(2)}) collective-permute-start(bf16[2,480,128]{2,1,0:T(8,128)(2,1)S(1)} %pad_maximum_fusion.1.refs_0_), channel_id=1, source_target_pairs={{0,96},{32,0},{64,32},{96,64},{1,97},{33,1},{65,33},{97,65},{2,98}... | collective-permute-start | bytes 737288 | tf_op jit(solution)/shard_map/ppermute | solution.py:181
  117.2 7.0 %collective-permute-start.12 = (bf16[2,480,128]{2,1,0:T(8,128)(2,1)S(1)}, bf16[2,480,128]{2,1,0:T(8,128)(2,1)S(1)}, u32[]{:S(2)}, u32[]{:S(2)}) collective-permute-start(bf16[2,480,128]{2,1,0:T(8,128)(2,1)S(1)} %pad_maximum_fusion.1.refs_0_), channel_id=1, source_target_pairs={{0,16},{16,0},{1,17},{17,1},{2,18},{18,2},{3,19},{19,3},{4,20},{20... | collective-permute-start | bytes 737288 | tf_op jit(solution)/shard_map/ppermute | solution.py:177
  121.0 3.2 %collective-permute-start.13 = (bf16[2,480,128]{2,1,0:T(8,128)(2,1)S(1)}, bf16[2,480,128]{2,1,0:T(8,128)(2,1)S(1)}, u32[]{:S(2)}, u32[]{:S(2)}) collective-permute-start(bf16[2,480,128]{2,1,0:T(8,128)(2,1)S(1)} %collective-permute-done.9.refs_1_), channel_id=1, source_target_pairs={{0,16},{16,0},{1,17},{17,1},{2,18},{18,2},{3,19},{19,3},{4,20},{20... | collective-permute-start | bytes 737288 | tf_op jit(solution)/shard_map/ppermute | solution.py:177
  123.6 1.5 %collective-permute-start.14 = (bf16[2,480,128]{2,1,0:T(8,128)(2,1)S(1)}, bf16[2,480,128]{2,1,0:T(8,128)(2,1)S(1)}, u32[]{:S(2)}, u32[]{:S(2)}) collective-permute-start(bf16[2,480,128]{2,1,0:T(8,128)(2,1)S(1)} %collective-permute-done.10.refs_2_), channel_id=1, source_target_pairs={{0,16},{16,0},{1,17},{17,1},{2,18},{18,2},{3,19},{19,3},{4,20},{20... | collective-permute-start | bytes 737288 | tf_op jit(solution)/shard_map/ppermute | solution.py:177
  123.6 1.9 %collective-permute-start.15 = (bf16[2,480,128]{2,1,0:T(8,128)(2,1)S(1)}, bf16[2,480,128]{2,1,0:T(8,128)(2,1)S(1)}, u32[]{:S(2)}, u32[]{:S(2)}) collective-permute-start(bf16[2,480,128]{2,1,0:T(8,128)(2,1)S(1)} %collective-permute-done.11.refs_3_), channel_id=1, source_target_pairs={{0,16},{16,0},{1,17},{17,1},{2,18},{18,2},{3,19},{19,3},{4,20},{20... | collective-permute-start | bytes 737288 | tf_op jit(solution)/shard_map/ppermute | solution.py:177

commit v5 on v3

--- a/solution.py
+++ b/solution.py
@@ -17,6 +17,7 @@
 
 CHIPS = ("zl", "y")
 HEADS = ("zh", "xh", "xl")
+X = ("xh", "xl")
 CTX = ("zl", "y", "co")
 
 LAST = (((1,), (1,)), ((), ()))
@@ -46,9 +47,8 @@
                 out[chip, 1, to, :] = (gv[rows, :] * keep).astype(jnp.bfloat16)
 
 
-def attention_kernel(order, counts, core, kv0, kv1, q_ref, do_ref, ao_ref, dq, mine, other, gk, gv, kt):
-    half = kv0.shape[0]
-    pieces = [(r, at) for r in (kv0, kv1) for at in range(0, half, CHUNK)]
+def attention_kernel(order, counts, core, kv0, kv1, kv2, q_ref, do_ref, ao_ref, dq, mine, other, gk, gv, kt):
+    pieces = [(r, at) for r in (kv0, kv1, kv2) for at in range(0, r.shape[0], CHUNK)]
     spans = [slice(i * CHUNK, (i + 1) * CHUNK) for i in range(len(pieces))]
     keys = lambda i: pieces[i][0][pieces[i][1] : pieces[i][1] + CHUNK, 0:HD]
     values = lambda i: pieces[i][0][pieces[i][1] : pieces[i][1] + CHUNK, HD : 2 * HD]
@@ -92,7 +92,7 @@
     grads = jax.ShapeDtypeStruct((8, 2, CAP * BR, HD), jnp.bfloat16)
     return pl.pallas_call(
         attention_kernel,
-        in_specs=[smem] * 3 + [vmem] * 5,
+        in_specs=[smem] * 3 + [vmem] * 6,
         out_specs=[vmem] * 3,
         out_shape=[jax.ShapeDtypeStruct(queries.shape, jnp.bfloat16), grads, grads],
         scratch_shapes=[
@@ -102,10 +102,30 @@
         ],
         compiler_params=pltpu.CompilerParams(vmem_limit_bytes=24 << 20),
         cost_estimate=pl.CostEstimate(
-            flops=10 * rows * width * image, transcendentals=rows * width // HD * image, bytes_accessed=5 << 20
+            flops=0, transcendentals=0, bytes_accessed=0
         ),
         name="attention",
-    )(order, counts, core, kv_here, kv_there, queries, out_grad, attn_out)
+    )(order, counts, core, kv_here, *kv_there, queries, out_grad, attn_out)
+
+
+def join_kernel(a, b, c, d, out):
+    part = a.shape[0]
+    for i, ref in enumerate((a, b, c, d)):
+        out[i * part : (i + 1) * part, :] = ref[...]
+
+
+def join(arrays, flops):
+    rows, cols = arrays[0].shape
+    vmem = pl.BlockSpec(memory_space=pltpu.VMEM)
+    return pl.pallas_call(
+        join_kernel,
+        in_specs=[vmem] * 4,
+        out_specs=vmem,
+        out_shape=jax.ShapeDtypeStruct((4 * rows, cols), jnp.bfloat16),
+        compiler_params=pltpu.CompilerParams(vmem_limit_bytes=4 << 20),
+        cost_estimate=pl.CostEstimate(flops=flops, transcendentals=0, bytes_accessed=1 << 20),
+        name="join",
+    )(*arrays)
 
 
 def product_kernel(at, w0, w1, w2, w3, wp, out):
@@ -136,36 +156,44 @@
     )(at, *pieces, proj_weight)
 
 
-def final_kernel(at, grads, *refs):
-    here, there, out = refs[:4], refs[4:8], refs[8]
+def final_kernel(at, heads_at, *refs):
+    grads, here, there, out, held = refs[:4], refs[4:8], refs[8:12], refs[12], refs[13]
+    rows = out.shape[1]
+    for kx in range(4):
+        for kz in range(4):
+            heads = lax.rem(heads_at[0] + 4 - kz, 4) * 4 + lax.rem(heads_at[1] + 4 - kx, 4)
+            held[heads] = grads[kx][kz * rows : (kz + 1) * rows, :]
     total = None
     for back in range(4):
         for lane in range(2):
             chip = (at[0] ^ lane) * 4 + lax.rem(at[1] + 4 - back, 4)
-            for product, c in ((here[back], at[2]), (there[back], 1 - at[2])):
-                term = lax.dot_general(
-                    product[lane], grads[2 * chip + c], LAST, preferred_element_type=jnp.float32
-                )
-                total = term if total is None else total + term
+            term = lax.dot_general(
+                jnp.concatenate([here[back][lane], there[back][lane]], axis=1),
+                jnp.concatenate([held[2 * chip + at[2]], held[2 * chip + 1 - at[2]]], axis=1),
+                LAST,
+                preferred_element_type=jnp.float32,
+            )
+            total = term if total is None else total + term
     out[...] = total.astype(jnp.bfloat16)
 
 
-def final_product(at, grads, here, there):
-    rows = grads.shape[1]
+def final_product(at, heads_at, grads, here, there):
+    rows = grads[0].shape[0] // 4
     width = here[0].shape[1]
     smem = pl.BlockSpec(memory_space=pltpu.SMEM)
     vmem = pl.BlockSpec(memory_space=pltpu.VMEM)
     return pl.pallas_call(
         final_kernel,
         out_shape=jax.ShapeDtypeStruct((width, rows), jnp.bfloat16),
-        in_specs=[smem] + [vmem] * 9,
+        in_specs=[smem] * 2 + [vmem] * 12,
         out_specs=vmem,
+        scratch_shapes=[pltpu.VMEM((16, rows, HD), jnp.bfloat16)],
         compiler_params=pltpu.CompilerParams(vmem_limit_bytes=16 << 20),
         cost_estimate=pl.CostEstimate(
             flops=2 * rows * width * 2048, transcendentals=0, bytes_accessed=4 << 20
         ),
         name="final_product",
-    )(at, grads, *here, *there)
+    )(at, heads_at, *grads, *here, *there)
 
 
 def everywhere(array, axes, count):
@@ -202,7 +230,7 @@
         lax.dynamic_slice_in_dim(key_weight, chip * HD, HD, 1),
         lax.dynamic_slice_in_dim(value_weight, chip * HD, HD, 1),
     )
-    w = jnp.concatenate(ring(w, "zh"), axis=0)
+    w = join(ring(w, "zh"), 100 << 30)
 
     own = jnp.concatenate(
         [
@@ -212,10 +240,9 @@
         axis=1,
     )
     kv = everywhere(own, CHIPS, 8).reshape(1024, 2 * HD)
-    kv, w = lax.optimization_barrier((kv, w))
     w = ring(w, ("xh", "xl"))
     d_query, mine, other = attention(
-        block_order, owner_counts, core.reshape(1), kv, swap("co", kv), queries, out_grad, attn_out
+        block_order, owner_counts, core.reshape(1), kv, [swap("co", kv[:512]), swap("co", kv[512:])], queries, out_grad, attn_out
     )
     other, *w = lax.optimization_barrier((other, *w))
     pair = mine.astype(jnp.float32) + swap("co", other).astype(jnp.float32)
@@ -234,9 +261,9 @@
     product = weight_product(heads_at, w, proj_weight)
     product = jnp.stack([product, swap("zl", product)])
     summed, product = lax.optimization_barrier((summed, product))
-    grads = everywhere(summed, HEADS, 16)
+    grads = ring(join(ring(summed, "zh"), 0), X)
     product = ring(product, "y")
-    d_vision = final_product(at, grads, product, [swap("co", p) for p in product])
+    d_vision = final_product(at, heads_at, grads, product, [swap("co", p) for p in product])
     return (d_query, d_vision.T)
 
 

time: 124 us -> 110 us (0.89)
  waiting for transfers between devices: 58.3 us -> 37.8 us
  starting transfers between devices: 39 us -> 47.3 us
  local copies, waits for them, and re-layouts: 6.16 us -> 4.9 us
    ppermute x9 -> x15, starting transfers between devices: 18.1 us -> 33.9 us  [ring(): lax.ppermute(array, axes, [(i, (i + k) % 4) for i in range(4)])]
    all_to_all x2 -> x1, waiting for transfers between devices: 11.4 us -> 0.52 us  [everywhere(): return lax.all_to_all(copies, axes, split_axis=0, concat_axis=0, tiled=True)]
    ppermute x9 -> x15, waiting for transfers between devices: 33.8 us -> 24.1 us  [ring(): lax.ppermute(array, axes, [(i, (i + k) % 4) for i in range(4)])]
    all_to_all x2 -> x1, starting transfers between devices: 12.9 us -> 4.92 us  [everywhere(): return lax.all_to_all(copies, axes, split_axis=0, concat_axis=0, tiled=True)]
    ppermute x7 -> x8, starting transfers between devices: 2.62 us -> 3.11 us  [swap(): return lax.ppermute(array, axis, [(0, 1), (1, 0)])]
    ppermute x7 -> x8, waiting for transfers between devices: 12.6 us -> 12.7 us  [swap(): return lax.ppermute(array, axis, [(0, 1), (1, 0)])]
    pallas_call x1 -> x3, Pallas kernels: 10 us -> 10.1 us  [the longest x1 10 us: attention(): pl.pallas_call(attention_kernel, in_specs=[smem] * 3 + [vmem] * 6, out_sp...]
  transfers between devices with their start and end apart: 19 -> 25, of which waited for: 11 -> 15; matrix products, arithmetic and copies ran while one was open for 1% -> 2% of each run, Pallas kernels for 10% -> 12%
where the time goes in v5:
time: 110 us; the launch traced here: 108 us
  starting transfers between devices  47.3 us (43%)
  waiting for transfers between devices  37.8 us (34%)
  Pallas kernels  14.9 us (14%)
  local copies, waits for them, and re-layouts  4.9 us (4%)
  other arithmetic  2.59 us (2%)
    ppermute x15, starting transfers between devices, ring(): lax.ppermute(array, axes, [(i, (i + k) % 4) for i in range(4)])  33.9 us
    ppermute x15, waiting for transfers between devices, ring(): lax.ppermute(array, axes, [(i, (i + k) % 4) for i in range(4)])  24.1 us
    ppermute x8, waiting for transfers between devices, swap(): return lax.ppermute(array, axis, [(0, 1), (1, 0)])  12.7 us
    pallas_call x1, Pallas kernels, attention(): pl.pallas_call(attention_kernel, in_specs=[smem] * 3 + [vmem] * 6, out_sp...  10 us
    all_to_all x1, starting transfers between devices, shards(): lax.all_to_all(pair, ('zl', 'y', 'xl'), split_axis=0, concat_axis=0, tile...  5.35 us
    all_to_all x1, starting transfers between devices, everywhere(): return lax.all_to_all(copies, axes, split_axis=0, concat_axis=0, tiled=True)  4.92 us
    unnamed x12, local copies, waits for them, and re-layouts  3.26 us
    ppermute x8, starting transfers between devices, swap(): return lax.ppermute(array, axis, [(0, 1), (1, 0)])  3.11 us
  transfers between devices with their start and end apart: 25, of which 15 were waited for; matrix products, arithmetic and copies ran while one was open for 2% of the time, Pallas kernels for 12%

profile of v5, /device:TPU:64, one launch (start us, length us, event | category | flops | bytes accessed | tf_op | source)
XLA Modules:
  0.0 108.3 jit_solution(5878259210766640199)
XLA Ops:
  0.6 1.0 dynamic-slice_select_fusion.a
  1.7 4.6 %collective-permute-start.2 = (bf16[512,128]{1,0:T(8,128)(2,1)S(1)}, bf16[512,128]{1,0:T(8,128)(2,1)S(1)}, u32[]{:S(2)}, u32[]{:S(2)}) collective-permute-start(bf16[512,128]{1,0:T(8,128)(2,1)S(1)} %dynamic-slice_select_fusion.a), channel_id=1, source_target_pairs={{0,4},{4,8},{8,12},{12,0},{1,5},{5,9},{9,13},{13,1},{2,6},{6,10},{... | collective-permute-start | bytes 393224 | tf_op jit(solution)/shard_map/ppermute | solution.py:209
  6.2 1.0 collective-permute-start.3
  7.2 2.8 %collective-permute-start.4 = (bf16[512,128]{1,0:T(8,128)(2,1)S(1)}, bf16[512,128]{1,0:T(8,128)(2,1)S(1)}, u32[]{:S(2)}, u32[]{:S(2)}) collective-permute-start(bf16[512,128]{1,0:T(8,128)(2,1)S(1)} %dynamic-slice_select_fusion.a), channel_id=1, source_target_pairs={{0,12},{4,0},{8,4},{12,8},{1,13},{5,1},{9,5},{13,9},{2,14},{6,2},{... | collective-permute-start | bytes 393224 | tf_op jit(solution)/shard_map/ppermute | solution.py:209
  10.1 0.8 constant_dynamic-slice_fusion
  10.8 0.8 broadcast_in_dim.3
  11.7 4.9 %all-to-all-start = ((bf16[8,128,256]{2,1,0:T(8,128)(2,1)}), bf16[8,128,256]{2,1,0:T(8,128)(2,1)S(1)}, u32[]{:S(2)}, u32[]{:S(2)}) async-start(bf16[8,128,256]{2,1,0:T(8,128)(2,1)} %broadcast_in_dim.3), calls=%async_computation | async-start | bytes 1048576 | tf_op jit(solution)/shard_map/all_to_all | solution.py:201
  16.6 0.0 copy-start.3
  16.7 3.3 %collective-permute-done.3.c = bf16[512,128]{1,0:T(8,128)(2,1)S(1)} collective-permute-done((bf16[512,128]{1,0:T(8,128)(2,1)S(1)}, bf16[512,128]{1,0:T(8,128)(2,1)S(1)}, u32[]{:S(2)}, u32[]{:S(2)}) %collective-permute-start.3) | collective-permute-done | bytes 131104 | tf_op jit(solution)/shard_map/ppermute | solution.py:209
  19.9 1.0 collective-permute-done.4.d
  21.0 1.6 %collective-permute-start.5 = (bf16[2048,128]{1,0:T(8,128)(2,1)S(1)}, bf16[2048,128]{1,0:T(8,128)(2,1)S(1)}, u32[]{:S(2)}, u32[]{:S(2)}) collective-permute-start(bf16[2048,128]{1,0:T(8,128)(2,1)S(1)} %join.2.w0), channel_id=1, source_target_pairs={{0,1},{1,2},{2,3},{3,0},{4,5},{5,6},{6,7},{7,4},{8,9},{9,10},{10,1... | collective-permute-start | bytes 1572872 | tf_op jit(solution)/shard_map/ppermute | solution.py:209
  22.6 2.7 %collective-permute-start.6 = (bf16[2048,128]{1,0:T(8,128)(2,1)S(1)}, bf16[2048,128]{1,0:T(8,128)(2,1)S(1)}, u32[]{:S(2)}, u32[]{:S(2)}) collective-permute-start(bf16[2048,128]{1,0:T(8,128)(2,1)S(1)} %join.2.w0), channel_id=1, source_target_pairs={{0,2},{1,3},{2,0},{3,1},{4,6},{5,7},{6,4},{7,5},{8,10},{9,11},{10,... | collective-permute-start | bytes 1572872 | tf_op jit(solution)/shard_map/ppermute | solution.py:209
  25.3 1.4 %collective-permute-start.7 = (bf16[2048,128]{1,0:T(8,128)(2,1)S(1)}, bf16[2048,128]{1,0:T(8,128)(2,1)S(1)}, u32[]{:S(2)}, u32[]{:S(2)}) collective-permute-start(bf16[2048,128]{1,0:T(8,128)(2,1)S(1)} %join.2.w0), channel_id=1, source_target_pairs={{0,3},{1,0},{2,1},{3,2},{4,7},{5,4},{6,5},{7,6},{8,11},{9,8},{10,9... | collective-permute-start | bytes 1572872 | tf_op jit(solution)/shard_map/ppermute | solution.py:209
  26.7 0.5 all-to-all-done
  27.3 0.1 collective-permute-start
  27.4 0.5 collective-permute-start.1
  27.9 1.0 collective-permute-done.kv1
  28.9 0.4 collective-permute-done.1.kv2
  29.3 10.0 %attention.1 = (bf16[256,512]{1,0:T(8,128)(2,1)}, bf16[8,2,256,128]{3,2,1,0:T(8,128)(2,1)S(1)}, bf16[8,2,256,128]{3,2,1,0:T(8,128)(2,1)S(1)}) custom-call(s32[32]{0:T(128)S(1)} %copy-done.4, s32[16]{0:T(128)S(1)} %copy-done.5, s32[1]{0:T(128)} %bitcast.core, bf16[1024,256]{1,0:T(8,128)(2,1)S(1)} %bitcast.12, bf16[512,256]{1,0:T(8,128)(2,1)S(1)} %collective-permute-done.kv1, ...), custom_call_target="tpu_custom_call" | custom-call | tf_op jit(solution)/shard_map/attention/pallas_call | solution.py:93
  39.3 8.5 %collective-permute-done.6.w2 = bf16[2048,128]{1,0:T(8,128)(2,1)S(1)} collective-permute-done((bf16[2048,128]{1,0:T(8,128)(2,1)S(1)}, bf16[2048,128]{1,0:T(8,128)(2,1)S(1)}, u32[]{:S(2)}, u32[]{:S(2)}) %collective-permute-start.6) | collective-permute-done | bytes 524320 | tf_op jit(solution)/shard_map/ppermute | solution.py:209
  47.9 2.7 %collective-permute-done.8 = bf16[8,2,256,128]{3,2,1,0:T(8,128)(2,1)S(1)} collective-permute-done((bf16[8,2,256,128]{3,2,1,0:T(8,128)(2,1)S(1)}, bf16[8,2,256,128]{3,2,1,0:T(8,128)(2,1)S(1)}, u32[]{:S(2)}, u32[]{:S(2)}) %collective-permute-start.8) | collective-permute-done | bytes 1048608 | tf_op jit(solution)/shard_map/ppermute | solution.py:205
  50.5 1.2 %add_convert_fusion = bf16[8,2,256,128]{3,2,1,0:T(8,128)(2,1)} fusion(bf16[8,2,256,128]{3,2,1,0:T(8,128)(2,1)S(1)} %collective-permute-done.8, bf16[8,2,256,128]{3,2,1,0:T(8,128)(2,1)S(1)} %get-tuple-element.13), kind=kLoop, calls=%fused_computation | loop fusion | flops 2097152 | bytes 3145728 | tf_op jit(solution)/shard_map/convert_element_type | solution.py:249
  51.8 5.3 %all-to-all-start.1 = ((bf16[16,256,128]{2,1,0:T(8,128)(2,1)}), bf16[16,256,128]{2,1,0:T(8,128)(2,1)S(1)}, u32[]{:S(2)}, u32[]{:S(2)}) async-start(bf16[16,256,128]{2,1,0:T(8,128)(2,1)} %bitcast.8), calls=%async_computation.1 | async-start | bytes 2097152 | tf_op jit(solution)/shard_map/all_to_all | solution.py:250
  57.2 0.1 pad_add_fusion.1.at.heads_at
  57.2 3.2 %copy-done = bf16[480,8192]{1,0:T(8,128)(2,1)S(1)} copy-done((bf16[480,8192]{1,0:T(8,128)(2,1)S(1)}, bf16[480,8192]{1,0:T(8,128)(2,1)}, u32[]{:S(2)}) %copy-start) | copy-done | bytes 7864344
  60.5 2.7 %weight_product.1 = bf16[480,128]{1,0:T(8,128)(2,1)S(1)} custom-call(s32[2]{0:T(128)S(1)} %pad_add_fusion.1.at.heads_at, bf16[2048,128]{1,0:T(8,128)(2,1)S(1)} %join.2.w0, bf16[2048,128]{1,0:T(8,128)(2,1)S(1)} %collective-permute-done.5.w1, bf16[2048,128]{1,0:T(8,128)(2,1)S(1)} %collective-permute-done.6.w2, ...), custom_call_target="tpu_custom_call" | custom-call | flops 1006632960 | bytes 10485760 | tf_op jit(solution)/shard_map/weight_product/pallas_call | solution.py:146
  63.2 2.0 %collective-permute-start.9 = (bf16[480,128]{1,0:T(8,128)(2,1)S(1)}, bf16[480,128]{1,0:T(8,128)(2,1)S(1)}, u32[]{:S(2)}, u32[]{:S(2)}) collective-permute-start(bf16[480,128]{1,0:T(8,128)(2,1)S(1)} %weight_product.1), channel_id=1, source_target_pairs={{0,128},{128,0},{1,129},{129,1},{2,130},{130,2},{3,131},{131,3},{4... | collective-permute-start | bytes 368648 | tf_op jit(solution)/shard_map/ppermute | solution.py:205
  65.2 8.7 %collective-permute-done.9 = bf16[480,128]{1,0:T(8,128)(2,1)S(1)} collective-permute-done((bf16[480,128]{1,0:T(8,128)(2,1)S(1)}, bf16[480,128]{1,0:T(8,128)(2,1)S(1)}, u32[]{:S(2)}, u32[]{:S(2)}) %collective-permute-start.9) | collective-permute-done | bytes 122912 | tf_op jit(solution)/shard_map/ppermute | solution.py:205
  73.9 0.5 all-to-all-done.1
  74.4 0.1 reduce_sum.12.a
  74.5 3.0 %collective-permute-start.10 = (bf16[256,128]{1,0:T(8,128)(2,1)S(1)}, bf16[256,128]{1,0:T(8,128)(2,1)S(1)}, u32[]{:S(2)}, u32[]{:S(2)}) collective-permute-start(bf16[256,128]{1,0:T(8,128)(2,1)S(1)} %reduce_sum.12.a), channel_id=1, source_target_pairs={{0,4},{4,8},{8,12},{12,0},{1,5},{5,9},{9,13},{13,1},{2,6},{6,10},{... | collective-permute-start | bytes 196616 | tf_op jit(solution)/shard_map/ppermute | solution.py:209
  77.5 2.6 %collective-permute-start.11 = (bf16[256,128]{1,0:T(8,128)(2,1)S(1)}, bf16[256,128]{1,0:T(8,128)(2,1)S(1)}, u32[]{:S(2)}, u32[]{:S(2)}) collective-permute-start(bf16[256,128]{1,0:T(8,128)(2,1)S(1)} %reduce_sum.12.a), channel_id=1, source_target_pairs={{0,8},{4,12},{8,0},{12,4},{1,9},{5,13},{9,1},{13,5},{2,10},{6,14},... | collective-permute-start | bytes 196616 | tf_op jit(solution)/shard_map/ppermute | solution.py:209
  80.1 2.4 %collective-permute-start.12 = (bf16[256,128]{1,0:T(8,128)(2,1)S(1)}, bf16[256,128]{1,0:T(8,128)(2,1)S(1)}, u32[]{:S(2)}, u32[]{:S(2)}) collective-permute-start(bf16[256,128]{1,0:T(8,128)(2,1)S(1)} %reduce_sum.12.a), channel_id=1, source_target_pairs={{0,12},{4,0},{8,4},{12,8},{1,13},{5,1},{9,5},{13,9},{2,14},{6,2},{... | collective-permute-start | bytes 196616 | tf_op jit(solution)/shard_map/ppermute | solution.py:209
  82.5 0.7 collective-permute-start.16
  83.2 2.9 %collective-permute-start.17 = (bf16[2,480,128]{2,1,0:T(8,128)(2,1)S(1)}, bf16[2,480,128]{2,1,0:T(8,128)(2,1)S(1)}, u32[]{:S(2)}, u32[]{:S(2)}) collective-permute-start(bf16[2,480,128]{2,1,0:T(8,128)(2,1)S(1)} %pad_maximum_fusion.refs_4_), channel_id=1, source_target_pairs={{0,64},{32,96},{64,0},{96,32},{1,65},{33,97},{65,1},{97,33},{2,66}... | collective-permute-start | bytes 737288 | tf_op jit(solution)/shard_map/ppermute | solution.py:209
  86.2 0.2 collective-permute-done.11.c
  86.4 1.3 %collective-permute-done.12.d = bf16[256,128]{1,0:T(8,128)(2,1)S(1)} collective-permute-done((bf16[256,128]{1,0:T(8,128)(2,1)S(1)}, bf16[256,128]{1,0:T(8,128)(2,1)S(1)}, u32[]{:S(2)}, u32[]{:S(2)}) %collective-permute-start.12) | collective-permute-done | bytes 65568 | tf_op jit(solution)/shard_map/ppermute | solution.py:209
  87.7 1.5 %collective-permute-start.13 = (bf16[1024,128]{1,0:T(8,128)(2,1)S(1)}, bf16[1024,128]{1,0:T(8,128)(2,1)S(1)}, u32[]{:S(2)}, u32[]{:S(2)}) collective-permute-start(bf16[1024,128]{1,0:T(8,128)(2,1)S(1)} %join.3.refs_0_), channel_id=1, source_target_pairs={{0,1},{1,2},{2,3},{3,0},{4,5},{5,6},{6,7},{7,4},{8,9},{9,10},{10,1... | collective-permute-start | bytes 786440 | tf_op jit(solution)/shard_map/ppermute | solution.py:209
  89.2 2.1 %collective-permute-start.18 = (bf16[2,480,128]{2,1,0:T(8,128)(2,1)S(1)}, bf16[2,480,128]{2,1,0:T(8,128)(2,1)S(1)}, u32[]{:S(2)}, u32[]{:S(2)}) collective-permute-start(bf16[2,480,128]{2,1,0:T(8,128)(2,1)S(1)} %pad_maximum_fusion.refs_4_), channel_id=1, source_target_pairs={{0,96},{32,0},{64,32},{96,64},{1,97},{33,1},{65,33},{97,65},{2,98}... | collective-permute-start | bytes 737288 | tf_op jit(solution)/shard_map/ppermute | solution.py:209
  91.3 1.3 %collective-permute-done.16.refs_5_ = bf16[2,480,128]{2,1,0:T(8,128)(2,1)S(1)} collective-permute-done((bf16[2,480,128]{2,1,0:T(8,128)(2,1)S(1)}, bf16[2,480,128]{2,1,0:T(8,128)(2,1)S(1)}, u32[]{:S(2)}, u32[]{:S(2)}) %collective-permute-start.16) | collective-permute-done | bytes 245792 | tf_op jit(solution)/shard_map/ppermute | solution.py:209
  92.5 2.4 %collective-permute-start.14 = (bf16[1024,128]{1,0:T(8,128)(2,1)S(1)}, bf16[1024,128]{1,0:T(8,128)(2,1)S(1)}, u32[]{:S(2)}, u32[]{:S(2)}) collective-permute-start(bf16[1024,128]{1,0:T(8,128)(2,1)S(1)} %join.3.refs_0_), channel_id=1, source_target_pairs={{0,2},{1,3},{2,0},{3,1},{4,6},{5,7},{6,4},{7,5},{8,10},{9,11},{10,... | collective-permute-start | bytes 786440 | tf_op jit(solution)/shard_map/ppermute | solution.py:209
  94.9 0.5 collective-permute-done.17.refs_6_
  95.5 2.2 %collective-permute-start.15 = (bf16[1024,128]{1,0:T(8,128)(2,1)S(1)}, bf16[1024,128]{1,0:T(8,128)(2,1)S(1)}, u32[]{:S(2)}, u32[]{:S(2)}) collective-permute-start(bf16[1024,128]{1,0:T(8,128)(2,1)S(1)} %join.3.refs_0_), channel_id=1, source_target_pairs={{0,3},{1,0},{2,1},{3,2},{4,7},{5,4},{6,5},{7,6},{8,11},{9,8},{10,9... | collective-permute-start | bytes 786440 | tf_op jit(solution)/shard_map/ppermute | solution.py:209
  97.7 0.5 collective-permute-start.21
  98.2 4.4 %collective-permute-done.13.refs_1_ = bf16[1024,128]{1,0:T(8,128)(2,1)S(1)} collective-permute-done((bf16[1024,128]{1,0:T(8,128)(2,1)S(1)}, bf16[1024,128]{1,0:T(8,128)(2,1)S(1)}, u32[]{:S(2)}, u32[]{:S(2)}) %collective-permute-start.13) | collective-permute-done | bytes 262176 | tf_op jit(solution)/shard_map/ppermute | solution.py:209
  102.6 0.1 pad_add_fusion.at
  102.7 3.5 %collective-permute-done.15.refs_3_ = bf16[1024,128]{1,0:T(8,128)(2,1)S(1)} collective-permute-done((bf16[1024,128]{1,0:T(8,128)(2,1)S(1)}, bf16[1024,128]{1,0:T(8,128)(2,1)S(1)}, u32[]{:S(2)}, u32[]{:S(2)}) %collective-permute-start.15) | collective-permute-done | bytes 262176 | tf_op jit(solution)/shard_map/ppermute | solution.py:209
  106.3 2.0 %final_product.1 = bf16[480,256]{1,0:T(8,128)(2,1)} custom-call(s32[3]{0:T(128)S(1)} %pad_add_fusion.at, s32[2]{0:T(128)S(1)} %pad_add_fusion.1.at.heads_at, bf16[1024,128]{1,0:T(8,128)(2,1)S(1)} %join.3.refs_0_, bf16[1024,128]{1,0:T(8,128)(2,1)S(1)} %collective-permute-done.13.refs_1_, bf16[1024,128]{1,0:T(8,128)(2,1)S(1)} %collective-permute-done.14.refs_2_, ...), custom_call_target="tpu_custom_call" | custom-call | flops 503316480 | bytes 4194304 | tf_op jit(solution)/shard_map/final_product/pallas_call | solution.py:185
  (29 shorter events, 0.2 us)
Async XLA Ops:
  1.7 15.0 %collective-permute-start.2 = (bf16[512,128]{1,0:T(8,128)(2,1)S(1)}, bf16[512,128]{1,0:T(8,128)(2,1)S(1)}, u32[]{:S(2)}, u32[]{:S(2)}) collective-permute-start(bf16[512,128]{1,0:T(8,128)(2,1)S(1)} %dynamic-slice_select_fusion.a), channel_id=1, source_target_pairs={{0,4},{4,8},{8,12},{12,0},{1,5},{5,9},{9,13},{13,1},{2,6},{6,10},{... | collective-permute-start | bytes 393224 | tf_op jit(solution)/shard_map/ppermute | solution.py:209
  6.2 13.7 %collective-permute-start.3 = (bf16[512,128]{1,0:T(8,128)(2,1)S(1)}, bf16[512,128]{1,0:T(8,128)(2,1)S(1)}, u32[]{:S(2)}, u32[]{:S(2)}) collective-permute-start(bf16[512,128]{1,0:T(8,128)(2,1)S(1)} %dynamic-slice_select_fusion.a), channel_id=1, source_target_pairs={{0,8},{4,12},{8,0},{12,4},{1,9},{5,13},{9,1},{13,5},{2,10},{6,14},... | collective-permute-start | bytes 393224 | tf_op jit(solution)/shard_map/ppermute | solution.py:209
  7.2 13.7 %collective-permute-start.4 = (bf16[512,128]{1,0:T(8,128)(2,1)S(1)}, bf16[512,128]{1,0:T(8,128)(2,1)S(1)}, u32[]{:S(2)}, u32[]{:S(2)}) collective-permute-start(bf16[512,128]{1,0:T(8,128)(2,1)S(1)} %dynamic-slice_select_fusion.a), channel_id=1, source_target_pairs={{0,12},{4,0},{8,4},{12,8},{1,13},{5,1},{9,5},{13,9},{2,14},{6,2},{... | collective-permute-start | bytes 393224 | tf_op jit(solution)/shard_map/ppermute | solution.py:209
  11.7 15.6 %all-to-all-start = ((bf16[8,128,256]{2,1,0:T(8,128)(2,1)}), bf16[8,128,256]{2,1,0:T(8,128)(2,1)S(1)}, u32[]{:S(2)}, u32[]{:S(2)}) async-start(bf16[8,128,256]{2,1,0:T(8,128)(2,1)} %broadcast_in_dim.3), calls=%async_computation | async-start | bytes 1048576 | tf_op jit(solution)/shard_map/all_to_all | solution.py:201
  16.6 12.7 %copy-start.1 = (bf16[256,512]{1,0:T(8,128)(2,1)S(1)}, bf16[256,512]{1,0:T(8,128)(2,1)}, u32[]{:S(2)}) copy-start(bf16[256,512]{1,0:T(8,128)(2,1)} %q_ref.1) | copy-start | bytes 786436
  16.6 12.7 %copy-start.2 = (bf16[256,512]{1,0:T(8,128)(2,1)S(1)}, bf16[256,512]{1,0:T(8,128)(2,1)}, u32[]{:S(2)}) copy-start(bf16[256,512]{1,0:T(8,128)(2,1)} %do_ref.1) | copy-start | bytes 786436
  16.6 12.7 %copy-start.3 = (bf16[256,512]{1,0:T(8,128)(2,1)S(1)}, bf16[256,512]{1,0:T(8,128)(2,1)}, u32[]{:S(2)}) copy-start(bf16[256,512]{1,0:T(8,128)(2,1)} %ao_ref.1) | copy-start | bytes 786436
  16.6 12.7 %copy-start.4 = (s32[32]{0:T(128)S(1)}, s32[32]{0:T(128)}, u32[]{:S(2)}) copy-start(s32[32]{0:T(128)} %order.1) | copy-start | bytes 388
  16.6 12.7 %copy-start.5 = (s32[16]{0:T(128)S(1)}, s32[16]{0:T(128)}, u32[]{:S(2)}) copy-start(s32[16]{0:T(128)} %counts.1) | copy-start | bytes 196
  21.0 18.3 %collective-permute-start.5 = (bf16[2048,128]{1,0:T(8,128)(2,1)S(1)}, bf16[2048,128]{1,0:T(8,128)(2,1)S(1)}, u32[]{:S(2)}, u32[]{:S(2)}) collective-permute-start(bf16[2048,128]{1,0:T(8,128)(2,1)S(1)} %join.2.w0), channel_id=1, source_target_pairs={{0,1},{1,2},{2,3},{3,0},{4,5},{5,6},{6,7},{7,4},{8,9},{9,10},{10,1... | collective-permute-start | bytes 1572872 | tf_op jit(solution)/shard_map/ppermute | solution.py:209
  22.6 25.3 %collective-permute-start.6 = (bf16[2048,128]{1,0:T(8,128)(2,1)S(1)}, bf16[2048,128]{1,0:T(8,128)(2,1)S(1)}, u32[]{:S(2)}, u32[]{:S(2)}) collective-permute-start(bf16[2048,128]{1,0:T(8,128)(2,1)S(1)} %join.2.w0), channel_id=1, source_target_pairs={{0,2},{1,3},{2,0},{3,1},{4,6},{5,7},{6,4},{7,5},{8,10},{9,11},{10,... | collective-permute-start | bytes 1572872 | tf_op jit(solution)/shard_map/ppermute | solution.py:209
  25.3 22.6 %collective-permute-start.7 = (bf16[2048,128]{1,0:T(8,128)(2,1)S(1)}, bf16[2048,128]{1,0:T(8,128)(2,1)S(1)}, u32[]{:S(2)}, u32[]{:S(2)}) collective-permute-start(bf16[2048,128]{1,0:T(8,128)(2,1)S(1)} %join.2.w0), channel_id=1, source_target_pairs={{0,3},{1,0},{2,1},{3,2},{4,7},{5,4},{6,5},{7,6},{8,11},{9,8},{10,9... | collective-permute-start | bytes 1572872 | tf_op jit(solution)/shard_map/ppermute | solution.py:209
  27.3 1.6 %collective-permute-start = (bf16[512,256]{1,0:T(8,128)(2,1)S(1)}, bf16[512,256]{1,0:T(8,128)(2,1)S(1)}, u32[]{:S(2)}, u32[]{:S(2)}) collective-permute-start(bf16[512,256]{1,0:T(8,128)(2,1)S(1)} %bitcast.15), channel_id=1, source_target_pairs={{0,16},{16,0},{1,17},{17,1},{2,18},{18,2},{3,19},{19,3},{4,20},{20... | collective-permute-start | bytes 786440 | tf_op jit(solution)/shard_map/ppermute | solution.py:205
  27.4 1.9 %collective-permute-start.1 = (bf16[512,256]{1,0:T(8,128)(2,1)S(1)}, bf16[512,256]{1,0:T(8,128)(2,1)S(1)}, u32[]{:S(2)}, u32[]{:S(2)}) collective-permute-start(bf16[512,256]{1,0:T(8,128)(2,1)S(1)} %bitcast.14), channel_id=1, source_target_pairs={{0,16},{16,0},{1,17},{17,1},{2,18},{18,2},{3,19},{19,3},{4,20},{20... | collective-permute-start | bytes 786440 | tf_op jit(solution)/shard_map/ppermute | solution.py:205
  47.9 2.7 %collective-permute-start.8 = (bf16[8,2,256,128]{3,2,1,0:T(8,128)(2,1)S(1)}, bf16[8,2,256,128]{3,2,1,0:T(8,128)(2,1)S(1)}, u32[]{:S(2)}, u32[]{:S(2)}) collective-permute-start(bf16[8,2,256,128]{3,2,1,0:T(8,128)(2,1)S(1)} %get-tuple-element.15), channel_id=1, source_target_pairs={{0,16},{16,0},{1,17},{17,1},{2,18},{18,2},{3,19},{19,3},{4,20},{20... | collective-permute-start | bytes 3145736 | tf_op jit(solution)/shard_map/ppermute | solution.py:205
  51.8 22.6 %all-to-all-start.1 = ((bf16[16,256,128]{2,1,0:T(8,128)(2,1)}), bf16[16,256,128]{2,1,0:T(8,128)(2,1)S(1)}, u32[]{:S(2)}, u32[]{:S(2)}) async-start(bf16[16,256,128]{2,1,0:T(8,128)(2,1)} %bitcast.8), calls=%async_computation.1 | async-start | bytes 2097152 | tf_op jit(solution)/shard_map/all_to_all | solution.py:250
  57.2 3.2 %copy-start = (bf16[480,8192]{1,0:T(8,128)(2,1)S(1)}, bf16[480,8192]{1,0:T(8,128)(2,1)}, u32[]{:S(2)}) copy-start(bf16[480,8192]{1,0:T(8,128)(2,1)} %wp.1) | copy-start | bytes 23592964
  63.2 10.7 %collective-permute-start.9 = (bf16[480,128]{1,0:T(8,128)(2,1)S(1)}, bf16[480,128]{1,0:T(8,128)(2,1)S(1)}, u32[]{:S(2)}, u32[]{:S(2)}) collective-permute-start(bf16[480,128]{1,0:T(8,128)(2,1)S(1)} %weight_product.1), channel_id=1, source_target_pairs={{0,128},{128,0},{1,129},{129,1},{2,130},{130,2},{3,131},{131,3},{4... | collective-permute-start | bytes 368648 | tf_op jit(solution)/shard_map/ppermute | solution.py:205
  74.5 11.6 %collective-permute-start.10 = (bf16[256,128]{1,0:T(8,128)(2,1)S(1)}, bf16[256,128]{1,0:T(8,128)(2,1)S(1)}, u32[]{:S(2)}, u32[]{:S(2)}) collective-permute-start(bf16[256,128]{1,0:T(8,128)(2,1)S(1)} %reduce_sum.12.a), channel_id=1, source_target_pairs={{0,4},{4,8},{8,12},{12,0},{1,5},{5,9},{9,13},{13,1},{2,6},{6,10},{... | collective-permute-start | bytes 196616 | tf_op jit(solution)/shard_map/ppermute | solution.py:209
  77.5 8.9 %collective-permute-start.11 = (bf16[256,128]{1,0:T(8,128)(2,1)S(1)}, bf16[256,128]{1,0:T(8,128)(2,1)S(1)}, u32[]{:S(2)}, u32[]{:S(2)}) collective-permute-start(bf16[256,128]{1,0:T(8,128)(2,1)S(1)} %reduce_sum.12.a), channel_id=1, source_target_pairs={{0,8},{4,12},{8,0},{12,4},{1,9},{5,13},{9,1},{13,5},{2,10},{6,14},... | collective-permute-start | bytes 196616 | tf_op jit(solution)/shard_map/ppermute | solution.py:209
  80.1 7.5 %collective-permute-start.12 = (bf16[256,128]{1,0:T(8,128)(2,1)S(1)}, bf16[256,128]{1,0:T(8,128)(2,1)S(1)}, u32[]{:S(2)}, u32[]{:S(2)}) collective-permute-start(bf16[256,128]{1,0:T(8,128)(2,1)S(1)} %reduce_sum.12.a), channel_id=1, source_target_pairs={{0,12},{4,0},{8,4},{12,8},{1,13},{5,1},{9,5},{13,9},{2,14},{6,2},{... | collective-permute-start | bytes 196616 | tf_op jit(solution)/shard_map/ppermute | solution.py:209
  82.5 10.0 %collective-permute-start.16 = (bf16[2,480,128]{2,1,0:T(8,128)(2,1)S(1)}, bf16[2,480,128]{2,1,0:T(8,128)(2,1)S(1)}, u32[]{:S(2)}, u32[]{:S(2)}) collective-permute-start(bf16[2,480,128]{2,1,0:T(8,128)(2,1)S(1)} %pad_maximum_fusion.refs_4_), channel_id=1, source_target_pairs={{0,32},{32,64},{64,96},{96,0},{1,33},{33,65},{65,97},{97,1},{2,34}... | collective-permute-start | bytes 737288 | tf_op jit(solution)/shard_map/ppermute | solution.py:209
  83.2 12.2 %collective-permute-start.17 = (bf16[2,480,128]{2,1,0:T(8,128)(2,1)S(1)}, bf16[2,480,128]{2,1,0:T(8,128)(2,1)S(1)}, u32[]{:S(2)}, u32[]{:S(2)}) collective-permute-start(bf16[2,480,128]{2,1,0:T(8,128)(2,1)S(1)} %pad_maximum_fusion.refs_4_), channel_id=1, source_target_pairs={{0,64},{32,96},{64,0},{96,32},{1,65},{33,97},{65,1},{97,33},{2,66}... | collective-permute-start | bytes 737288 | tf_op jit(solution)/shard_map/ppermute | solution.py:209
  87.7 14.9 %collective-permute-start.13 = (bf16[1024,128]{1,0:T(8,128)(2,1)S(1)}, bf16[1024,128]{1,0:T(8,128)(2,1)S(1)}, u32[]{:S(2)}, u32[]{:S(2)}) collective-permute-start(bf16[1024,128]{1,0:T(8,128)(2,1)S(1)} %join.3.refs_0_), channel_id=1, source_target_pairs={{0,1},{1,2},{2,3},{3,0},{4,5},{5,6},{6,7},{7,4},{8,9},{9,10},{10,1... | collective-permute-start | bytes 786440 | tf_op jit(solution)/shard_map/ppermute | solution.py:209
  89.2 8.5 %collective-permute-start.18 = (bf16[2,480,128]{2,1,0:T(8,128)(2,1)S(1)}, bf16[2,480,128]{2,1,0:T(8,128)(2,1)S(1)}, u32[]{:S(2)}, u32[]{:S(2)}) collective-permute-start(bf16[2,480,128]{2,1,0:T(8,128)(2,1)S(1)} %pad_maximum_fusion.refs_4_), channel_id=1, source_target_pairs={{0,96},{32,0},{64,32},{96,64},{1,97},{33,1},{65,33},{97,65},{2,98}... | collective-permute-start | bytes 737288 | tf_op jit(solution)/shard_map/ppermute | solution.py:209
  91.3 6.5 %collective-permute-start.19 = (bf16[2,480,128]{2,1,0:T(8,128)(2,1)S(1)}, bf16[2,480,128]{2,1,0:T(8,128)(2,1)S(1)}, u32[]{:S(2)}, u32[]{:S(2)}) collective-permute-start(bf16[2,480,128]{2,1,0:T(8,128)(2,1)S(1)} %pad_maximum_fusion.refs_4_), channel_id=1, source_target_pairs={{0,16},{16,0},{1,17},{17,1},{2,18},{18,2},{3,19},{19,3},{4,20},{20... | collective-permute-start | bytes 737288 | tf_op jit(solution)/shard_map/ppermute | solution.py:205
  92.5 10.2 %collective-permute-start.14 = (bf16[1024,128]{1,0:T(8,128)(2,1)S(1)}, bf16[1024,128]{1,0:T(8,128)(2,1)S(1)}, u32[]{:S(2)}, u32[]{:S(2)}) collective-permute-start(bf16[1024,128]{1,0:T(8,128)(2,1)S(1)} %join.3.refs_0_), channel_id=1, source_target_pairs={{0,2},{1,3},{2,0},{3,1},{4,6},{5,7},{6,4},{7,5},{8,10},{9,11},{10,... | collective-permute-start | bytes 786440 | tf_op jit(solution)/shard_map/ppermute | solution.py:209
  95.5 10.8 %collective-permute-start.15 = (bf16[1024,128]{1,0:T(8,128)(2,1)S(1)}, bf16[1024,128]{1,0:T(8,128)(2,1)S(1)}, u32[]{:S(2)}, u32[]{:S(2)}) collective-permute-start(bf16[1024,128]{1,0:T(8,128)(2,1)S(1)} %join.3.refs_0_), channel_id=1, source_target_pairs={{0,3},{1,0},{2,1},{3,2},{4,7},{5,4},{6,5},{7,6},{8,11},{9,8},{10,9... | collective-permute-start | bytes 786440 | tf_op jit(solution)/shard_map/ppermute | solution.py:209
  97.7 8.5 %collective-permute-start.20 = (bf16[2,480,128]{2,1,0:T(8,128)(2,1)S(1)}, bf16[2,480,128]{2,1,0:T(8,128)(2,1)S(1)}, u32[]{:S(2)}, u32[]{:S(2)}) collective-permute-start(bf16[2,480,128]{2,1,0:T(8,128)(2,1)S(1)} %collective-permute-done.16.refs_5_), channel_id=1, source_target_pairs={{0,16},{16,0},{1,17},{17,1},{2,18},{18,2},{3,19},{19,3},{4,20},{20... | collective-permute-start | bytes 737288 | tf_op jit(solution)/shard_map/ppermute | solution.py:205
  97.7 8.5 %collective-permute-start.21 = (bf16[2,480,128]{2,1,0:T(8,128)(2,1)S(1)}, bf16[2,480,128]{2,1,0:T(8,128)(2,1)S(1)}, u32[]{:S(2)}, u32[]{:S(2)}) collective-permute-start(bf16[2,480,128]{2,1,0:T(8,128)(2,1)S(1)} %collective-permute-done.17.refs_6_), channel_id=1, source_target_pairs={{0,16},{16,0},{1,17},{17,1},{2,18},{18,2},{3,19},{19,3},{4,20},{20... | collective-permute-start | bytes 737288 | tf_op jit(solution)/shard_map/ppermute | solution.py:205
  102.6 3.6 %collective-permute-start.22 = (bf16[2,480,128]{2,1,0:T(8,128)(2,1)S(1)}, bf16[2,480,128]{2,1,0:T(8,128)(2,1)S(1)}, u32[]{:S(2)}, u32[]{:S(2)}) collective-permute-start(bf16[2,480,128]{2,1,0:T(8,128)(2,1)S(1)} %collective-permute-done.18.refs_7_), channel_id=1, source_target_pairs={{0,16},{16,0},{1,17},{17,1},{2,18},{18,2},{3,19},{19,3},{4,20},{20... | collective-permute-start | bytes 737288 | tf_op jit(solution)/shard_map/ppermute | solution.py:205

commit v6 on v5

--- a/solution.py
+++ b/solution.py
@@ -128,6 +128,24 @@
     )(*arrays)
 
 
+def hold_kernel(*refs):
+    for ref, out in zip(refs[:4], refs[4:]):
+        out[...] = ref[...]
+
+
+def hold(arrays):
+    vmem = pl.BlockSpec(memory_space=pltpu.VMEM)
+    return pl.pallas_call(
+        hold_kernel,
+        in_specs=[vmem] * 4,
+        out_specs=[vmem] * 4,
+        out_shape=[jax.ShapeDtypeStruct(a.shape, a.dtype) for a in arrays],
+        compiler_params=pltpu.CompilerParams(vmem_limit_bytes=4 << 20),
+        cost_estimate=pl.CostEstimate(flops=100 << 30, transcendentals=0, bytes_accessed=2 << 20),
+        name="hold",
+    )(*arrays)
+
+
 def product_kernel(at, w0, w1, w2, w3, wp, out):
     part = w0.shape[0] // 4
     total = None
@@ -157,12 +175,12 @@
 
 
 def final_kernel(at, heads_at, *refs):
-    grads, here, there, out, held = refs[:4], refs[4:8], refs[8:12], refs[12], refs[13]
+    grads, here, there, out, held = refs[0], refs[1:5], refs[5:9], refs[9], refs[10]
     rows = out.shape[1]
-    for kx in range(4):
+    for x in range(4):
         for kz in range(4):
-            heads = lax.rem(heads_at[0] + 4 - kz, 4) * 4 + lax.rem(heads_at[1] + 4 - kx, 4)
-            held[heads] = grads[kx][kz * rows : (kz + 1) * rows, :]
+            heads = lax.rem(heads_at[0] + 4 - kz, 4) * 4 + x
+            held[heads] = grads[x, kz * rows : (kz + 1) * rows, :]
     total = None
     for back in range(4):
         for lane in range(2):
@@ -178,14 +196,14 @@
 
 
 def final_product(at, heads_at, grads, here, there):
-    rows = grads[0].shape[0] // 4
+    rows = grads.shape[1] // 4
     width = here[0].shape[1]
     smem = pl.BlockSpec(memory_space=pltpu.SMEM)
     vmem = pl.BlockSpec(memory_space=pltpu.VMEM)
     return pl.pallas_call(
         final_kernel,
         out_shape=jax.ShapeDtypeStruct((width, rows), jnp.bfloat16),
-        in_specs=[smem] * 2 + [vmem] * 12,
+        in_specs=[smem] * 2 + [vmem] * 9,
         out_specs=vmem,
         scratch_shapes=[pltpu.VMEM((16, rows, HD), jnp.bfloat16)],
         compiler_params=pltpu.CompilerParams(vmem_limit_bytes=16 << 20),
@@ -193,7 +211,7 @@
             flops=2 * rows * width * 2048, transcendentals=0, bytes_accessed=4 << 20
         ),
         name="final_product",
-    )(at, heads_at, *grads, *here, *there)
+    )(at, heads_at, grads, *here, *there)
 
 
 def everywhere(array, axes, count):
@@ -261,8 +279,8 @@
     product = weight_product(heads_at, w, proj_weight)
     product = jnp.stack([product, swap("zl", product)])
     summed, product = lax.optimization_barrier((summed, product))
-    grads = ring(join(ring(summed, "zh"), 0), X)
-    product = ring(product, "y")
+    grads = everywhere(join(ring(summed, "zh"), 30 << 30), X, 4)
+    product = hold(ring(product, "y"))
     d_vision = final_product(at, heads_at, grads, product, [swap("co", p) for p in product])
     return (d_query, d_vision.T)
 

time: 110 us -> 110 us (level); the launches traced: 108 us -> 110 us
  waiting for transfers between devices: 37.8 us -> 40.8 us
  starting transfers between devices: 47.3 us -> 44.6 us
  local copies, waits for them, and re-layouts: 4.9 us -> 6.01 us
    all_to_all x1 -> x2, waiting for transfers between devices: 0.52 us -> 9.99 us  [everywhere(): return lax.all_to_all(copies, axes, split_axis=0, concat_axis=0, tiled=True)]
    ppermute x15 -> x12, waiting for transfers between devices: 24.1 us -> 16.1 us  [ring(): lax.ppermute(array, axes, [(i, (i + k) % 4) for i in range(4)])]
    ppermute x15 -> x12, starting transfers between devices: 33.9 us -> 27 us  [ring(): lax.ppermute(array, axes, [(i, (i + k) % 4) for i in range(4)])]
    all_to_all x1 -> x2, starting transfers between devices: 4.92 us -> 8.58 us  [everywhere(): return lax.all_to_all(copies, axes, split_axis=0, concat_axis=0, tiled=True)]
    ppermute x8, waiting for transfers between devices: 12.7 us -> 14.2 us  [swap(): return lax.ppermute(array, axis, [(0, 1), (1, 0)])]
    broadcast_in_dim x1 -> x2, local copies, waits for them, and re-layouts: 0.82 us -> 1.93 us  [everywhere(): copies = jnp.broadcast_to(array, (count, *array.shape))]
  transfers between devices with their start and end apart: 25 -> 23, of which waited for: 15 -> 17; matrix products, arithmetic and copies ran while one was open for 2% -> 3% of each run, Pallas kernels for 12% -> 12%
where the time goes in v6:
time: 110 us
  starting transfers between devices  44.6 us (41%)
  waiting for transfers between devices  40.8 us (37%)
  Pallas kernels  14.9 us (14%)
  local copies, waits for them, and re-layouts  6.01 us (5%)
  other arithmetic  2.59 us (2%)
    ppermute x12, starting transfers between devices, ring(): lax.ppermute(array, axes, [(i, (i + k) % 4) for i in range(4)])  27 us
    ppermute x12, waiting for transfers between devices, ring(): lax.ppermute(array, axes, [(i, (i + k) % 4) for i in range(4)])  16.1 us
    ppermute x8, waiting for transfers between devices, swap(): return lax.ppermute(array, axis, [(0, 1), (1, 0)])  14.2 us
    pallas_call x1, Pallas kernels, attention(): pl.pallas_call(attention_kernel, in_specs=[smem] * 3 + [vmem] * 6, out_sp...  10 us
    all_to_all x2, waiting for transfers between devices, everywhere(): return lax.all_to_all(copies, axes, split_axis=0, concat_axis=0, tiled=True)  9.99 us
    all_to_all x2, starting transfers between devices, everywhere(): return lax.all_to_all(copies, axes, split_axis=0, concat_axis=0, tiled=True)  8.58 us
    all_to_all x1, starting transfers between devices, shards(): lax.all_to_all(pair, ('zl', 'y', 'xl'), split_axis=0, concat_axis=0, tile...  5.35 us
    ppermute x8, starting transfers between devices, swap(): return lax.ppermute(array, axis, [(0, 1), (1, 0)])  3.7 us
  transfers between devices with their start and end apart: 23, of which 17 were waited for; matrix products, arithmetic and copies ran while one was open for 3% of the time, Pallas kernels for 12%

profile of v6, /device:TPU:64, one launch (start us, length us, event | category | flops | bytes accessed | tf_op | source)
XLA Modules:
  0.0 109.7 jit_solution(14394704458786262823)
XLA Ops:
  0.6 1.0 dynamic-slice_select_fusion.a
  1.7 4.6 %collective-permute-start.2 = (bf16[512,128]{1,0:T(8,128)(2,1)S(1)}, bf16[512,128]{1,0:T(8,128)(2,1)S(1)}, u32[]{:S(2)}, u32[]{:S(2)}) collective-permute-start(bf16[512,128]{1,0:T(8,128)(2,1)S(1)} %dynamic-slice_select_fusion.a), channel_id=1, source_target_pairs={{0,4},{4,8},{8,12},{12,0},{1,5},{5,9},{9,13},{13,1},{2,6},{6,10},{... | collective-permute-start | bytes 393224 | tf_op jit(solution)/shard_map/ppermute | solution.py:227
  6.2 1.0 collective-permute-start.3
  7.2 2.8 %collective-permute-start.4 = (bf16[512,128]{1,0:T(8,128)(2,1)S(1)}, bf16[512,128]{1,0:T(8,128)(2,1)S(1)}, u32[]{:S(2)}, u32[]{:S(2)}) collective-permute-start(bf16[512,128]{1,0:T(8,128)(2,1)S(1)} %dynamic-slice_select_fusion.a), channel_id=1, source_target_pairs={{0,12},{4,0},{8,4},{12,8},{1,13},{5,1},{9,5},{13,9},{2,14},{6,2},{... | collective-permute-start | bytes 393224 | tf_op jit(solution)/shard_map/ppermute | solution.py:227
  10.1 0.8 constant_dynamic-slice_fusion
  10.8 0.8 broadcast_in_dim.6
  11.7 4.9 %all-to-all-start = ((bf16[8,128,256]{2,1,0:T(8,128)(2,1)}), bf16[8,128,256]{2,1,0:T(8,128)(2,1)S(1)}, u32[]{:S(2)}, u32[]{:S(2)}) async-start(bf16[8,128,256]{2,1,0:T(8,128)(2,1)} %broadcast_in_dim.6), calls=%async_computation | async-start | bytes 1048576 | tf_op jit(solution)/shard_map/all_to_all | solution.py:219
  16.7 3.3 %collective-permute-done.3.c = bf16[512,128]{1,0:T(8,128)(2,1)S(1)} collective-permute-done((bf16[512,128]{1,0:T(8,128)(2,1)S(1)}, bf16[512,128]{1,0:T(8,128)(2,1)S(1)}, u32[]{:S(2)}, u32[]{:S(2)}) %collective-permute-start.3) | collective-permute-done | bytes 131104 | tf_op jit(solution)/shard_map/ppermute | solution.py:227
  19.9 1.0 collective-permute-done.4.d
  21.0 1.6 %collective-permute-start.5 = (bf16[2048,128]{1,0:T(8,128)(2,1)S(1)}, bf16[2048,128]{1,0:T(8,128)(2,1)S(1)}, u32[]{:S(2)}, u32[]{:S(2)}) collective-permute-start(bf16[2048,128]{1,0:T(8,128)(2,1)S(1)} %join.2.w0), channel_id=1, source_target_pairs={{0,1},{1,2},{2,3},{3,0},{4,5},{5,6},{6,7},{7,4},{8,9},{9,10},{10,1... | collective-permute-start | bytes 1572872 | tf_op jit(solution)/shard_map/ppermute | solution.py:227
  22.6 2.7 %collective-permute-start.6 = (bf16[2048,128]{1,0:T(8,128)(2,1)S(1)}, bf16[2048,128]{1,0:T(8,128)(2,1)S(1)}, u32[]{:S(2)}, u32[]{:S(2)}) collective-permute-start(bf16[2048,128]{1,0:T(8,128)(2,1)S(1)} %join.2.w0), channel_id=1, source_target_pairs={{0,2},{1,3},{2,0},{3,1},{4,6},{5,7},{6,4},{7,5},{8,10},{9,11},{10,... | collective-permute-start | bytes 1572872 | tf_op jit(solution)/shard_map/ppermute | solution.py:227
  25.3 1.4 %collective-permute-start.7 = (bf16[2048,128]{1,0:T(8,128)(2,1)S(1)}, bf16[2048,128]{1,0:T(8,128)(2,1)S(1)}, u32[]{:S(2)}, u32[]{:S(2)}) collective-permute-start(bf16[2048,128]{1,0:T(8,128)(2,1)S(1)} %join.2.w0), channel_id=1, source_target_pairs={{0,3},{1,0},{2,1},{3,2},{4,7},{5,4},{6,5},{7,6},{8,11},{9,8},{10,9... | collective-permute-start | bytes 1572872 | tf_op jit(solution)/shard_map/ppermute | solution.py:227
  26.7 0.5 all-to-all-done
  27.3 0.1 collective-permute-start
  27.4 0.5 collective-permute-start.1
  27.9 1.0 collective-permute-done.kv1
  28.9 0.4 collective-permute-done.1.kv2
  29.3 10.0 %attention.1 = (bf16[256,512]{1,0:T(8,128)(2,1)}, bf16[8,2,256,128]{3,2,1,0:T(8,128)(2,1)S(1)}, bf16[8,2,256,128]{3,2,1,0:T(8,128)(2,1)S(1)}) custom-call(s32[32]{0:T(128)S(1)} %copy-done.4, s32[16]{0:T(128)S(1)} %copy-done.5, s32[1]{0:T(128)} %bitcast.core, bf16[1024,256]{1,0:T(8,128)(2,1)S(1)} %bitcast.12, bf16[512,256]{1,0:T(8,128)(2,1)S(1)} %collective-permute-done.kv1, ...), custom_call_target="tpu_custom_call" | custom-call | tf_op jit(solution)/shard_map/attention/pallas_call | solution.py:93
  39.3 8.5 %collective-permute-done.6.w2 = bf16[2048,128]{1,0:T(8,128)(2,1)S(1)} collective-permute-done((bf16[2048,128]{1,0:T(8,128)(2,1)S(1)}, bf16[2048,128]{1,0:T(8,128)(2,1)S(1)}, u32[]{:S(2)}, u32[]{:S(2)}) %collective-permute-start.6) | collective-permute-done | bytes 524320 | tf_op jit(solution)/shard_map/ppermute | solution.py:227
  47.9 2.7 %collective-permute-done.8 = bf16[8,2,256,128]{3,2,1,0:T(8,128)(2,1)S(1)} collective-permute-done((bf16[8,2,256,128]{3,2,1,0:T(8,128)(2,1)S(1)}, bf16[8,2,256,128]{3,2,1,0:T(8,128)(2,1)S(1)}, u32[]{:S(2)}, u32[]{:S(2)}) %collective-permute-start.8) | collective-permute-done | bytes 1048608 | tf_op jit(solution)/shard_map/ppermute | solution.py:223
  50.5 1.2 %add_convert_fusion = bf16[8,2,256,128]{3,2,1,0:T(8,128)(2,1)} fusion(bf16[8,2,256,128]{3,2,1,0:T(8,128)(2,1)S(1)} %collective-permute-done.8, bf16[8,2,256,128]{3,2,1,0:T(8,128)(2,1)S(1)} %get-tuple-element.17), kind=kLoop, calls=%fused_computation | loop fusion | flops 2097152 | bytes 3145728 | tf_op jit(solution)/shard_map/convert_element_type | solution.py:267
  51.8 5.3 %all-to-all-start.1 = ((bf16[16,256,128]{2,1,0:T(8,128)(2,1)}), bf16[16,256,128]{2,1,0:T(8,128)(2,1)S(1)}, u32[]{:S(2)}, u32[]{:S(2)}) async-start(bf16[16,256,128]{2,1,0:T(8,128)(2,1)} %bitcast.8), calls=%async_computation.1 | async-start | bytes 2097152 | tf_op jit(solution)/shard_map/all_to_all | solution.py:268
  57.2 3.2 %copy-done = bf16[480,8192]{1,0:T(8,128)(2,1)S(1)} copy-done((bf16[480,8192]{1,0:T(8,128)(2,1)S(1)}, bf16[480,8192]{1,0:T(8,128)(2,1)}, u32[]{:S(2)}) %copy-start) | copy-done | bytes 7864344
  60.5 2.7 %weight_product.1 = bf16[480,128]{1,0:T(8,128)(2,1)S(1)} custom-call(s32[2]{0:T(128)S(1)} %pad_add_fusion.1.at.heads_at, bf16[2048,128]{1,0:T(8,128)(2,1)S(1)} %join.2.w0, bf16[2048,128]{1,0:T(8,128)(2,1)S(1)} %collective-permute-done.5.w1, bf16[2048,128]{1,0:T(8,128)(2,1)S(1)} %collective-permute-done.6.w2, ...), custom_call_target="tpu_custom_call" | custom-call | flops 1006632960 | bytes 10485760 | tf_op jit(solution)/shard_map/weight_product/pallas_call | solution.py:164
  63.2 2.0 %collective-permute-start.9 = (bf16[480,128]{1,0:T(8,128)(2,1)S(1)}, bf16[480,128]{1,0:T(8,128)(2,1)S(1)}, u32[]{:S(2)}, u32[]{:S(2)}) collective-permute-start(bf16[480,128]{1,0:T(8,128)(2,1)S(1)} %weight_product.1), channel_id=1, source_target_pairs={{0,128},{128,0},{1,129},{129,1},{2,130},{130,2},{3,131},{131,3},{4... | collective-permute-start | bytes 368648 | tf_op jit(solution)/shard_map/ppermute | solution.py:223
  65.2 8.7 %collective-permute-done.9 = bf16[480,128]{1,0:T(8,128)(2,1)S(1)} collective-permute-done((bf16[480,128]{1,0:T(8,128)(2,1)S(1)}, bf16[480,128]{1,0:T(8,128)(2,1)S(1)}, u32[]{:S(2)}, u32[]{:S(2)}) %collective-permute-start.9) | collective-permute-done | bytes 122912 | tf_op jit(solution)/shard_map/ppermute | solution.py:223
  73.9 0.5 all-to-all-done.1
  74.4 0.1 reduce_sum.12.a
  74.5 3.0 %collective-permute-start.10 = (bf16[256,128]{1,0:T(8,128)(2,1)S(1)}, bf16[256,128]{1,0:T(8,128)(2,1)S(1)}, u32[]{:S(2)}, u32[]{:S(2)}) collective-permute-start(bf16[256,128]{1,0:T(8,128)(2,1)S(1)} %reduce_sum.12.a), channel_id=1, source_target_pairs={{0,4},{4,8},{8,12},{12,0},{1,5},{5,9},{9,13},{13,1},{2,6},{6,10},{... | collective-permute-start | bytes 196616 | tf_op jit(solution)/shard_map/ppermute | solution.py:227
  77.5 2.6 %collective-permute-start.11 = (bf16[256,128]{1,0:T(8,128)(2,1)S(1)}, bf16[256,128]{1,0:T(8,128)(2,1)S(1)}, u32[]{:S(2)}, u32[]{:S(2)}) collective-permute-start(bf16[256,128]{1,0:T(8,128)(2,1)S(1)} %reduce_sum.12.a), channel_id=1, source_target_pairs={{0,8},{4,12},{8,0},{12,4},{1,9},{5,13},{9,1},{13,5},{2,10},{6,14},... | collective-permute-start | bytes 196616 | tf_op jit(solution)/shard_map/ppermute | solution.py:227
  80.1 2.4 %collective-permute-start.12 = (bf16[256,128]{1,0:T(8,128)(2,1)S(1)}, bf16[256,128]{1,0:T(8,128)(2,1)S(1)}, u32[]{:S(2)}, u32[]{:S(2)}) collective-permute-start(bf16[256,128]{1,0:T(8,128)(2,1)S(1)} %reduce_sum.12.a), channel_id=1, source_target_pairs={{0,12},{4,0},{8,4},{12,8},{1,13},{5,1},{9,5},{13,9},{2,14},{6,2},{... | collective-permute-start | bytes 196616 | tf_op jit(solution)/shard_map/ppermute | solution.py:227
  82.5 0.7 collective-permute-start.13
  83.2 2.9 %collective-permute-start.14 = (bf16[2,480,128]{2,1,0:T(8,128)(2,1)S(1)}, bf16[2,480,128]{2,1,0:T(8,128)(2,1)S(1)}, u32[]{:S(2)}, u32[]{:S(2)}) collective-permute-start(bf16[2,480,128]{2,1,0:T(8,128)(2,1)S(1)} %pad_maximum_fusion.refs_0_), channel_id=1, source_target_pairs={{0,64},{32,96},{64,0},{96,32},{1,65},{33,97},{65,1},{97,33},{2,66}... | collective-permute-start | bytes 737288 | tf_op jit(solution)/shard_map/ppermute | solution.py:227
  86.2 1.2 %collective-permute-start.15 = (bf16[2,480,128]{2,1,0:T(8,128)(2,1)S(1)}, bf16[2,480,128]{2,1,0:T(8,128)(2,1)S(1)}, u32[]{:S(2)}, u32[]{:S(2)}) collective-permute-start(bf16[2,480,128]{2,1,0:T(8,128)(2,1)S(1)} %pad_maximum_fusion.refs_0_), channel_id=1, source_target_pairs={{0,96},{32,0},{64,32},{96,64},{1,97},{33,1},{65,33},{97,65},{2,98}... | collective-permute-start | bytes 737288 | tf_op jit(solution)/shard_map/ppermute | solution.py:227
  87.4 0.3 collective-permute-done.12.d
  87.7 1.1 %broadcast_in_dim.7 = bf16[4,1024,128]{2,1,0:T(8,128)(2,1)} broadcast(bf16[1024,128]{1,0:T(8,128)(2,1)S(1)} %join.3), dimensions={1,2} | broadcast | bytes 1310720 | tf_op jit(solution)/shard_map/broadcast_in_dim | solution.py:218
  88.8 3.7 %all-to-all-start.2 = ((bf16[4,1024,128]{2,1,0:T(8,128)(2,1)}), bf16[4,1024,128]{2,1,0:T(8,128)(2,1)S(1)}, u32[]{:S(2)}, u32[]{:S(2)}) async-start(bf16[4,1024,128]{2,1,0:T(8,128)(2,1)} %broadcast_in_dim.7), calls=%async_computation.2 | async-start | bytes 2097152 | tf_op jit(solution)/shard_map/all_to_all | solution.py:219
  92.5 2.9 %collective-permute-done.14.refs_2_ = bf16[2,480,128]{2,1,0:T(8,128)(2,1)S(1)} collective-permute-done((bf16[2,480,128]{2,1,0:T(8,128)(2,1)S(1)}, bf16[2,480,128]{2,1,0:T(8,128)(2,1)S(1)}, u32[]{:S(2)}, u32[]{:S(2)}) %collective-permute-start.14) | collective-permute-done | bytes 245792 | tf_op jit(solution)/shard_map/ppermute | solution.py:227
  95.5 0.1 collective-permute-start.16
  95.6 0.5 collective-permute-start.17
  96.1 0.1 collective-permute-start.18
  96.2 0.4 collective-permute-start.19
  96.7 0.4 collective-permute-done.16.refs_5_
  97.1 0.4 collective-permute-done.17.refs_6_
  97.5 0.4 collective-permute-done.18.refs_7_
  97.8 0.4 collective-permute-done.19.refs_8_
  98.2 9.5 %all-to-all-done.2.refs_0_ = bf16[4,1024,128]{2,1,0:T(8,128)(2,1)S(1)} async-done(((bf16[4,1024,128]{2,1,0:T(8,128)(2,1)}), bf16[4,1024,128]{2,1,0:T(8,128)(2,1)S(1)}, u32[]{:S(2)}, u32[]{:S(2)}) %all-to-all-start.2) | async-done | bytes 1048608 | tf_op jit(solution)/shard_map/all_to_all | solution.py:219
  107.7 2.0 %final_product.1 = bf16[480,256]{1,0:T(8,128)(2,1)} custom-call(s32[3]{0:T(128)S(1)} %pad_add_fusion.at, s32[2]{0:T(128)S(1)} %pad_add_fusion.1.at.heads_at, bf16[4,1024,128]{2,1,0:T(8,128)(2,1)S(1)} %all-to-all-done.2.refs_0_, bf16[2,480,128]{2,1,0:T(8,128)(2,1)S(1)} %get-tuple-element.26.refs_1_, bf16[2,480,128]{2,1,0:T(8,128)(2,1)S(1)} %get-tuple-element.27.refs_2_, ...), custom_call_target="tpu_custom_call" | custom-call | flops 503316480 | bytes 4194304 | tf_op jit(solution)/shard_map/final_product/pallas_call | solution.py:203
  (27 shorter events, 0.4 us)
Async XLA Ops:
  1.7 15.0 %collective-permute-start.2 = (bf16[512,128]{1,0:T(8,128)(2,1)S(1)}, bf16[512,128]{1,0:T(8,128)(2,1)S(1)}, u32[]{:S(2)}, u32[]{:S(2)}) collective-permute-start(bf16[512,128]{1,0:T(8,128)(2,1)S(1)} %dynamic-slice_select_fusion.a), channel_id=1, source_target_pairs={{0,4},{4,8},{8,12},{12,0},{1,5},{5,9},{9,13},{13,1},{2,6},{6,10},{... | collective-permute-start | bytes 393224 | tf_op jit(solution)/shard_map/ppermute | solution.py:227
  6.2 13.7 %collective-permute-start.3 = (bf16[512,128]{1,0:T(8,128)(2,1)S(1)}, bf16[512,128]{1,0:T(8,128)(2,1)S(1)}, u32[]{:S(2)}, u32[]{:S(2)}) collective-permute-start(bf16[512,128]{1,0:T(8,128)(2,1)S(1)} %dynamic-slice_select_fusion.a), channel_id=1, source_target_pairs={{0,8},{4,12},{8,0},{12,4},{1,9},{5,13},{9,1},{13,5},{2,10},{6,14},... | collective-permute-start | bytes 393224 | tf_op jit(solution)/shard_map/ppermute | solution.py:227
  7.2 13.7 %collective-permute-start.4 = (bf16[512,128]{1,0:T(8,128)(2,1)S(1)}, bf16[512,128]{1,0:T(8,128)(2,1)S(1)}, u32[]{:S(2)}, u32[]{:S(2)}) collective-permute-start(bf16[512,128]{1,0:T(8,128)(2,1)S(1)} %dynamic-slice_select_fusion.a), channel_id=1, source_target_pairs={{0,12},{4,0},{8,4},{12,8},{1,13},{5,1},{9,5},{13,9},{2,14},{6,2},{... | collective-permute-start | bytes 393224 | tf_op jit(solution)/shard_map/ppermute | solution.py:227
  11.7 15.6 %all-to-all-start = ((bf16[8,128,256]{2,1,0:T(8,128)(2,1)}), bf16[8,128,256]{2,1,0:T(8,128)(2,1)S(1)}, u32[]{:S(2)}, u32[]{:S(2)}) async-start(bf16[8,128,256]{2,1,0:T(8,128)(2,1)} %broadcast_in_dim.6), calls=%async_computation | async-start | bytes 1048576 | tf_op jit(solution)/shard_map/all_to_all | solution.py:219
  16.6 12.7 %copy-start.1 = (bf16[256,512]{1,0:T(8,128)(2,1)S(1)}, bf16[256,512]{1,0:T(8,128)(2,1)}, u32[]{:S(2)}) copy-start(bf16[256,512]{1,0:T(8,128)(2,1)} %q_ref.1) | copy-start | bytes 786436
  16.6 12.7 %copy-start.2 = (bf16[256,512]{1,0:T(8,128)(2,1)S(1)}, bf16[256,512]{1,0:T(8,128)(2,1)}, u32[]{:S(2)}) copy-start(bf16[256,512]{1,0:T(8,128)(2,1)} %do_ref.1) | copy-start | bytes 786436
  16.6 12.7 %copy-start.3 = (bf16[256,512]{1,0:T(8,128)(2,1)S(1)}, bf16[256,512]{1,0:T(8,128)(2,1)}, u32[]{:S(2)}) copy-start(bf16[256,512]{1,0:T(8,128)(2,1)} %ao_ref.1) | copy-start | bytes 786436
  16.6 12.7 %copy-start.4 = (s32[32]{0:T(128)S(1)}, s32[32]{0:T(128)}, u32[]{:S(2)}) copy-start(s32[32]{0:T(128)} %order.1) | copy-start | bytes 388
  16.6 12.7 %copy-start.5 = (s32[16]{0:T(128)S(1)}, s32[16]{0:T(128)}, u32[]{:S(2)}) copy-start(s32[16]{0:T(128)} %counts.1) | copy-start | bytes 196
  21.0 18.3 %collective-permute-start.5 = (bf16[2048,128]{1,0:T(8,128)(2,1)S(1)}, bf16[2048,128]{1,0:T(8,128)(2,1)S(1)}, u32[]{:S(2)}, u32[]{:S(2)}) collective-permute-start(bf16[2048,128]{1,0:T(8,128)(2,1)S(1)} %join.2.w0), channel_id=1, source_target_pairs={{0,1},{1,2},{2,3},{3,0},{4,5},{5,6},{6,7},{7,4},{8,9},{9,10},{10,1... | collective-permute-start | bytes 1572872 | tf_op jit(solution)/shard_map/ppermute | solution.py:227
  22.6 25.3 %collective-permute-start.6 = (bf16[2048,128]{1,0:T(8,128)(2,1)S(1)}, bf16[2048,128]{1,0:T(8,128)(2,1)S(1)}, u32[]{:S(2)}, u32[]{:S(2)}) collective-permute-start(bf16[2048,128]{1,0:T(8,128)(2,1)S(1)} %join.2.w0), channel_id=1, source_target_pairs={{0,2},{1,3},{2,0},{3,1},{4,6},{5,7},{6,4},{7,5},{8,10},{9,11},{10,... | collective-permute-start | bytes 1572872 | tf_op jit(solution)/shard_map/ppermute | solution.py:227
  25.3 22.6 %collective-permute-start.7 = (bf16[2048,128]{1,0:T(8,128)(2,1)S(1)}, bf16[2048,128]{1,0:T(8,128)(2,1)S(1)}, u32[]{:S(2)}, u32[]{:S(2)}) collective-permute-start(bf16[2048,128]{1,0:T(8,128)(2,1)S(1)} %join.2.w0), channel_id=1, source_target_pairs={{0,3},{1,0},{2,1},{3,2},{4,7},{5,4},{6,5},{7,6},{8,11},{9,8},{10,9... | collective-permute-start | bytes 1572872 | tf_op jit(solution)/shard_map/ppermute | solution.py:227
  27.3 1.6 %collective-permute-start = (bf16[512,256]{1,0:T(8,128)(2,1)S(1)}, bf16[512,256]{1,0:T(8,128)(2,1)S(1)}, u32[]{:S(2)}, u32[]{:S(2)}) collective-permute-start(bf16[512,256]{1,0:T(8,128)(2,1)S(1)} %bitcast.15), channel_id=1, source_target_pairs={{0,16},{16,0},{1,17},{17,1},{2,18},{18,2},{3,19},{19,3},{4,20},{20... | collective-permute-start | bytes 786440 | tf_op jit(solution)/shard_map/ppermute | solution.py:223
  27.4 1.9 %collective-permute-start.1 = (bf16[512,256]{1,0:T(8,128)(2,1)S(1)}, bf16[512,256]{1,0:T(8,128)(2,1)S(1)}, u32[]{:S(2)}, u32[]{:S(2)}) collective-permute-start(bf16[512,256]{1,0:T(8,128)(2,1)S(1)} %bitcast.14), channel_id=1, source_target_pairs={{0,16},{16,0},{1,17},{17,1},{2,18},{18,2},{3,19},{19,3},{4,20},{20... | collective-permute-start | bytes 786440 | tf_op jit(solution)/shard_map/ppermute | solution.py:223
  47.9 2.7 %collective-permute-start.8 = (bf16[8,2,256,128]{3,2,1,0:T(8,128)(2,1)S(1)}, bf16[8,2,256,128]{3,2,1,0:T(8,128)(2,1)S(1)}, u32[]{:S(2)}, u32[]{:S(2)}) collective-permute-start(bf16[8,2,256,128]{3,2,1,0:T(8,128)(2,1)S(1)} %get-tuple-element.19), channel_id=1, source_target_pairs={{0,16},{16,0},{1,17},{17,1},{2,18},{18,2},{3,19},{19,3},{4,20},{20... | collective-permute-start | bytes 3145736 | tf_op jit(solution)/shard_map/ppermute | solution.py:223
  51.8 22.6 %all-to-all-start.1 = ((bf16[16,256,128]{2,1,0:T(8,128)(2,1)}), bf16[16,256,128]{2,1,0:T(8,128)(2,1)S(1)}, u32[]{:S(2)}, u32[]{:S(2)}) async-start(bf16[16,256,128]{2,1,0:T(8,128)(2,1)} %bitcast.8), calls=%async_computation.1 | async-start | bytes 2097152 | tf_op jit(solution)/shard_map/all_to_all | solution.py:268
  57.2 3.2 %copy-start = (bf16[480,8192]{1,0:T(8,128)(2,1)S(1)}, bf16[480,8192]{1,0:T(8,128)(2,1)}, u32[]{:S(2)}) copy-start(bf16[480,8192]{1,0:T(8,128)(2,1)} %wp.1) | copy-start | bytes 23592964
  63.2 10.7 %collective-permute-start.9 = (bf16[480,128]{1,0:T(8,128)(2,1)S(1)}, bf16[480,128]{1,0:T(8,128)(2,1)S(1)}, u32[]{:S(2)}, u32[]{:S(2)}) collective-permute-start(bf16[480,128]{1,0:T(8,128)(2,1)S(1)} %weight_product.1), channel_id=1, source_target_pairs={{0,128},{128,0},{1,129},{129,1},{2,130},{130,2},{3,131},{131,3},{4... | collective-permute-start | bytes 368648 | tf_op jit(solution)/shard_map/ppermute | solution.py:223
  74.5 11.6 %collective-permute-start.10 = (bf16[256,128]{1,0:T(8,128)(2,1)S(1)}, bf16[256,128]{1,0:T(8,128)(2,1)S(1)}, u32[]{:S(2)}, u32[]{:S(2)}) collective-permute-start(bf16[256,128]{1,0:T(8,128)(2,1)S(1)} %reduce_sum.12.a), channel_id=1, source_target_pairs={{0,4},{4,8},{8,12},{12,0},{1,5},{5,9},{9,13},{13,1},{2,6},{6,10},{... | collective-permute-start | bytes 196616 | tf_op jit(solution)/shard_map/ppermute | solution.py:227
  77.5 9.9 %collective-permute-start.11 = (bf16[256,128]{1,0:T(8,128)(2,1)S(1)}, bf16[256,128]{1,0:T(8,128)(2,1)S(1)}, u32[]{:S(2)}, u32[]{:S(2)}) collective-permute-start(bf16[256,128]{1,0:T(8,128)(2,1)S(1)} %reduce_sum.12.a), channel_id=1, source_target_pairs={{0,8},{4,12},{8,0},{12,4},{1,9},{5,13},{9,1},{13,5},{2,10},{6,14},... | collective-permute-start | bytes 196616 | tf_op jit(solution)/shard_map/ppermute | solution.py:227
  80.1 7.5 %collective-permute-start.12 = (bf16[256,128]{1,0:T(8,128)(2,1)S(1)}, bf16[256,128]{1,0:T(8,128)(2,1)S(1)}, u32[]{:S(2)}, u32[]{:S(2)}) collective-permute-start(bf16[256,128]{1,0:T(8,128)(2,1)S(1)} %reduce_sum.12.a), channel_id=1, source_target_pairs={{0,12},{4,0},{8,4},{12,8},{1,13},{5,1},{9,5},{13,9},{2,14},{6,2},{... | collective-permute-start | bytes 196616 | tf_op jit(solution)/shard_map/ppermute | solution.py:227
  82.5 10.0 %collective-permute-start.13 = (bf16[2,480,128]{2,1,0:T(8,128)(2,1)S(1)}, bf16[2,480,128]{2,1,0:T(8,128)(2,1)S(1)}, u32[]{:S(2)}, u32[]{:S(2)}) collective-permute-start(bf16[2,480,128]{2,1,0:T(8,128)(2,1)S(1)} %pad_maximum_fusion.refs_0_), channel_id=1, source_target_pairs={{0,32},{32,64},{64,96},{96,0},{1,33},{33,65},{65,97},{97,1},{2,34}... | collective-permute-start | bytes 737288 | tf_op jit(solution)/shard_map/ppermute | solution.py:227
  83.2 12.2 %collective-permute-start.14 = (bf16[2,480,128]{2,1,0:T(8,128)(2,1)S(1)}, bf16[2,480,128]{2,1,0:T(8,128)(2,1)S(1)}, u32[]{:S(2)}, u32[]{:S(2)}) collective-permute-start(bf16[2,480,128]{2,1,0:T(8,128)(2,1)S(1)} %pad_maximum_fusion.refs_0_), channel_id=1, source_target_pairs={{0,64},{32,96},{64,0},{96,32},{1,65},{33,97},{65,1},{97,33},{2,66}... | collective-permute-start | bytes 737288 | tf_op jit(solution)/shard_map/ppermute | solution.py:227
  86.2 9.3 %collective-permute-start.15 = (bf16[2,480,128]{2,1,0:T(8,128)(2,1)S(1)}, bf16[2,480,128]{2,1,0:T(8,128)(2,1)S(1)}, u32[]{:S(2)}, u32[]{:S(2)}) collective-permute-start(bf16[2,480,128]{2,1,0:T(8,128)(2,1)S(1)} %pad_maximum_fusion.refs_0_), channel_id=1, source_target_pairs={{0,96},{32,0},{64,32},{96,64},{1,97},{33,1},{65,33},{97,65},{2,98}... | collective-permute-start | bytes 737288 | tf_op jit(solution)/shard_map/ppermute | solution.py:227
  88.8 18.9 %all-to-all-start.2 = ((bf16[4,1024,128]{2,1,0:T(8,128)(2,1)}), bf16[4,1024,128]{2,1,0:T(8,128)(2,1)S(1)}, u32[]{:S(2)}, u32[]{:S(2)}) async-start(bf16[4,1024,128]{2,1,0:T(8,128)(2,1)} %broadcast_in_dim.7), calls=%async_computation.2 | async-start | bytes 2097152 | tf_op jit(solution)/shard_map/all_to_all | solution.py:219
  95.5 1.6 %collective-permute-start.16 = (bf16[2,480,128]{2,1,0:T(8,128)(2,1)S(1)}, bf16[2,480,128]{2,1,0:T(8,128)(2,1)S(1)}, u32[]{:S(2)}, u32[]{:S(2)}) collective-permute-start(bf16[2,480,128]{2,1,0:T(8,128)(2,1)S(1)} %get-tuple-element.26.refs_1_), channel_id=1, source_target_pairs={{0,16},{16,0},{1,17},{17,1},{2,18},{18,2},{3,19},{19,3},{4,20},{20... | collective-permute-start | bytes 737288 | tf_op jit(solution)/shard_map/ppermute | solution.py:223
  95.6 1.9 %collective-permute-start.17 = (bf16[2,480,128]{2,1,0:T(8,128)(2,1)S(1)}, bf16[2,480,128]{2,1,0:T(8,128)(2,1)S(1)}, u32[]{:S(2)}, u32[]{:S(2)}) collective-permute-start(bf16[2,480,128]{2,1,0:T(8,128)(2,1)S(1)} %get-tuple-element.27.refs_2_), channel_id=1, source_target_pairs={{0,16},{16,0},{1,17},{17,1},{2,18},{18,2},{3,19},{19,3},{4,20},{20... | collective-permute-start | bytes 737288 | tf_op jit(solution)/shard_map/ppermute | solution.py:223
  96.1 1.7 %collective-permute-start.18 = (bf16[2,480,128]{2,1,0:T(8,128)(2,1)S(1)}, bf16[2,480,128]{2,1,0:T(8,128)(2,1)S(1)}, u32[]{:S(2)}, u32[]{:S(2)}) collective-permute-start(bf16[2,480,128]{2,1,0:T(8,128)(2,1)S(1)} %get-tuple-element.28.refs_3_), channel_id=1, source_target_pairs={{0,16},{16,0},{1,17},{17,1},{2,18},{18,2},{3,19},{19,3},{4,20},{20... | collective-permute-start | bytes 737288 | tf_op jit(solution)/shard_map/ppermute | solution.py:223
  96.2 2.0 %collective-permute-start.19 = (bf16[2,480,128]{2,1,0:T(8,128)(2,1)S(1)}, bf16[2,480,128]{2,1,0:T(8,128)(2,1)S(1)}, u32[]{:S(2)}, u32[]{:S(2)}) collective-permute-start(bf16[2,480,128]{2,1,0:T(8,128)(2,1)S(1)} %get-tuple-element.29.refs_4_), channel_id=1, source_target_pairs={{0,16},{16,0},{1,17},{17,1},{2,18},{18,2},{3,19},{19,3},{4,20},{20... | collective-permute-start | bytes 737288 | tf_op jit(solution)/shard_map/ppermute | solution.py:223
